TPU v7x, 32 devices: a whole 2x2x4 slice. The times are simulated.
32 devices in a mesh: groups: 2 (over y), cand: 4 (over z), mp: 4 (over x, core).
Axes of the slice: x: 2, y: 2, z: 4, core: 2. Of those that a mesh axis runs over, the one named last changes fastest.
Arguments:
- user_feats: bfloat16 [8, 4096], P(('groups', 'cand')), parts along dimension 0, may hold values from -6 to 6
- user_slot: int32 [2], P('groups'), parts along dimension 0, may hold values from 0 to 3, as said below
- cand_pool: bfloat16 [512, 4096], P('groups'), parts along dimension 0, may hold values from -6 to 6
- cand_ids: int32 [2, 64], P('groups'), parts along dimension 0, may hold values from 0 to 255
- first_weight: bfloat16 [8192, 8192], P('mp', 'cand'), may hold values from -0.0625 to 0.0625
- first_bias: float32 [8192], P('cand'), may hold values from -5 to 5
- second_weight: bfloat16 [8192, 8192], P('cand', 'mp'), may hold values from -0.0625 to 0.0625
- second_bias: float32 [8192], P('mp'), may hold values from -5 to 5
- third_weight: bfloat16 [8192, 8192], P('mp', 'cand'), may hold values from -0.0625 to 0.0625
- third_bias: float32 [8192], P('cand'), may hold values from -5 to 5
- score_weight: bfloat16 [8192], P('cand'), may hold values from -0.0625 to 0.0625
Outputs:
- crossed: bfloat16 [128, 8192], P(('groups', 'mp'), 'cand'), parts along dimension 0
- logits: float32 [128], P(('groups', 'mp')), parts along dimension 0
There are 2 independent parts, one for each index of `groups`. A program takes and returns all parts, laid end to end along the dimension named above; an argument that names none is the same for every part. Nothing has to cross between parts.
Inputs may be any that keep to these rules, and one draw needn't show every extreme that they name: `user_slot`: the users' slots are distinct.
All inputs are finite; a program needn't handle non-finite values.
Results may differ from a plain program's by a relative error of at most 0.022.
Values may be sent and summed in bfloat16 or wider, within the bound.
No kernel may reach another device: no remote copies, remote signals or barrier semaphores. Data moves between devices by JAX's collectives and lax.ppermute only.
A program may use at most 64 MiB of HBM per device.

v0:
```python
import functools

import jax
import jax.numpy as jnp
from jax import lax
from jax.experimental import pallas as pl
from jax.experimental.pallas import tpu as pltpu
from jax.sharding import PartitionSpec as P


F32 = jnp.float32
BF16 = jnp.bfloat16
DIRECT = 4
MIB = 1024 * 1024
STAGE_FLOPS = 1 << 34


def bits_of(count):
    bits, bit = [], 1
    while bit < count:
        bits.append(bit)
        bit *= 2
    assert bit == count
    return bits


def swap(value, axis, bit):
    count = lax.axis_size(axis)
    return lax.ppermute(value, axis, [(i, i ^ bit) for i in range(count)])


def call(kernel, outs, args, scratch=(), hbm=(), smem=(), flops=0, limit=6 * MIB):
    moved = sum(a.size * a.dtype.itemsize for a in args if a.size < 2 * MIB)
    moved += sum(functools.reduce(lambda a, b: a * b, s) * jnp.dtype(d).itemsize for s, d in outs)
    return pl.pallas_call(
        kernel,
        out_shape=[jax.ShapeDtypeStruct(s, d) for s, d in outs],
        in_specs=[
            pl.BlockSpec(
                memory_space=pltpu.HBM if i in hbm else pltpu.SMEM if i in smem else pltpu.VMEM
            )
            for i in range(len(args))
        ],
        out_specs=[pl.BlockSpec(memory_space=pltpu.VMEM)] * len(outs),
        scratch_shapes=list(scratch),
        compiler_params=pltpu.CompilerParams(vmem_limit_bytes=limit),
        cost_estimate=pl.CostEstimate(flops=flops, bytes_accessed=moved, transcendentals=0),
    )(*[pltpu.with_memory_space_constraint(a, pltpu.HBM) if i in hbm else a for i, a in enumerate(args)])


def aligned(index, size):
    return pl.ds(pl.multiple_of(index * size, size), size)


def add_to(*refs):
    *part_refs, out_ref = refs
    total = part_refs[0][...]
    for part_ref in part_refs[1:]:
        total = total + part_ref[...]
    out_ref[...] = total


def stage(out_ref):
    out_ref[...] = jnp.zeros_like(out_ref)


def choose_user(local, bit, slot_ref, own_ref, other_ref, out_ref):
    want = (slot_ref[...] // local) ^ lax.axis_index("cand")
    other, own = other_ref[...].astype(F32), own_ref[...].astype(F32)
    out_ref[...] = jnp.where((jnp.broadcast_to(want, own.shape) & bit) != 0, other, own).astype(BF16)


def owner_steps(local, slot_ref, out_ref):
    row = lax.broadcasted_iota(jnp.int32, out_ref.shape, 0)
    want = jnp.zeros(out_ref.shape, jnp.int32)
    for user in range(out_ref.shape[0]):
        owner = lax.div(slot_ref[user], local) ^ lax.axis_index("cand")
        want = jnp.where(row == user, owner, want)
    out_ref[...] = want


def choose_pool(
    half, ids_ref, pool_ref, _, model_ref, cand_ref
):
    users, rows = ids_ref.shape
    numbers = lax.broadcasted_iota(jnp.int32, (pool_ref.shape[0], rows), 0)
    for axis, out_ref in (("mp", model_ref), ("cand", cand_ref)):
        width = out_ref.shape[1]
        cols = aligned(lax.axis_index(axis) % (half // width), width)
        for user in range(users):
            chosen = (numbers == ids_ref[pl.ds(user, 1), :]).astype(BF16)
            out_ref[pl.ds(user * rows, rows), :] = lax.dot_general(
                chosen, pool_ref[:, cols], (((0,), (0,)), ((), ())), preferred_element_type=F32
            ).astype(BF16)


def tiles(width, step=512):
    step = min(step, width)
    return [pl.ds(i, step) for i in range(0, width, step)]


def multiply(rows_ref, weight_ref, out_ref, scale_ref=None):
    for cols in tiles(out_ref.shape[1]):
        value = jnp.dot(rows_ref[...], weight_ref[:, cols], preferred_element_type=F32)
        out_ref[:, cols] = value if scale_ref is None else scale_ref[:, cols].astype(F32) * value


def pool_terms(half, rows_ref, weight_ref, keep_ref, send_ref, terms_ref):
    inside = lax.axis_index("mp") < half // rows_ref.shape[1]

    @pl.when(inside)
    def _():
        keep_ref[...] = jnp.zeros_like(keep_ref)
        send_ref[...] = jnp.zeros_like(send_ref)

    @pl.when(jnp.logical_not(inside))
    def _():
        multiply(rows_ref, weight_ref, terms_ref)
        low = lax.axis_index("mp") % 2
        size = keep_ref.shape[0]
        keep_ref[...] = terms_ref[aligned(low, size), :]
        send_ref[...] = terms_ref[aligned(1 - low, size), :].astype(BF16)


def user_terms(
    half, want_ref, weight_ref, pool_model_ref, pool_cand_ref, *refs
):
    *part_refs, model_ref, cand_ref, terms_ref = refs
    users = part_refs[0].shape[0]
    terms_ref[...] = jnp.zeros_like(terms_ref)
    for axis, pool_ref, out_ref in (
        ("mp", pool_model_ref, model_ref),
        ("cand", pool_cand_ref, cand_ref),
    ):
        rows, width = out_ref.shape
        block = lax.axis_index(axis)
        inside = block < half // width

        @pl.when(inside)
        def _():
            cols = aligned(block % (half // width), width)
            parts = [part_ref[:, cols] for part_ref in part_refs]
            chosen = parts[0].astype(F32)
            want = jnp.broadcast_to(want_ref[:, :1], chosen.shape)
            for bit in range(1, len(parts)):
                chosen = jnp.where(want == bit, parts[bit].astype(F32), chosen)
            for user in range(users):
                out_ref[pl.ds(user * (rows // users), rows // users), :] = jnp.broadcast_to(
                    chosen[user : user + 1], (rows // users, width)
                ).astype(BF16)
            if axis == "mp":
                padded = chosen
                if users < 8:
                    padded = jnp.concatenate([chosen, jnp.zeros((8 - users, width), F32)], axis=0)
                padded = padded.astype(BF16)
                for tile in tiles(terms_ref.shape[1]):
                    value = jnp.dot(padded, weight_ref[:, tile], preferred_element_type=F32)
                    terms_ref[:, tile] = value[:users]

        @pl.when(jnp.logical_not(inside))
        def _():
            out_ref[...] = pool_ref[...]


def add_up(keep_ref, other_ref, sum_ref, send_ref):
    total = keep_ref[...] + other_ref[...].astype(F32)
    sum_ref[...] = total
    send_ref[...] = total.astype(BF16)


def add_own_columns(terms_ref, rows_ref, have, want):
    width, wanted = rows_ref.shape[1], terms_ref.shape[1]
    small = min(width, wanted)
    ratio = max(width, wanted) // small
    assert max(width, wanted) == ratio * small
    if width >= wanted:
        inside, here, there = want // ratio == have, aligned(want % ratio, small), slice(None)
    else:
        inside, here, there = have // ratio == want, slice(None), aligned(have % ratio, small)

    @pl.when(inside)
    def _():
        terms_ref[:, there] += rows_ref[:, here].astype(F32)


def layer_two(
    mine_ref, other_ref, user_ref, user_other_ref, bias_ref, cand_ref, base_ref, weight_ref, *refs
):
    *out_refs, rows_ref, terms_ref, user_sum_ref = refs
    low = lax.axis_index("mp") % 2
    size = mine_ref.shape[0]
    users = user_ref.shape[0]
    assert users == 1 or users % 2 == 0
    user_sum_ref[...] = user_ref[...] + user_other_ref[...] + bias_ref[...]
    each = max(users // 2, 1)
    for index, pool_ref in ((low, mine_ref), (1 - low, other_ref)):
        for piece in range(each):
            user = index * each + piece if users > 1 else 0
            part = pl.ds(piece * (size // each), size // each)
            here = aligned(index * each + piece, size // each)
            base = cand_ref[here, :].astype(F32)
            total = pool_ref[part, :].astype(F32) + user_sum_ref[pl.ds(user, 1), :]
            rows_ref[here, :] = (base * total + base).astype(BF16)
    multiply(rows_ref, weight_ref, terms_ref, base_ref)
    cand = lax.axis_index("cand")
    add_own_columns(terms_ref, rows_ref, cand, lax.axis_index("mp"))
    if len(out_refs) == 1:
        out_refs[0][...] = terms_ref[...].astype(BF16)
        return
    for bit, out_ref in enumerate(out_refs):
        out_ref[...] = terms_ref[aligned(cand ^ bit, out_ref.shape[0]), :].astype(out_ref.dtype)


def cross_rows(base_ref, bias_ref, *refs):
    *part_refs, out_ref = refs
    total = part_refs[0][...].astype(F32)
    for part_ref in part_refs[1:]:
        total = total + part_ref[...].astype(F32)
    base = base_ref[aligned(lax.axis_index("cand"), out_ref.shape[0]), :].astype(F32)
    out_ref[...] = (total + base * bias_ref[...]).astype(BF16)


def split_low(axis_bit, terms_ref, keep_ref, send_ref, size):
    for pair in range(keep_ref.shape[0] // size):
        rows = pl.ds(pair * size, size)
        keep_ref[rows, :] = terms_ref[aligned(2 * pair + axis_bit, size), :]
        send_ref[rows, :] = terms_ref[aligned(2 * pair + 1 - axis_bit, size), :].astype(BF16)


def score_map(base_ref, score_ref, weight_ref, out_ref, rows_ref, score_row_ref):
    rows_ref[...] = (base_ref[...].astype(F32) * score_ref[...].astype(F32)).astype(BF16)
    for part in tiles(out_ref.shape[1]):
        out_ref[:, part] = lax.dot_general(
            rows_ref[...], weight_ref[part, :], (((1,), (1,)), ((), ())), preferred_element_type=F32
        )
    score_row_ref[...] = jnp.broadcast_to(score_ref[...].astype(F32), score_row_ref.shape)
    add_own_columns(out_ref, score_row_ref, lax.axis_index("cand"), lax.axis_index("mp"))


def score_rows(map_ref, base_ref, bias_ref, score_ref, *refs):
    *part_refs, rows_ref, logit_ref = refs
    cand = lax.axis_index("cand")
    if len(part_refs) == 1:
        rows_ref[...] = part_refs[0][...]
    else:
        for bit, part_ref in enumerate(part_refs):
            rows_ref[aligned(cand ^ bit, part_ref.shape[0]), :] = part_ref[...]
    once = (lax.axis_index("mp") == 0).astype(F32)
    blocks, size = logit_ref.shape
    lanes = 128
    for block in range(blocks):
        rows = pl.ds(block * size, size)
        total = jnp.zeros((size, lanes), F32)
        for start in range(0, map_ref.shape[1], lanes):
            cols = pl.ds(start, lanes)
            total = total + rows_ref[rows, cols].astype(F32) * map_ref[rows, cols]
        for start in range(0, base_ref.shape[1], lanes):
            cols = pl.ds(start, lanes)
            weight = bias_ref[:, cols] * score_ref[:, cols].astype(F32) * once
            total = total + base_ref[rows, cols].astype(F32) * weight
        logit_ref[pl.ds(block, 1), :] = jnp.sum(total.T, axis=0, keepdims=True)


def layer_three(row_block, base_ref, weight_ref, rows_ref, keep_ref, send_ref, terms_ref):
    multiply(rows_ref, weight_ref, terms_ref, base_ref)
    model = lax.axis_index("mp")
    add_own_columns(terms_ref, rows_ref, model, lax.axis_index("cand"))
    split_low(model % 2, terms_ref, keep_ref, send_ref, row_block)


def halve(row_block, bit, keep_ref, other_ref, kept_ref, send_ref, terms_ref):
    terms_ref[...] = keep_ref[...] + other_ref[...].astype(F32)
    split_low((lax.axis_index("mp") // bit) % 2, terms_ref, kept_ref, send_ref, row_block)


def finish(keep_ref, other_ref, base_ref, bias_ref, *refs):
    *part_refs, out_ref, logit_ref, sum_ref = refs
    model = lax.axis_index("mp")
    base = base_ref[aligned(model, out_ref.shape[0]), :].astype(F32)
    cross = keep_ref[...] + other_ref[...].astype(F32) + base * bias_ref[...]
    out_ref[...] = cross.astype(BF16)
    total = part_refs[0][...]
    for part_ref in part_refs[1:]:
        total = total + part_ref[...]
    sum_ref[...] = total
    logit_ref[...] = sum_ref[pl.ds(model, 1), :]


def body(
    user_feats,
    user_slot,
    cand_pool,
    cand_ids,
    first_weight,
    first_bias,
    second_weight,
    second_bias,
    third_weight,
    third_bias,
    score_weight,
):
    cand_count = lax.axis_size("cand")
    model_count = lax.axis_size("mp")
    local, half_width = user_feats.shape
    full_width = 2 * half_width
    user_count, per_user = cand_ids.shape
    row_total = user_count * per_user
    col_block = full_width // cand_count
    feat_block = full_width // model_count
    local_rows = row_total // cand_count
    row_block = row_total // model_count
    half_rows = row_total // 2
    flops = 2 * row_total * col_block * feat_block
    direct = cand_count <= DIRECT

    if local > 1:
        user_feats = jnp.take(user_feats, user_slot % local, axis=0)
    elif user_count > 1:
        user_feats = jnp.broadcast_to(user_feats, (user_count, half_width))
    (staged,) = call(stage, [((8, 128), F32)], [], flops=STAGE_FLOPS)
    users = user_feats
    pool_model, pool_cand = call(
        functools.partial(choose_pool, half_width),
        [
            ((row_total, feat_block), BF16),
            ((row_total, col_block), BF16),
        ],
        [cand_ids, cand_pool, staged],
        limit=8 * MIB,
    )
    (want,) = call(
        functools.partial(owner_steps, local),
        [((user_count, 128), jnp.int32)],
        [user_slot],
        smem=(0,),
    )
    if direct:
        users = [users] + [swap(users, "cand", bit) for bit in range(1, cand_count)]
    else:
        slots = user_slot.reshape(-1, 1)
        for bit in bits_of(cand_count):
            (users,) = call(
                functools.partial(choose_user, local, bit),
                [((user_count, half_width), BF16)],
                [slots, users, swap(users, "cand", bit)],
            )
        users = [users]

    half_outs = [((half_rows, col_block), F32), ((half_rows, col_block), BF16)]
    keep, send = call(
        functools.partial(pool_terms, half_width),
        half_outs,
        [pool_model, first_weight],
        scratch=[pltpu.VMEM((row_total, col_block), F32)],
        flops=flops,
        limit=12 * MIB,
    )
    for bit in bits_of(model_count):
        keep, send = call(add_up, half_outs, [keep, swap(send, "mp", bit)])
    pool_other = swap(send, "mp", 1)

    base_model, base_cand, user_sum = call(
        functools.partial(user_terms, half_width),
        [
            ((row_total, feat_block), BF16),
            ((row_total, col_block), BF16),
            ((user_count, col_block), F32),
        ],
        [want, first_weight, pool_model, pool_cand, *users],
        flops=flops,
        limit=12 * MIB,
    )
    *bits, last_bit = bits_of(model_count)
    for bit in bits:
        other = swap(user_sum, "mp", bit)
        (user_sum,) = call(add_to, [((user_count, col_block), F32)], [user_sum, other])
    user_other = swap(user_sum, "mp", last_bit)

    if direct:
        outs = [((local_rows, feat_block), BF16 if bit else F32) for bit in range(cand_count)]
    else:
        outs = [((row_total, feat_block), BF16)]
    parts = call(
        layer_two,
        outs,
        [
            keep, pool_other, user_sum, user_other, first_bias.reshape(1, -1), base_cand,
            base_model, second_weight,
        ],
        scratch=[
            pltpu.VMEM((row_total, col_block), BF16),
            pltpu.VMEM((row_total, feat_block), F32),
            pltpu.VMEM((user_count, col_block), F32),
        ],
        flops=flops,
        limit=12 * MIB,
    )
    if direct:
        parts = [parts[0]] + [swap(parts[bit], "cand", bit) for bit in range(1, cand_count)]
    else:
        parts = [lax.psum_scatter(parts[0], "cand", scatter_dimension=0, tiled=True)]
    score = score_weight.reshape(1, -1)
    (mapped,) = call(
        score_map,
        [((row_total, feat_block), F32)],
        [base_cand, score, third_weight],
        scratch=[pltpu.VMEM((row_total, col_block), BF16), pltpu.VMEM((row_total, col_block), F32)],
        flops=flops,
        limit=12 * MIB,
    )
    (block,) = call(
        cross_rows,
        [((local_rows, feat_block), BF16)],
        [base_model, second_bias.reshape(1, -1), *parts],
    )
    if direct:
        parts = [block] + [swap(block, "cand", bit) for bit in range(1, cand_count)]
    else:
        parts = [lax.all_gather(block, "cand", axis=0, tiled=True)]

    bias = third_bias.reshape(1, -1)
    logit_out = [((model_count, row_block), F32)]
    cross_two, logits = call(
        score_rows,
        [((row_total, feat_block), BF16)] + logit_out,
        [mapped, base_cand, bias, score, *parts],
    )
    rows = row_total // 2
    keep, send = call(
        functools.partial(layer_three, row_block),
        [((rows, col_block), F32), ((rows, col_block), BF16)],
        [base_cand, third_weight, cross_two],
        scratch=[pltpu.VMEM((row_total, col_block), F32)],
        flops=flops,
        limit=12 * MIB,
    )
    other = swap(send, "mp", 1)
    for bit in bits_of(model_count)[1:]:
        scratch = [pltpu.VMEM((rows, col_block), F32)]
        rows //= 2
        keep, send = call(
            functools.partial(halve, row_block, bit),
            [((rows, col_block), F32), ((rows, col_block), BF16)],
            [keep, other],
            scratch=scratch,
        )
        other = swap(send, "mp", bit)

    for bit in bits_of(model_count):
        (logits,) = call(add_to, logit_out, [logits, swap(logits, "mp", bit)])
    if direct:
        parts = [logits]
        parts += [swap(logits, "cand", bit) for bit in range(1, cand_count)]
    else:
        for bit in bits_of(cand_count):
            (logits,) = call(add_to, logit_out, [logits, swap(logits, "cand", bit)])
        parts = [logits]
    crossed, logits = call(
        finish,
        [((row_block, col_block), BF16), ((1, row_block), F32)],
        [keep, other, base_cand, bias, *parts],
        scratch=[pltpu.VMEM((model_count, row_block), F32)],
    )
    return (crossed, logits.reshape(-1))


def solution(mesh):
    in_specs = (
        P(("groups", "cand"), None),
        P("groups"),
        P("groups", None),
        P("groups", None),
        P("mp", "cand"),
        P("cand"),
        P("cand", "mp"),
        P("mp"),
        P("mp", "cand"),
        P("cand"),
        P("cand"),
    )
    out_specs = (P(("groups", "mp"), "cand"), P(("groups", "mp")))

    return jax.shard_map(body, mesh=mesh, in_specs=in_specs, out_specs=out_specs, check_vma=False)
```

profile of v0, /device:TPU:0, one launch (start us, length us, event | category | flops | bytes accessed | tf_op | source)
XLA Modules:
  0.0 64.5 jit_solution(15283648303104156019)
XLA Ops:
  0.7 0.6 copy-done.6
  1.3 1.0 %copy-done.1 = bf16[256,4096]{1,0:T(8,128)(2,1)S(1)} copy-done((bf16[256,4096]{1,0:T(8,128)(2,1)S(1)}, bf16[256,4096]{1,0:T(8,128)(2,1)}, u32[]{:S(2)}) %copy-start.1) | copy-done | bytes 2097176
  2.2 0.5 shard_map.124
  2.8 1.9 %copy-done = bf16[2048,2048]{1,0:T(8,128)(2,1)S(1)} copy-done((bf16[2048,2048]{1,0:T(8,128)(2,1)S(1)}, bf16[2048,2048]{1,0:T(8,128)(2,1)}, u32[]{:S(2)}) %copy-start) | copy-done | bytes 8388632
  4.7 0.6 collective-permute-start.3
  5.3 1.0 %collective-permute-done.3.other_ref = bf16[32,2048]{1,0:T(8,128)(2,1)S(1)} collective-permute-done((bf16[32,2048]{1,0:T(8,128)(2,1)S(1)}, bf16[32,2048]{1,0:T(8,128)(2,1)S(1)}, u32[]{:S(2)}, u32[]{:S(2)}) %collective-permute-start.3) | collective-permute-done | bytes 131104 | tf_op jit(solution)/shard_map/ppermute | solution.py:29
  6.3 4.5 %collective-permute-start.4 = (bf16[32,2048]{1,0:T(8,128)(2,1)S(1)}, bf16[32,2048]{1,0:T(8,128)(2,1)S(1)}, u32[]{:S(2)}, u32[]{:S(2)}) collective-permute-start(bf16[32,2048]{1,0:T(8,128)(2,1)S(1)} %get-tuple-element.32), channel_id=1, source_target_pairs={{0,2},{1,3},{2,0},{3,1},{4,6},{5,7},{6,4},{7,5},{8,10},{9,11},{10,... | collective-permute-start | bytes 393224 | tf_op jit(solution)/shard_map/ppermute | solution.py:29
  10.8 3.8 %collective-permute-done.4.other_ref = bf16[32,2048]{1,0:T(8,128)(2,1)S(1)} collective-permute-done((bf16[32,2048]{1,0:T(8,128)(2,1)S(1)}, bf16[32,2048]{1,0:T(8,128)(2,1)S(1)}, u32[]{:S(2)}, u32[]{:S(2)}) %collective-permute-start.4) | collective-permute-done | bytes 131104 | tf_op jit(solution)/shard_map/ppermute | solution.py:29
  14.7 0.1 collective-permute-start.5
  14.7 2.7 %collective-permute-start.1 = (bf16[1,4096]{1,0:T(2,128)(2,1)S(1)}, bf16[1,4096]{1,0:T(2,128)(2,1)S(1)}, u32[]{:S(2)}, u32[]{:S(2)}) collective-permute-start(bf16[1,4096]{1,0:T(2,128)(2,1)S(1)} %copy-done.3), channel_id=1, source_target_pairs={{0,8},{4,12},{8,0},{12,4},{1,9},{5,13},{9,1},{13,5},{2,10},{6,14},... | collective-permute-start | bytes 24584 | tf_op jit(solution)/shard_map/ppermute | solution.py:29
  17.4 1.6 %collective-permute-start = (bf16[1,4096]{1,0:T(2,128)(2,1)S(1)}, bf16[1,4096]{1,0:T(2,128)(2,1)S(1)}, u32[]{:S(2)}, u32[]{:S(2)}) collective-permute-start(bf16[1,4096]{1,0:T(2,128)(2,1)S(1)} %copy-done.3), channel_id=1, source_target_pairs={{0,4},{4,0},{8,12},{12,8},{1,5},{5,1},{9,13},{13,9},{2,6},{6,2},{1... | collective-permute-start | bytes 24584 | tf_op jit(solution)/shard_map/ppermute | solution.py:29
  19.0 0.2 collective-permute-start.2
  19.9 0.0 collective-permute-done.1.refs_2_
  19.9 1.3 %collective-permute-done.refs_1_ = bf16[1,4096]{1,0:T(2,128)(2,1)S(1)} collective-permute-done((bf16[1,4096]{1,0:T(2,128)(2,1)S(1)}, bf16[1,4096]{1,0:T(2,128)(2,1)S(1)}, u32[]{:S(2)}, u32[]{:S(2)}) %collective-permute-start) | collective-permute-done | bytes 8224 | tf_op jit(solution)/shard_map/ppermute | solution.py:29
  21.1 3.4 %collective-permute-done.2.refs_3_ = bf16[1,4096]{1,0:T(2,128)(2,1)S(1)} collective-permute-done((bf16[1,4096]{1,0:T(2,128)(2,1)S(1)}, bf16[1,4096]{1,0:T(2,128)(2,1)S(1)}, u32[]{:S(2)}, u32[]{:S(2)}) %collective-permute-start.2) | collective-permute-done | bytes 8224 | tf_op jit(solution)/shard_map/ppermute | solution.py:29
  24.5 1.3 %shard_map.125 = (bf16[64,2048]{1,0:T(8,128)(2,1)S(1)}, bf16[64,2048]{1,0:T(8,128)(2,1)S(1)}, f32[1,2048]{1,0:T(1,128)S(1)}) custom-call(s32[1,128]{1,0:T(1,128)S(1)} %shard_map.122.want_ref, bf16[2048,2048]{1,0:T(8,128)(2,1)S(1)} %copy-done, bf16[64,2048]{1,0:T(8,128)(2,1)S(1)} %get-tuple-element.25.pool_model_ref.rows_ref, ...), custom_call_target="tpu_custom_call" | custom-call | flops 536870912 | bytes 1090048 | tf_op jit(solution)/shard_map/pallas_call | solution.py:35
  25.9 0.1 collective-permute-start.6
  25.9 1.2 %collective-permute-done.6.refs_1_ = f32[1,2048]{1,0:T(1,128)S(1)} collective-permute-done((f32[1,2048]{1,0:T(1,128)S(1)}, f32[1,2048]{1,0:T(1,128)S(1)}, u32[]{:S(2)}, u32[]{:S(2)}) %collective-permute-start.6) | collective-permute-done | bytes 8224 | tf_op jit(solution)/shard_map/ppermute | solution.py:29
  27.1 0.5 collective-permute-start.7
  27.6 3.1 %collective-permute-done.7.user_other_ref = f32[1,2048]{1,0:T(1,128)S(1)} collective-permute-done((f32[1,2048]{1,0:T(1,128)S(1)}, f32[1,2048]{1,0:T(1,128)S(1)}, u32[]{:S(2)}, u32[]{:S(2)}) %collective-permute-start.7) | collective-permute-done | bytes 8224 | tf_op jit(solution)/shard_map/ppermute | solution.py:29
  30.8 0.0 collective-permute-done.5.other_ref
  30.8 0.0 slice-start.1
  30.8 0.0 copy-start.2
  30.8 1.7 %shard_map.131 = (f32[16,2048]{1,0:T(8,128)S(1)}, bf16[16,2048]{1,0:T(8,128)(2,1)S(1)}, bf16[16,2048]{1,0:T(8,128)(2,1)S(1)}, bf16[16,2048]{1,0:T(8,128)(2,1)S(1)}) custom-call(f32[32,2048]{1,0:T(8,128)S(1)} %get-tuple-element.33.mine_ref, bf16[32,2048]{1,0:T(8,128)(2,1)S(1)} %collective-permute-done.5.other_ref, f32[1,2048]{1,0:T(1,128)S(1)} %shard_map.130.user_ref, ...), custom_call_target="tpu_custom_call" | custom-call | flops 536870912 | bytes 1269760 | tf_op jit(solution)/shard_map/pallas_call | solution.py:35
  32.5 0.1 collective-permute-start.8
  32.6 0.7 %collective-permute-start.9 = (bf16[16,2048]{1,0:T(8,128)(2,1)S(1)}, bf16[16,2048]{1,0:T(8,128)(2,1)S(1)}, u32[]{:S(2)}, u32[]{:S(2)}) collective-permute-start(bf16[16,2048]{1,0:T(8,128)(2,1)S(1)} %get-tuple-element.38), channel_id=1, source_target_pairs={{0,8},{4,12},{8,0},{12,4},{1,9},{5,13},{9,1},{13,5},{2,10},{6,14},... | collective-permute-start | bytes 196616 | tf_op jit(solution)/shard_map/ppermute | solution.py:29
  33.3 3.7 %collective-permute-start.10 = (bf16[16,2048]{1,0:T(8,128)(2,1)S(1)}, bf16[16,2048]{1,0:T(8,128)(2,1)S(1)}, u32[]{:S(2)}, u32[]{:S(2)}) collective-permute-start(bf16[16,2048]{1,0:T(8,128)(2,1)S(1)} %get-tuple-element.39), channel_id=1, source_target_pairs={{0,12},{4,8},{8,4},{12,0},{1,13},{5,9},{9,5},{13,1},{2,14},{6,10},... | collective-permute-start | bytes 196616 | tf_op jit(solution)/shard_map/ppermute | solution.py:29
  37.0 0.0 collective-permute-done.8.refs_1_
  37.0 3.1 %collective-permute-done.9.refs_2_ = bf16[16,2048]{1,0:T(8,128)(2,1)S(1)} collective-permute-done((bf16[16,2048]{1,0:T(8,128)(2,1)S(1)}, bf16[16,2048]{1,0:T(8,128)(2,1)S(1)}, u32[]{:S(2)}, u32[]{:S(2)}) %collective-permute-start.9) | collective-permute-done | bytes 65568 | tf_op jit(solution)/shard_map/ppermute | solution.py:29
  40.0 0.0 collective-permute-done.10.refs_3_
  40.1 3.1 %collective-permute-start.13 = (bf16[16,2048]{1,0:T(8,128)(2,1)S(1)}, bf16[16,2048]{1,0:T(8,128)(2,1)S(1)}, u32[]{:S(2)}, u32[]{:S(2)}) collective-permute-start(bf16[16,2048]{1,0:T(8,128)(2,1)S(1)} %shard_map.132.refs_0_), channel_id=1, source_target_pairs={{0,12},{4,8},{8,4},{12,0},{1,13},{5,9},{9,5},{13,1},{2,14},{6,10},... | collective-permute-start | bytes 196616 | tf_op jit(solution)/shard_map/ppermute | solution.py:29
  43.3 1.3 %collective-permute-start.11 = (bf16[16,2048]{1,0:T(8,128)(2,1)S(1)}, bf16[16,2048]{1,0:T(8,128)(2,1)S(1)}, u32[]{:S(2)}, u32[]{:S(2)}) collective-permute-start(bf16[16,2048]{1,0:T(8,128)(2,1)S(1)} %shard_map.132.refs_0_), channel_id=1, source_target_pairs={{0,4},{4,0},{8,12},{12,8},{1,5},{5,1},{9,13},{13,9},{2,6},{6,2},{1... | collective-permute-start | bytes 196616 | tf_op jit(solution)/shard_map/ppermute | solution.py:29
  44.6 2.7 %shard_map.126.map_ref = f32[64,2048]{1,0:T(8,128)S(1)} custom-call(bf16[64,2048]{1,0:T(8,128)(2,1)S(1)} %get-tuple-element.27.base_ref.cand_ref, bf16[1,2048]{1,0:T(2,128)(2,1)S(1)} %reshape.19.score_ref, bf16[2048,2048]{1,0:T(8,128)(2,1)S(1)} %bitcast.5), custom_call_target="tpu_custom_call" | custom-call | flops 536870912 | bytes 790528 | tf_op jit(solution)/shard_map/pallas_call | solution.py:35
  47.3 0.0 collective-permute-done.13.refs_3_
  47.3 1.1 %collective-permute-done.12.refs_2_ = bf16[16,2048]{1,0:T(8,128)(2,1)S(1)} collective-permute-done((bf16[16,2048]{1,0:T(8,128)(2,1)S(1)}, bf16[16,2048]{1,0:T(8,128)(2,1)S(1)}, u32[]{:S(2)}, u32[]{:S(2)}) %collective-permute-start.12) | collective-permute-done | bytes 65568 | tf_op jit(solution)/shard_map/ppermute | solution.py:29
  48.4 0.3 shard_map.133
  48.7 1.7 %shard_map.134 = (f32[32,2048]{1,0:T(8,128)S(1)}, bf16[32,2048]{1,0:T(8,128)(2,1)S(1)}) custom-call(bf16[64,2048]{1,0:T(8,128)(2,1)S(1)} %get-tuple-element.27.base_ref.cand_ref, bf16[2048,2048]{1,0:T(8,128)(2,1)S(1)} %bitcast.5, bf16[64,2048]{1,0:T(8,128)(2,1)S(1)} %get-tuple-element.40.rows_ref), custom_call_target="tpu_custom_call" | custom-call | flops 536870912 | bytes 917504 | tf_op jit(solution)/shard_map/pallas_call | solution.py:35
  50.4 0.1 collective-permute-start.14
  50.5 1.3 %collective-permute-done.14.other_ref = bf16[32,2048]{1,0:T(8,128)(2,1)S(1)} collective-permute-done((bf16[32,2048]{1,0:T(8,128)(2,1)S(1)}, bf16[32,2048]{1,0:T(8,128)(2,1)S(1)}, u32[]{:S(2)}, u32[]{:S(2)}) %collective-permute-start.14) | collective-permute-done | bytes 131104 | tf_op jit(solution)/shard_map/ppermute | solution.py:29
  51.8 0.5 collective-permute-start.15
  52.4 1.2 %collective-permute-done.16.refs_1_ = f32[4,16]{1,0:T(4,128)S(1)} collective-permute-done((f32[4,16]{1,0:T(4,128)S(1)}, f32[4,16]{1,0:T(4,128)S(1)}, u32[]{:S(2)}, u32[]{:S(2)}) %collective-permute-start.16) | collective-permute-done | bytes 288 | tf_op jit(solution)/shard_map/ppermute | solution.py:29
  53.5 1.6 %collective-permute-start.17 = (f32[4,16]{1,0:T(4,128)S(1)}, f32[4,16]{1,0:T(4,128)S(1)}, u32[]{:S(2)}, u32[]{:S(2)}) collective-permute-start(f32[4,16]{1,0:T(4,128)S(1)} %shard_map.136.refs_0_), channel_id=1, source_target_pairs={{0,2},{1,3},{2,0},{3,1},{4,6},{5,7},{6,4},{7,5},{8,10},{9,11},{10,... | collective-permute-start | bytes 776 | tf_op jit(solution)/shard_map/ppermute | solution.py:29
  55.1 2.0 %collective-permute-done.17.refs_1_ = f32[4,16]{1,0:T(4,128)S(1)} collective-permute-done((f32[4,16]{1,0:T(4,128)S(1)}, f32[4,16]{1,0:T(4,128)S(1)}, u32[]{:S(2)}, u32[]{:S(2)}) %collective-permute-start.17) | collective-permute-done | bytes 288 | tf_op jit(solution)/shard_map/ppermute | solution.py:29
  57.1 2.2 %collective-permute-start.20 = (f32[4,16]{1,0:T(4,128)S(1)}, f32[4,16]{1,0:T(4,128)S(1)}, u32[]{:S(2)}, u32[]{:S(2)}) collective-permute-start(f32[4,16]{1,0:T(4,128)S(1)} %shard_map.137.refs_0_), channel_id=1, source_target_pairs={{0,12},{4,8},{8,4},{12,0},{1,13},{5,9},{9,5},{13,1},{2,14},{6,10},... | collective-permute-start | bytes 776 | tf_op jit(solution)/shard_map/ppermute | solution.py:29
  59.3 2.2 %collective-permute-start.18 = (f32[4,16]{1,0:T(4,128)S(1)}, f32[4,16]{1,0:T(4,128)S(1)}, u32[]{:S(2)}, u32[]{:S(2)}) collective-permute-start(f32[4,16]{1,0:T(4,128)S(1)} %shard_map.137.refs_0_), channel_id=1, source_target_pairs={{0,4},{4,0},{8,12},{12,8},{1,5},{5,1},{9,13},{13,9},{2,6},{6,2},{1... | collective-permute-start | bytes 776 | tf_op jit(solution)/shard_map/ppermute | solution.py:29
  61.5 1.0 %collective-permute-done.20.refs_3_ = f32[4,16]{1,0:T(4,128)S(1)} collective-permute-done((f32[4,16]{1,0:T(4,128)S(1)}, f32[4,16]{1,0:T(4,128)S(1)}, u32[]{:S(2)}, u32[]{:S(2)}) %collective-permute-start.20) | collective-permute-done | bytes 288 | tf_op jit(solution)/shard_map/ppermute | solution.py:29
  62.5 1.3 %collective-permute-done.19.refs_2_ = f32[4,16]{1,0:T(4,128)S(1)} collective-permute-done((f32[4,16]{1,0:T(4,128)S(1)}, f32[4,16]{1,0:T(4,128)S(1)}, u32[]{:S(2)}, u32[]{:S(2)}) %collective-permute-start.19) | collective-permute-done | bytes 288 | tf_op jit(solution)/shard_map/ppermute | solution.py:29
  63.8 0.7 %shard_map.138 = (bf16[16,2048]{1,0:T(8,128)(2,1)}, f32[1,16]{1,0:T(1,128)}) custom-call(f32[16,2048]{1,0:T(8,128)S(1)} %get-tuple-element.43.keep_ref, bf16[16,2048]{1,0:T(8,128)(2,1)S(1)} %collective-permute-done.15.other_ref, bf16[64,2048]{1,0:T(8,128)(2,1)S(1)} %get-tuple-element.27.base_ref.cand_ref, f32[1,2048]{1,0:T(1,128)S(1)} %bitcast.9, ...), custom_call_target="tpu_custom_call" | custom-call | bytes 533568 | tf_op jit(solution)/shard_map/pallas_call | solution.py:35
  (38 shorter events, 0.3 us)
Async XLA Ops:
  0.6 0.7 %copy-start.6 = (s32[1,64]{1,0:T(1,128)S(1)}, s32[1,64]{1,0:T(1,128)}, u32[]{:S(2)}) copy-start(s32[1,64]{1,0:T(1,128)} %ids_ref.1) | copy-start | bytes 772
  0.6 1.6 %copy-start.1 = (bf16[256,4096]{1,0:T(8,128)(2,1)S(1)}, bf16[256,4096]{1,0:T(8,128)(2,1)}, u32[]{:S(2)}) copy-start(bf16[256,4096]{1,0:T(8,128)(2,1)} %pool_ref.1) | copy-start | bytes 6291460
  0.7 4.0 %copy-start = (bf16[2048,2048]{1,0:T(8,128)(2,1)S(1)}, bf16[2048,2048]{1,0:T(8,128)(2,1)}, u32[]{:S(2)}) copy-start(bf16[2048,2048]{1,0:T(8,128)(2,1)} %weight_ref.7) | copy-start | bytes 25165828
  2.2 12.5 %copy-start.3 = (bf16[1,4096]{1,0:T(2,128)(2,1)S(1)}, bf16[1,4096]{1,0:T(2,128)(2,1)}, u32[]{:S(2)}) copy-start(bf16[1,4096]{1,0:T(2,128)(2,1)} %refs_0_.1) | copy-start | bytes 24580
  4.7 26.1 %slice-start.2 = ((s8[8388608]{0:T(1024)(128)(4,1)}), s8[4194304]{0:T(1024)(128)(4,1)S(1)}, s32[]{:S(2)}) async-start(s8[8388608]{0:T(1024)(128)(4,1)} %bitcast.6), calls=%async_computation.2 | async-start | bytes 8388608
  4.7 26.1 %copy-start.5 = (f32[2048]{0:T(1024)S(1)}, f32[2048]{0:T(1024)}, u32[]{:S(2)}) copy-start(f32[2048]{0:T(1024)} %param.16) | copy-start | bytes 24580
  4.7 1.5 %collective-permute-start.3 = (bf16[32,2048]{1,0:T(8,128)(2,1)S(1)}, bf16[32,2048]{1,0:T(8,128)(2,1)S(1)}, u32[]{:S(2)}, u32[]{:S(2)}) collective-permute-start(bf16[32,2048]{1,0:T(8,128)(2,1)S(1)} %get-tuple-element.30), channel_id=1, source_target_pairs={{0,1},{1,0},{2,3},{3,2},{4,5},{5,4},{6,7},{7,6},{8,9},{9,8},{10,11... | collective-permute-start | bytes 393224 | tf_op jit(solution)/shard_map/ppermute | solution.py:29
  6.3 8.3 %collective-permute-start.4 = (bf16[32,2048]{1,0:T(8,128)(2,1)S(1)}, bf16[32,2048]{1,0:T(8,128)(2,1)S(1)}, u32[]{:S(2)}, u32[]{:S(2)}) collective-permute-start(bf16[32,2048]{1,0:T(8,128)(2,1)S(1)} %get-tuple-element.32), channel_id=1, source_target_pairs={{0,2},{1,3},{2,0},{3,1},{4,6},{5,7},{6,4},{7,5},{8,10},{9,11},{10,... | collective-permute-start | bytes 393224 | tf_op jit(solution)/shard_map/ppermute | solution.py:29
  14.6 16.2 %slice-start.3 = ((s8[8388608]{0:T(1024)(128)(4,1)}), s8[4194304]{0:T(1024)(128)(4,1)S(1)}, s32[]{:S(2)}) async-start(s8[8388608]{0:T(1024)(128)(4,1)} %bitcast.6), calls=%async_computation.3 | async-start | bytes 8388608
  14.7 16.1 %collective-permute-start.5 = (bf16[32,2048]{1,0:T(8,128)(2,1)S(1)}, bf16[32,2048]{1,0:T(8,128)(2,1)S(1)}, u32[]{:S(2)}, u32[]{:S(2)}) collective-permute-start(bf16[32,2048]{1,0:T(8,128)(2,1)S(1)} %get-tuple-element.34), channel_id=1, source_target_pairs={{0,1},{1,0},{2,3},{3,2},{4,5},{5,4},{6,7},{7,6},{8,9},{9,8},{10,11... | collective-permute-start | bytes 393224 | tf_op jit(solution)/shard_map/ppermute | solution.py:29
  14.7 5.1 %collective-permute-start.1 = (bf16[1,4096]{1,0:T(2,128)(2,1)S(1)}, bf16[1,4096]{1,0:T(2,128)(2,1)S(1)}, u32[]{:S(2)}, u32[]{:S(2)}) collective-permute-start(bf16[1,4096]{1,0:T(2,128)(2,1)S(1)} %copy-done.3), channel_id=1, source_target_pairs={{0,8},{4,12},{8,0},{12,4},{1,9},{5,13},{9,1},{13,5},{2,10},{6,14},... | collective-permute-start | bytes 24584 | tf_op jit(solution)/shard_map/ppermute | solution.py:29
  17.4 3.7 %collective-permute-start = (bf16[1,4096]{1,0:T(2,128)(2,1)S(1)}, bf16[1,4096]{1,0:T(2,128)(2,1)S(1)}, u32[]{:S(2)}, u32[]{:S(2)}) collective-permute-start(bf16[1,4096]{1,0:T(2,128)(2,1)S(1)} %copy-done.3), channel_id=1, source_target_pairs={{0,4},{4,0},{8,12},{12,8},{1,5},{5,1},{9,13},{13,9},{2,6},{6,2},{1... | collective-permute-start | bytes 24584 | tf_op jit(solution)/shard_map/ppermute | solution.py:29
  19.0 5.5 %collective-permute-start.2 = (bf16[1,4096]{1,0:T(2,128)(2,1)S(1)}, bf16[1,4096]{1,0:T(2,128)(2,1)S(1)}, u32[]{:S(2)}, u32[]{:S(2)}) collective-permute-start(bf16[1,4096]{1,0:T(2,128)(2,1)S(1)} %copy-done.3), channel_id=1, source_target_pairs={{0,12},{4,8},{8,4},{12,0},{1,13},{5,9},{9,5},{13,1},{2,14},{6,10},... | collective-permute-start | bytes 24584 | tf_op jit(solution)/shard_map/ppermute | solution.py:29
  24.5 15.5 %copy-start.4 = (f32[2048]{0:T(1024)S(1)}, f32[2048]{0:T(1024)}, u32[]{:S(2)}) copy-start(f32[2048]{0:T(1024)} %param.18) | copy-start | bytes 24580
  24.5 20.1 %copy-start.7 = (bf16[2048]{0:T(1024)(128)(2,1)S(1)}, bf16[2048]{0:T(1024)(128)(2,1)}, u32[]{:S(2)}) copy-start(bf16[2048]{0:T(1024)(128)(2,1)} %param.21) | copy-start | bytes 12292
  24.5 20.1 %slice-start = ((s8[8388608]{0:T(1024)(128)(4,1)}), s8[4194304]{0:T(1024)(128)(4,1)S(1)}, s32[]{:S(2)}) async-start(s8[8388608]{0:T(1024)(128)(4,1)} %bitcast.4), calls=%async_computation | async-start | bytes 8388608
  25.9 1.2 %collective-permute-start.6 = (f32[1,2048]{1,0:T(1,128)S(1)}, f32[1,2048]{1,0:T(1,128)S(1)}, u32[]{:S(2)}, u32[]{:S(2)}) collective-permute-start(f32[1,2048]{1,0:T(1,128)S(1)} %get-tuple-element.35.refs_0_), channel_id=1, source_target_pairs={{0,1},{1,0},{2,3},{3,2},{4,5},{5,4},{6,7},{7,6},{8,9},{9,8},{10,11... | collective-permute-start | bytes 24584 | tf_op jit(solution)/shard_map/ppermute | solution.py:29
  27.1 3.7 %collective-permute-start.7 = (f32[1,2048]{1,0:T(1,128)S(1)}, f32[1,2048]{1,0:T(1,128)S(1)}, u32[]{:S(2)}, u32[]{:S(2)}) collective-permute-start(f32[1,2048]{1,0:T(1,128)S(1)} %shard_map.130.user_ref), channel_id=1, source_target_pairs={{0,2},{1,3},{2,0},{3,1},{4,6},{5,7},{6,4},{7,5},{8,10},{9,11},{10,... | collective-permute-start | bytes 24584 | tf_op jit(solution)/shard_map/ppermute | solution.py:29
  30.8 13.8 %slice-start.1 = ((s8[8388608]{0:T(1024)(128)(4,1)}), s8[4194304]{0:T(1024)(128)(4,1)S(1)}, s32[]{:S(2)}) async-start(s8[8388608]{0:T(1024)(128)(4,1)} %bitcast.4), calls=%async_computation.1 | async-start | bytes 8388608
  30.8 17.6 %copy-start.2 = (f32[2048]{0:T(1024)S(1)}, f32[2048]{0:T(1024)}, u32[]{:S(2)}) copy-start(f32[2048]{0:T(1024)} %param.20) | copy-start | bytes 24580
  32.5 4.5 %collective-permute-start.8 = (bf16[16,2048]{1,0:T(8,128)(2,1)S(1)}, bf16[16,2048]{1,0:T(8,128)(2,1)S(1)}, u32[]{:S(2)}, u32[]{:S(2)}) collective-permute-start(bf16[16,2048]{1,0:T(8,128)(2,1)S(1)} %get-tuple-element.37), channel_id=1, source_target_pairs={{0,4},{4,0},{8,12},{12,8},{1,5},{5,1},{9,13},{13,9},{2,6},{6,2},{1... | collective-permute-start | bytes 196616 | tf_op jit(solution)/shard_map/ppermute | solution.py:29
  32.6 7.5 %collective-permute-start.9 = (bf16[16,2048]{1,0:T(8,128)(2,1)S(1)}, bf16[16,2048]{1,0:T(8,128)(2,1)S(1)}, u32[]{:S(2)}, u32[]{:S(2)}) collective-permute-start(bf16[16,2048]{1,0:T(8,128)(2,1)S(1)} %get-tuple-element.38), channel_id=1, source_target_pairs={{0,8},{4,12},{8,0},{12,4},{1,9},{5,13},{9,1},{13,5},{2,10},{6,14},... | collective-permute-start | bytes 196616 | tf_op jit(solution)/shard_map/ppermute | solution.py:29
  33.3 6.8 %collective-permute-start.10 = (bf16[16,2048]{1,0:T(8,128)(2,1)S(1)}, bf16[16,2048]{1,0:T(8,128)(2,1)S(1)}, u32[]{:S(2)}, u32[]{:S(2)}) collective-permute-start(bf16[16,2048]{1,0:T(8,128)(2,1)S(1)} %get-tuple-element.39), channel_id=1, source_target_pairs={{0,12},{4,8},{8,4},{12,0},{1,13},{5,9},{9,5},{13,1},{2,14},{6,10},... | collective-permute-start | bytes 196616 | tf_op jit(solution)/shard_map/ppermute | solution.py:29
  40.1 7.2 %collective-permute-start.13 = (bf16[16,2048]{1,0:T(8,128)(2,1)S(1)}, bf16[16,2048]{1,0:T(8,128)(2,1)S(1)}, u32[]{:S(2)}, u32[]{:S(2)}) collective-permute-start(bf16[16,2048]{1,0:T(8,128)(2,1)S(1)} %shard_map.132.refs_0_), channel_id=1, source_target_pairs={{0,12},{4,8},{8,4},{12,0},{1,13},{5,9},{9,5},{13,1},{2,14},{6,10},... | collective-permute-start | bytes 196616 | tf_op jit(solution)/shard_map/ppermute | solution.py:29
  43.3 5.2 %collective-permute-start.12 = (bf16[16,2048]{1,0:T(8,128)(2,1)S(1)}, bf16[16,2048]{1,0:T(8,128)(2,1)S(1)}, u32[]{:S(2)}, u32[]{:S(2)}) collective-permute-start(bf16[16,2048]{1,0:T(8,128)(2,1)S(1)} %shard_map.132.refs_0_), channel_id=1, source_target_pairs={{0,8},{4,12},{8,0},{12,4},{1,9},{5,13},{9,1},{13,5},{2,10},{6,14},... | collective-permute-start | bytes 196616 | tf_op jit(solution)/shard_map/ppermute | solution.py:29
  43.3 5.2 %collective-permute-start.11 = (bf16[16,2048]{1,0:T(8,128)(2,1)S(1)}, bf16[16,2048]{1,0:T(8,128)(2,1)S(1)}, u32[]{:S(2)}, u32[]{:S(2)}) collective-permute-start(bf16[16,2048]{1,0:T(8,128)(2,1)S(1)} %shard_map.132.refs_0_), channel_id=1, source_target_pairs={{0,4},{4,0},{8,12},{12,8},{1,5},{5,1},{9,13},{13,9},{2,6},{6,2},{1... | collective-permute-start | bytes 196616 | tf_op jit(solution)/shard_map/ppermute | solution.py:29
  50.4 1.4 %collective-permute-start.14 = (bf16[32,2048]{1,0:T(8,128)(2,1)S(1)}, bf16[32,2048]{1,0:T(8,128)(2,1)S(1)}, u32[]{:S(2)}, u32[]{:S(2)}) collective-permute-start(bf16[32,2048]{1,0:T(8,128)(2,1)S(1)} %get-tuple-element.42), channel_id=1, source_target_pairs={{0,1},{1,0},{2,3},{3,2},{4,5},{5,4},{6,7},{7,6},{8,9},{9,8},{10,11... | collective-permute-start | bytes 393224 | tf_op jit(solution)/shard_map/ppermute | solution.py:29
  51.8 11.9 %collective-permute-start.15 = (bf16[16,2048]{1,0:T(8,128)(2,1)S(1)}, bf16[16,2048]{1,0:T(8,128)(2,1)S(1)}, u32[]{:S(2)}, u32[]{:S(2)}) collective-permute-start(bf16[16,2048]{1,0:T(8,128)(2,1)S(1)} %get-tuple-element.44), channel_id=1, source_target_pairs={{0,2},{1,3},{2,0},{3,1},{4,6},{5,7},{6,4},{7,5},{8,10},{9,11},{10,... | collective-permute-start | bytes 196616 | tf_op jit(solution)/shard_map/ppermute | solution.py:29
  52.4 1.2 %collective-permute-start.16 = (f32[4,16]{1,0:T(4,128)S(1)}, f32[4,16]{1,0:T(4,128)S(1)}, u32[]{:S(2)}, u32[]{:S(2)}) collective-permute-start(f32[4,16]{1,0:T(4,128)S(1)} %get-tuple-element.45.refs_0_), channel_id=1, source_target_pairs={{0,1},{1,0},{2,3},{3,2},{4,5},{5,4},{6,7},{7,6},{8,9},{9,8},{10,11... | collective-permute-start | bytes 776 | tf_op jit(solution)/shard_map/ppermute | solution.py:29
  53.5 3.6 %collective-permute-start.17 = (f32[4,16]{1,0:T(4,128)S(1)}, f32[4,16]{1,0:T(4,128)S(1)}, u32[]{:S(2)}, u32[]{:S(2)}) collective-permute-start(f32[4,16]{1,0:T(4,128)S(1)} %shard_map.136.refs_0_), channel_id=1, source_target_pairs={{0,2},{1,3},{2,0},{3,1},{4,6},{5,7},{6,4},{7,5},{8,10},{9,11},{10,... | collective-permute-start | bytes 776 | tf_op jit(solution)/shard_map/ppermute | solution.py:29
  57.1 5.4 %collective-permute-start.20 = (f32[4,16]{1,0:T(4,128)S(1)}, f32[4,16]{1,0:T(4,128)S(1)}, u32[]{:S(2)}, u32[]{:S(2)}) collective-permute-start(f32[4,16]{1,0:T(4,128)S(1)} %shard_map.137.refs_0_), channel_id=1, source_target_pairs={{0,12},{4,8},{8,4},{12,0},{1,13},{5,9},{9,5},{13,1},{2,14},{6,10},... | collective-permute-start | bytes 776 | tf_op jit(solution)/shard_map/ppermute | solution.py:29
  59.3 4.5 %collective-permute-start.19 = (f32[4,16]{1,0:T(4,128)S(1)}, f32[4,16]{1,0:T(4,128)S(1)}, u32[]{:S(2)}, u32[]{:S(2)}) collective-permute-start(f32[4,16]{1,0:T(4,128)S(1)} %shard_map.137.refs_0_), channel_id=1, source_target_pairs={{0,8},{4,12},{8,0},{12,4},{1,9},{5,13},{9,1},{13,5},{2,10},{6,14},... | collective-permute-start | bytes 776 | tf_op jit(solution)/shard_map/ppermute | solution.py:29
  59.3 4.5 %collective-permute-start.18 = (f32[4,16]{1,0:T(4,128)S(1)}, f32[4,16]{1,0:T(4,128)S(1)}, u32[]{:S(2)}, u32[]{:S(2)}) collective-permute-start(f32[4,16]{1,0:T(4,128)S(1)} %shard_map.137.refs_0_), channel_id=1, source_target_pairs={{0,4},{4,0},{8,12},{12,8},{1,5},{5,1},{9,13},{13,9},{2,6},{6,2},{1... | collective-permute-start | bytes 776 | tf_op jit(solution)/shard_map/ppermute | solution.py:29
where the time goes:
time: 64.6 us; the launch traced here: 64.5 us
  starting transfers between devices  25.6 us (40%)
  waiting for transfers between devices  24.7 us (38%)
  Pallas kernels  9.07 us (14%)
  local copies, waits for them, and re-layouts  3.54 us (5%)
  between operations  1.53 us (2%)
    ppermute x21, starting transfers between devices, swap(): return lax.ppermute(value, axis, [(i, i ^ bit) for i in range(count)])  25.6 us
    ppermute x21, waiting for transfers between devices, swap(): return lax.ppermute(value, axis, [(i, i ^ bit) for i in range(count)])  24.7 us
    pallas_call x17, Pallas kernels, call(): pl.pallas_call(kernel, out_shape=[jax.ShapeDtypeStruct(s, d) for s, d in...  9.07 us
    unnamed x24, local copies, waits for them, and re-layouts  3.53 us
  transfers between devices with their start and end apart: 21, of which 13 were waited for; matrix products, arithmetic and copies ran while one was open for 0% of the time, Pallas kernels for 6%

commit v1 on v0

--- a/solution.py
+++ b/solution.py
@@ -10,6 +10,7 @@
 
 F32 = jnp.float32
 BF16 = jnp.bfloat16
+LANES = 128
 DIRECT = 4
 MIB = 1024 * 1024
 STAGE_FLOPS = 1 << 34
@@ -220,6 +221,90 @@
     out_ref[...] = (total + base * bias_ref[...]).astype(BF16)
 
 
+def score_map(half, users, base_ref, score_ref, bias_ref, weight_ref, *refs):
+    *out_refs, rows_ref, map_ref, score_row_ref = refs
+    rows, width = base_ref.shape
+    columns = map_ref.shape[1]
+    each = rows // users
+    inside = lax.axis_index("cand") < half // width
+    score = score_ref[...].astype(F32)
+
+    def product(count):
+        for part in tiles(columns):
+            map_ref[pl.ds(0, count), part] = lax.dot_general(
+                rows_ref[pl.ds(0, count), :],
+                weight_ref[part, :],
+                (((1,), (1,)), ((), ())),
+                preferred_element_type=F32,
+            )
+
+    @pl.when(inside)
+    def _():
+        small = max(users, 16)
+        score_row_ref[pl.ds(0, small), :] = jnp.zeros((small, width), F32)
+        for user in range(users):
+            base = base_ref[pl.ds(user * each, each), :].astype(F32)[:1]
+            score_row_ref[pl.ds(user, 1), :] = base * score
+        rows_ref[pl.ds(0, small), :] = score_row_ref[pl.ds(0, small), :].astype(BF16)
+        product(small)
+        for user in reversed(range(users)):
+            row = map_ref[pl.ds(user, 1), :]
+            map_ref[pl.ds(user * each, each), :] = jnp.broadcast_to(row, (each, columns))
+
+    @pl.when(jnp.logical_not(inside))
+    def _():
+        rows_ref[...] = (base_ref[...].astype(F32) * score).astype(BF16)
+        product(rows)
+
+    score_row_ref[...] = jnp.broadcast_to(score, score_row_ref.shape)
+    add_own_columns(map_ref, score_row_ref, lax.axis_index("cand"), lax.axis_index("mp"))
+    weight = bias_ref[...] * score
+    for bit, out_ref in enumerate(out_refs):
+        size = out_ref.shape[0]
+        block = aligned(lax.axis_index("cand") ^ bit, size)
+        out_ref[:, pl.ds(0, columns)] = map_ref[block, :].astype(out_ref.dtype)
+        total = jnp.zeros((size, LANES), F32)
+        for start in range(0, width, LANES):
+            cols = pl.ds(start, LANES)
+            total = total + base_ref[block, cols].astype(F32) * weight[:, start : start + LANES]
+        out_ref[:, pl.ds(columns, LANES)] = total.astype(out_ref.dtype)
+
+
+def cross_scored(count, base_ref, bias_ref, *refs):
+    part_refs, map_refs, (out_ref,) = refs[:count], refs[count : 2 * count], refs[2 * count :]
+    size, width = part_refs[0].shape
+    base = base_ref[aligned(lax.axis_index("cand"), size), :].astype(F32)
+    once = (lax.axis_index("mp") == 0).astype(F32)
+
+    def added(refs, cols):
+        total = refs[0][:, cols].astype(F32)
+        for ref in refs[1:]:
+            total = total + ref[:, cols].astype(F32)
+        return total
+
+    score = added(map_refs, pl.ds(width, LANES)) * once
+    for start in range(0, width, LANES):
+        cols = pl.ds(start, LANES)
+        cross = added(part_refs, cols) + base[:, start : start + LANES] * bias_ref[:, cols]
+        rounded = cross.astype(BF16)
+        out_ref[:, cols] = rounded
+        score = score + rounded.astype(F32) * added(map_refs, cols)
+    high = score.astype(BF16)
+    out_ref[:, pl.ds(width, LANES)] = high
+    out_ref[:, pl.ds(width + LANES, LANES)] = (score - high.astype(F32)).astype(BF16)
+
+
+def assemble(*refs):
+    *part_refs, rows_ref, logit_ref = refs
+    width = rows_ref.shape[1]
+    for bit, part_ref in enumerate(part_refs):
+        block = lax.axis_index("cand") ^ bit
+        rows_ref[aligned(block, part_ref.shape[0]), :] = part_ref[:, pl.ds(0, width)]
+        lanes = part_ref[:, pl.ds(width, LANES)].astype(F32)
+        lanes = lanes + part_ref[:, pl.ds(width + LANES, LANES)].astype(F32)
+        logit_ref[pl.ds(block, 1), :] = jnp.sum(lanes.T, axis=0, keepdims=True)
+
+
 def split_low(axis_bit, terms_ref, keep_ref, send_ref, size):
     for pair in range(keep_ref.shape[0] // size):
         rows = pl.ds(pair * size, size)
@@ -227,40 +312,6 @@
         send_ref[rows, :] = terms_ref[aligned(2 * pair + 1 - axis_bit, size), :].astype(BF16)
 
 
-def score_map(base_ref, score_ref, weight_ref, out_ref, rows_ref, score_row_ref):
-    rows_ref[...] = (base_ref[...].astype(F32) * score_ref[...].astype(F32)).astype(BF16)
-    for part in tiles(out_ref.shape[1]):
-        out_ref[:, part] = lax.dot_general(
-            rows_ref[...], weight_ref[part, :], (((1,), (1,)), ((), ())), preferred_element_type=F32
-        )
-    score_row_ref[...] = jnp.broadcast_to(score_ref[...].astype(F32), score_row_ref.shape)
-    add_own_columns(out_ref, score_row_ref, lax.axis_index("cand"), lax.axis_index("mp"))
-
-
-def score_rows(map_ref, base_ref, bias_ref, score_ref, *refs):
-    *part_refs, rows_ref, logit_ref = refs
-    cand = lax.axis_index("cand")
-    if len(part_refs) == 1:
-        rows_ref[...] = part_refs[0][...]
-    else:
-        for bit, part_ref in enumerate(part_refs):
-            rows_ref[aligned(cand ^ bit, part_ref.shape[0]), :] = part_ref[...]
-    once = (lax.axis_index("mp") == 0).astype(F32)
-    blocks, size = logit_ref.shape
-    lanes = 128
-    for block in range(blocks):
-        rows = pl.ds(block * size, size)
-        total = jnp.zeros((size, lanes), F32)
-        for start in range(0, map_ref.shape[1], lanes):
-            cols = pl.ds(start, lanes)
-            total = total + rows_ref[rows, cols].astype(F32) * map_ref[rows, cols]
-        for start in range(0, base_ref.shape[1], lanes):
-            cols = pl.ds(start, lanes)
-            weight = bias_ref[:, cols] * score_ref[:, cols].astype(F32) * once
-            total = total + base_ref[rows, cols].astype(F32) * weight
-        logit_ref[pl.ds(block, 1), :] = jnp.sum(total.T, axis=0, keepdims=True)
-
-
 def layer_three(row_block, base_ref, weight_ref, rows_ref, keep_ref, send_ref, terms_ref):
     multiply(rows_ref, weight_ref, terms_ref, base_ref)
     model = lax.axis_index("mp")
@@ -273,17 +324,20 @@
     split_low((lax.axis_index("mp") // bit) % 2, terms_ref, kept_ref, send_ref, row_block)
 
 
-def finish(keep_ref, other_ref, base_ref, bias_ref, *refs):
-    *part_refs, out_ref, logit_ref, sum_ref = refs
+def finish(keep_ref, other_ref, base_ref, bias_ref, total_ref, part_ref, out_ref, logit_ref, sum_ref):
     model = lax.axis_index("mp")
     base = base_ref[aligned(model, out_ref.shape[0]), :].astype(F32)
     cross = keep_ref[...] + other_ref[...].astype(F32) + base * bias_ref[...]
     out_ref[...] = cross.astype(BF16)
-    total = part_refs[0][...]
-    for part_ref in part_refs[1:]:
-        total = total + part_ref[...]
-    sum_ref[...] = total
+    sum_ref[...] = total_ref[...] + part_ref[...]
     logit_ref[...] = sum_ref[pl.ds(model, 1), :]
+
+
+def finish_scored(keep_ref, other_ref, base_ref, bias_ref, score_ref, out_ref, logit_ref):
+    base = base_ref[aligned(lax.axis_index("mp"), out_ref.shape[0]), :].astype(F32)
+    cross = keep_ref[...] + other_ref[...].astype(F32) + base * bias_ref[...]
+    out_ref[...] = cross.astype(BF16)
+    logit_ref[...] = jnp.sum(cross * score_ref[...].astype(F32), axis=1, keepdims=True)
 
 
 def body(
@@ -311,7 +365,8 @@
     row_block = row_total // model_count
     half_rows = row_total // 2
     flops = 2 * row_total * col_block * feat_block
-    direct = cand_count <= DIRECT
+    direct = cand_count <= DIRECT and cand_count == model_count
+    score, bias = score_weight.reshape(1, -1), third_bias.reshape(1, -1)
 
     if local > 1:
         user_feats = jnp.take(user_feats, user_slot % local, axis=0)
@@ -377,6 +432,22 @@
     user_other = swap(user_sum, "mp", last_bit)
 
     if direct:
+        outs = [
+            ((local_rows, feat_block + LANES), BF16 if bit else F32) for bit in range(cand_count)
+        ]
+        maps = call(
+            functools.partial(score_map, half_width, user_count),
+            outs,
+            [base_cand, score, bias, third_weight],
+            scratch=[
+                pltpu.VMEM((row_total, col_block), BF16),
+                pltpu.VMEM((row_total, feat_block), F32),
+                pltpu.VMEM((row_total, col_block), F32),
+            ],
+            flops=flops,
+            limit=12 * MIB,
+        )
+        maps = [maps[0]] + [swap(maps[bit], "cand", bit) for bit in range(1, cand_count)]
         outs = [((local_rows, feat_block), BF16 if bit else F32) for bit in range(cand_count)]
     else:
         outs = [((row_total, feat_block), BF16)]
@@ -399,32 +470,21 @@
         parts = [parts[0]] + [swap(parts[bit], "cand", bit) for bit in range(1, cand_count)]
     else:
         parts = [lax.psum_scatter(parts[0], "cand", scatter_dimension=0, tiled=True)]
-    score = score_weight.reshape(1, -1)
-    (mapped,) = call(
-        score_map,
-        [((row_total, feat_block), F32)],
-        [base_cand, score, third_weight],
-        scratch=[pltpu.VMEM((row_total, col_block), BF16), pltpu.VMEM((row_total, col_block), F32)],
-        flops=flops,
-        limit=12 * MIB,
-    )
-    (block,) = call(
-        cross_rows,
-        [((local_rows, feat_block), BF16)],
-        [base_model, second_bias.reshape(1, -1), *parts],
-    )
+    bias_two = second_bias.reshape(1, -1)
     if direct:
+        (block,) = call(
+            functools.partial(cross_scored, cand_count),
+            [((local_rows, feat_block + 2 * LANES), BF16)],
+            [base_model, bias_two, *parts, *maps],
+        )
         parts = [block] + [swap(block, "cand", bit) for bit in range(1, cand_count)]
+        logit_out = [((cand_count, local_rows), F32)]
+        cross_two, logits = call(assemble, [((row_total, feat_block), BF16)] + logit_out, parts)
     else:
-        parts = [lax.all_gather(block, "cand", axis=0, tiled=True)]
-
-    bias = third_bias.reshape(1, -1)
-    logit_out = [((model_count, row_block), F32)]
-    cross_two, logits = call(
-        score_rows,
-        [((row_total, feat_block), BF16)] + logit_out,
-        [mapped, base_cand, bias, score, *parts],
-    )
+        (block,) = call(
+            cross_rows, [((local_rows, feat_block), BF16)], [base_model, bias_two, *parts]
+        )
+        cross_two = lax.all_gather(block, "cand", axis=0, tiled=True)
     rows = row_total // 2
     keep, send = call(
         functools.partial(layer_three, row_block),
@@ -446,21 +506,20 @@
         )
         other = swap(send, "mp", bit)
 
-    for bit in bits_of(model_count):
-        (logits,) = call(add_to, logit_out, [logits, swap(logits, "mp", bit)])
+    rows = [keep, other, base_cand, bias]
+    crossed_out = ((row_block, col_block), BF16)
     if direct:
-        parts = [logits]
-        parts += [swap(logits, "cand", bit) for bit in range(1, cand_count)]
+        for bit in bits:
+            (logits,) = call(add_to, logit_out, [logits, swap(logits, "mp", bit)])
+        crossed, logits = call(
+            finish,
+            [crossed_out, ((1, row_block), F32)],
+            [*rows, logits, swap(logits, "mp", last_bit)],
+            scratch=[pltpu.VMEM((cand_count, local_rows), F32)],
+        )
     else:
-        for bit in bits_of(cand_count):
-            (logits,) = call(add_to, logit_out, [logits, swap(logits, "cand", bit)])
-        parts = [logits]
-    crossed, logits = call(
-        finish,
-        [((row_block, col_block), BF16), ((1, row_block), F32)],
-        [keep, other, base_cand, bias, *parts],
-        scratch=[pltpu.VMEM((model_count, row_block), F32)],
-    )
+        crossed, logits = call(finish_scored, [crossed_out, ((row_block, 1), F32)], [*rows, score])
+        logits = lax.psum(logits, "cand")
     return (crossed, logits.reshape(-1))
 
 

time: 64.6 us -> 64.3 us (level)
    pallas_call x17 -> x16, Pallas kernels: 9.07 us -> 8.79 us  [call(): pl.pallas_call(kernel, out_shape=[jax.ShapeDtypeStruct(s, d) for s, d in...]
  transfers between devices with their start and end apart: 21 -> 21, of which waited for: 13 -> 13; matrix products, arithmetic and copies ran while one was open for 0% -> 0% of each run, Pallas kernels for 6% -> 9%
where the time goes in v1:
time: 64.3 us; the launch traced here: 64.1 us
  starting transfers between devices  25.6 us (40%)
  waiting for transfers between devices  24.7 us (38%)
  Pallas kernels  8.79 us (14%)
  local copies, waits for them, and re-layouts  3.53 us (5%)
  between operations  1.54 us (2%)
    ppermute x21, starting transfers between devices, swap(): return lax.ppermute(value, axis, [(i, i ^ bit) for i in range(count)])  25.6 us
    ppermute x21, waiting for transfers between devices, swap(): return lax.ppermute(value, axis, [(i, i ^ bit) for i in range(count)])  24.7 us
    pallas_call x16, Pallas kernels, call(): pl.pallas_call(kernel, out_shape=[jax.ShapeDtypeStruct(s, d) for s, d in...  8.79 us
    unnamed x24, local copies, waits for them, and re-layouts  3.52 us
  transfers between devices with their start and end apart: 21, of which 13 were waited for; matrix products, arithmetic and copies ran while one was open for 0% of the time, Pallas kernels for 9%

profile of v1, /device:TPU:0, one launch (start us, length us, event | category | flops | bytes accessed | tf_op | source)
XLA Modules:
  0.0 64.1 jit_solution(255434822503238834)
XLA Ops:
  0.7 0.6 copy-done.6
  1.3 1.0 %copy-done.1 = bf16[256,4096]{1,0:T(8,128)(2,1)S(1)} copy-done((bf16[256,4096]{1,0:T(8,128)(2,1)S(1)}, bf16[256,4096]{1,0:T(8,128)(2,1)}, u32[]{:S(2)}) %copy-start.1) | copy-done | bytes 2097176
  2.2 0.5 shard_map.124
  2.8 1.9 %copy-done = bf16[2048,2048]{1,0:T(8,128)(2,1)S(1)} copy-done((bf16[2048,2048]{1,0:T(8,128)(2,1)S(1)}, bf16[2048,2048]{1,0:T(8,128)(2,1)}, u32[]{:S(2)}) %copy-start) | copy-done | bytes 8388632
  4.7 0.6 collective-permute-start.3
  5.3 1.0 %collective-permute-done.3.other_ref = bf16[32,2048]{1,0:T(8,128)(2,1)S(1)} collective-permute-done((bf16[32,2048]{1,0:T(8,128)(2,1)S(1)}, bf16[32,2048]{1,0:T(8,128)(2,1)S(1)}, u32[]{:S(2)}, u32[]{:S(2)}) %collective-permute-start.3) | collective-permute-done | bytes 131104 | tf_op jit(solution)/shard_map/ppermute | solution.py:30
  6.3 4.5 %collective-permute-start.4 = (bf16[32,2048]{1,0:T(8,128)(2,1)S(1)}, bf16[32,2048]{1,0:T(8,128)(2,1)S(1)}, u32[]{:S(2)}, u32[]{:S(2)}) collective-permute-start(bf16[32,2048]{1,0:T(8,128)(2,1)S(1)} %get-tuple-element.36), channel_id=1, source_target_pairs={{0,2},{1,3},{2,0},{3,1},{4,6},{5,7},{6,4},{7,5},{8,10},{9,11},{10,... | collective-permute-start | bytes 393224 | tf_op jit(solution)/shard_map/ppermute | solution.py:30
  10.8 3.8 %collective-permute-done.4.other_ref = bf16[32,2048]{1,0:T(8,128)(2,1)S(1)} collective-permute-done((bf16[32,2048]{1,0:T(8,128)(2,1)S(1)}, bf16[32,2048]{1,0:T(8,128)(2,1)S(1)}, u32[]{:S(2)}, u32[]{:S(2)}) %collective-permute-start.4) | collective-permute-done | bytes 131104 | tf_op jit(solution)/shard_map/ppermute | solution.py:30
  14.7 0.1 collective-permute-start.5
  14.7 1.6 %collective-permute-start = (bf16[1,4096]{1,0:T(2,128)(2,1)S(1)}, bf16[1,4096]{1,0:T(2,128)(2,1)S(1)}, u32[]{:S(2)}, u32[]{:S(2)}) collective-permute-start(bf16[1,4096]{1,0:T(2,128)(2,1)S(1)} %copy-done.3), channel_id=1, source_target_pairs={{0,4},{4,0},{8,12},{12,8},{1,5},{5,1},{9,13},{13,9},{2,6},{6,2},{1... | collective-permute-start | bytes 24584 | tf_op jit(solution)/shard_map/ppermute | solution.py:30
  16.4 2.6 %collective-permute-start.1 = (bf16[1,4096]{1,0:T(2,128)(2,1)S(1)}, bf16[1,4096]{1,0:T(2,128)(2,1)S(1)}, u32[]{:S(2)}, u32[]{:S(2)}) collective-permute-start(bf16[1,4096]{1,0:T(2,128)(2,1)S(1)} %copy-done.3), channel_id=1, source_target_pairs={{0,8},{4,12},{8,0},{12,4},{1,9},{5,13},{9,1},{13,5},{2,10},{6,14},... | collective-permute-start | bytes 24584 | tf_op jit(solution)/shard_map/ppermute | solution.py:30
  19.0 0.2 collective-permute-start.2
  19.9 0.0 collective-permute-done.refs_1_
  19.9 1.2 %collective-permute-done.1.refs_2_ = bf16[1,4096]{1,0:T(2,128)(2,1)S(1)} collective-permute-done((bf16[1,4096]{1,0:T(2,128)(2,1)S(1)}, bf16[1,4096]{1,0:T(2,128)(2,1)S(1)}, u32[]{:S(2)}, u32[]{:S(2)}) %collective-permute-start.1) | collective-permute-done | bytes 8224 | tf_op jit(solution)/shard_map/ppermute | solution.py:30
  21.1 3.4 %collective-permute-done.2.refs_3_ = bf16[1,4096]{1,0:T(2,128)(2,1)S(1)} collective-permute-done((bf16[1,4096]{1,0:T(2,128)(2,1)S(1)}, bf16[1,4096]{1,0:T(2,128)(2,1)S(1)}, u32[]{:S(2)}, u32[]{:S(2)}) %collective-permute-start.2) | collective-permute-done | bytes 8224 | tf_op jit(solution)/shard_map/ppermute | solution.py:30
  24.5 1.3 %shard_map.125 = (bf16[64,2048]{1,0:T(8,128)(2,1)S(1)}, bf16[64,2048]{1,0:T(8,128)(2,1)S(1)}, f32[1,2048]{1,0:T(1,128)S(1)}) custom-call(s32[1,128]{1,0:T(1,128)S(1)} %shard_map.122.want_ref, bf16[2048,2048]{1,0:T(8,128)(2,1)S(1)} %copy-done, bf16[64,2048]{1,0:T(8,128)(2,1)S(1)} %get-tuple-element.29.pool_model_ref.rows_ref, ...), custom_call_target="tpu_custom_call" | custom-call | flops 536870912 | bytes 1090048 | tf_op jit(solution)/shard_map/pallas_call | solution.py:36
  25.9 0.0 copy-start.4
  25.9 2.5 %shard_map.131 = (f32[16,2176]{1,0:T(8,128)S(1)}, bf16[16,2176]{1,0:T(8,128)(2,1)S(1)}, bf16[16,2176]{1,0:T(8,128)(2,1)S(1)}, bf16[16,2176]{1,0:T(8,128)(2,1)S(1)}) custom-call(bf16[64,2048]{1,0:T(8,128)(2,1)S(1)} %get-tuple-element.31.cand_ref.base_ref, bf16[1,2048]{1,0:T(2,128)(2,1)S(1)} %reshape.21.score_ref, f32[1,2048]{1,0:T(1,128)S(1)} %bitcast.8, ...), custom_call_target="tpu_custom_call" | custom-call | flops 536870912 | bytes 622592 | tf_op jit(solution)/shard_map/pallas_call | solution.py:36
  28.4 0.1 collective-permute-start.11
  28.5 0.1 collective-permute-start.6
  28.6 1.2 %collective-permute-done.6.refs_1_ = f32[1,2048]{1,0:T(1,128)S(1)} collective-permute-done((f32[1,2048]{1,0:T(1,128)S(1)}, f32[1,2048]{1,0:T(1,128)S(1)}, u32[]{:S(2)}, u32[]{:S(2)}) %collective-permute-start.6) | collective-permute-done | bytes 8224 | tf_op jit(solution)/shard_map/ppermute | solution.py:30
  29.7 0.5 collective-permute-start.7
  30.2 1.0 %collective-permute-start.12 = (bf16[16,2176]{1,0:T(8,128)(2,1)S(1)}, bf16[16,2176]{1,0:T(8,128)(2,1)S(1)}, u32[]{:S(2)}, u32[]{:S(2)}) collective-permute-start(bf16[16,2176]{1,0:T(8,128)(2,1)S(1)} %get-tuple-element.46), channel_id=1, source_target_pairs={{0,8},{4,12},{8,0},{12,4},{1,9},{5,13},{9,1},{13,5},{2,10},{6,14},... | collective-permute-start | bytes 208904 | tf_op jit(solution)/shard_map/ppermute | solution.py:30
  31.2 3.3 %collective-permute-start.13 = (bf16[16,2176]{1,0:T(8,128)(2,1)S(1)}, bf16[16,2176]{1,0:T(8,128)(2,1)S(1)}, u32[]{:S(2)}, u32[]{:S(2)}) collective-permute-start(bf16[16,2176]{1,0:T(8,128)(2,1)S(1)} %get-tuple-element.47), channel_id=1, source_target_pairs={{0,12},{4,8},{8,4},{12,0},{1,13},{5,9},{9,5},{13,1},{2,14},{6,10},... | collective-permute-start | bytes 208904 | tf_op jit(solution)/shard_map/ppermute | solution.py:30
  34.5 0.0 collective-permute-done.7.user_other_ref
  34.5 0.0 collective-permute-done.5.other_ref
  34.5 1.7 %shard_map.130 = (f32[16,2048]{1,0:T(8,128)S(1)}, bf16[16,2048]{1,0:T(8,128)(2,1)S(1)}, bf16[16,2048]{1,0:T(8,128)(2,1)S(1)}, bf16[16,2048]{1,0:T(8,128)(2,1)S(1)}) custom-call(f32[32,2048]{1,0:T(8,128)S(1)} %get-tuple-element.37.mine_ref, bf16[32,2048]{1,0:T(8,128)(2,1)S(1)} %collective-permute-done.5.other_ref, f32[1,2048]{1,0:T(1,128)S(1)} %shard_map.129.user_ref, ...), custom_call_target="tpu_custom_call" | custom-call | flops 536870912 | bytes 1269760 | tf_op jit(solution)/shard_map/pallas_call | solution.py:36
  36.2 0.8 %collective-permute-start.8 = (bf16[16,2048]{1,0:T(8,128)(2,1)S(1)}, bf16[16,2048]{1,0:T(8,128)(2,1)S(1)}, u32[]{:S(2)}, u32[]{:S(2)}) collective-permute-start(bf16[16,2048]{1,0:T(8,128)(2,1)S(1)} %get-tuple-element.41), channel_id=1, source_target_pairs={{0,4},{4,0},{8,12},{12,8},{1,5},{5,1},{9,13},{13,9},{2,6},{6,2},{1... | collective-permute-start | bytes 196616 | tf_op jit(solution)/shard_map/ppermute | solution.py:30
  37.1 0.2 collective-permute-start.9
  37.3 3.4 %collective-permute-start.10 = (bf16[16,2048]{1,0:T(8,128)(2,1)S(1)}, bf16[16,2048]{1,0:T(8,128)(2,1)S(1)}, u32[]{:S(2)}, u32[]{:S(2)}) collective-permute-start(bf16[16,2048]{1,0:T(8,128)(2,1)S(1)} %get-tuple-element.43), channel_id=1, source_target_pairs={{0,12},{4,8},{8,4},{12,0},{1,13},{5,9},{9,5},{13,1},{2,14},{6,10},... | collective-permute-start | bytes 196616 | tf_op jit(solution)/shard_map/ppermute | solution.py:30
  40.7 0.2 collective-permute-done.8.refs_1_
  40.9 3.5 %collective-permute-done.9.refs_2_ = bf16[16,2048]{1,0:T(8,128)(2,1)S(1)} collective-permute-done((bf16[16,2048]{1,0:T(8,128)(2,1)S(1)}, bf16[16,2048]{1,0:T(8,128)(2,1)S(1)}, u32[]{:S(2)}, u32[]{:S(2)}) %collective-permute-start.9) | collective-permute-done | bytes 65568 | tf_op jit(solution)/shard_map/ppermute | solution.py:30
  44.5 0.1 shard_map.132.refs_0_
  44.6 1.3 %collective-permute-start.14 = (bf16[16,2304]{1,0:T(8,128)(2,1)S(1)}, bf16[16,2304]{1,0:T(8,128)(2,1)S(1)}, u32[]{:S(2)}, u32[]{:S(2)}) collective-permute-start(bf16[16,2304]{1,0:T(8,128)(2,1)S(1)} %shard_map.132.refs_0_), channel_id=1, source_target_pairs={{0,4},{4,0},{8,12},{12,8},{1,5},{5,1},{9,13},{13,9},{2,6},{6,2},{1... | collective-permute-start | bytes 221192 | tf_op jit(solution)/shard_map/ppermute | solution.py:30
  45.9 1.7 %collective-permute-start.15 = (bf16[16,2304]{1,0:T(8,128)(2,1)S(1)}, bf16[16,2304]{1,0:T(8,128)(2,1)S(1)}, u32[]{:S(2)}, u32[]{:S(2)}) collective-permute-start(bf16[16,2304]{1,0:T(8,128)(2,1)S(1)} %shard_map.132.refs_0_), channel_id=1, source_target_pairs={{0,8},{4,12},{8,0},{12,4},{1,9},{5,13},{9,1},{13,5},{2,10},{6,14},... | collective-permute-start | bytes 221192 | tf_op jit(solution)/shard_map/ppermute | solution.py:30
  47.6 1.5 %collective-permute-start.16 = (bf16[16,2304]{1,0:T(8,128)(2,1)S(1)}, bf16[16,2304]{1,0:T(8,128)(2,1)S(1)}, u32[]{:S(2)}, u32[]{:S(2)}) collective-permute-start(bf16[16,2304]{1,0:T(8,128)(2,1)S(1)} %shard_map.132.refs_0_), channel_id=1, source_target_pairs={{0,12},{4,8},{8,4},{12,0},{1,13},{5,9},{9,5},{13,1},{2,14},{6,10},... | collective-permute-start | bytes 221192 | tf_op jit(solution)/shard_map/ppermute | solution.py:30
  49.0 1.6 %collective-permute-done.14.refs_1_ = bf16[16,2304]{1,0:T(8,128)(2,1)S(1)} collective-permute-done((bf16[16,2304]{1,0:T(8,128)(2,1)S(1)}, bf16[16,2304]{1,0:T(8,128)(2,1)S(1)}, u32[]{:S(2)}, u32[]{:S(2)}) %collective-permute-start.14) | collective-permute-done | bytes 73760 | tf_op jit(solution)/shard_map/ppermute | solution.py:30
  50.6 2.1 %collective-permute-done.15.refs_2_ = bf16[16,2304]{1,0:T(8,128)(2,1)S(1)} collective-permute-done((bf16[16,2304]{1,0:T(8,128)(2,1)S(1)}, bf16[16,2304]{1,0:T(8,128)(2,1)S(1)}, u32[]{:S(2)}, u32[]{:S(2)}) %collective-permute-start.15) | collective-permute-done | bytes 73760 | tf_op jit(solution)/shard_map/ppermute | solution.py:30
  52.7 1.1 %collective-permute-done.16.refs_3_ = bf16[16,2304]{1,0:T(8,128)(2,1)S(1)} collective-permute-done((bf16[16,2304]{1,0:T(8,128)(2,1)S(1)}, bf16[16,2304]{1,0:T(8,128)(2,1)S(1)}, u32[]{:S(2)}, u32[]{:S(2)}) %collective-permute-start.16) | collective-permute-done | bytes 73760 | tf_op jit(solution)/shard_map/ppermute | solution.py:30
  53.8 0.1 shard_map.133
  54.0 1.7 %shard_map.134 = (f32[32,2048]{1,0:T(8,128)S(1)}, bf16[32,2048]{1,0:T(8,128)(2,1)S(1)}) custom-call(bf16[64,2048]{1,0:T(8,128)(2,1)S(1)} %get-tuple-element.31.cand_ref.base_ref, bf16[2048,2048]{1,0:T(8,128)(2,1)S(1)} %bitcast.5, bf16[64,2048]{1,0:T(8,128)(2,1)S(1)} %get-tuple-element.48.rows_ref), custom_call_target="tpu_custom_call" | custom-call | flops 536870912 | bytes 917504 | tf_op jit(solution)/shard_map/pallas_call | solution.py:36
  55.6 0.1 collective-permute-start.17
  55.7 1.3 %collective-permute-done.17.other_ref = bf16[32,2048]{1,0:T(8,128)(2,1)S(1)} collective-permute-done((bf16[32,2048]{1,0:T(8,128)(2,1)S(1)}, bf16[32,2048]{1,0:T(8,128)(2,1)S(1)}, u32[]{:S(2)}, u32[]{:S(2)}) %collective-permute-start.17) | collective-permute-done | bytes 131104 | tf_op jit(solution)/shard_map/ppermute | solution.py:30
  57.1 1.6 %collective-permute-start.18 = (bf16[16,2048]{1,0:T(8,128)(2,1)S(1)}, bf16[16,2048]{1,0:T(8,128)(2,1)S(1)}, u32[]{:S(2)}, u32[]{:S(2)}) collective-permute-start(bf16[16,2048]{1,0:T(8,128)(2,1)S(1)} %get-tuple-element.52), channel_id=1, source_target_pairs={{0,2},{1,3},{2,0},{3,1},{4,6},{5,7},{6,4},{7,5},{8,10},{9,11},{10,... | collective-permute-start | bytes 196616 | tf_op jit(solution)/shard_map/ppermute | solution.py:30
  58.7 1.2 %collective-permute-done.19.refs_1_ = f32[4,16]{1,0:T(4,128)S(1)} collective-permute-done((f32[4,16]{1,0:T(4,128)S(1)}, f32[4,16]{1,0:T(4,128)S(1)}, u32[]{:S(2)}, u32[]{:S(2)}) %collective-permute-start.19) | collective-permute-done | bytes 288 | tf_op jit(solution)/shard_map/ppermute | solution.py:30
  59.9 0.5 collective-permute-start.20
  60.4 3.1 %collective-permute-done.20.part_ref = f32[4,16]{1,0:T(4,128)S(1)} collective-permute-done((f32[4,16]{1,0:T(4,128)S(1)}, f32[4,16]{1,0:T(4,128)S(1)}, u32[]{:S(2)}, u32[]{:S(2)}) %collective-permute-start.20) | collective-permute-done | bytes 288 | tf_op jit(solution)/shard_map/ppermute | solution.py:30
  63.5 0.7 %shard_map.137 = (bf16[16,2048]{1,0:T(8,128)(2,1)}, f32[1,16]{1,0:T(1,128)}) custom-call(f32[16,2048]{1,0:T(8,128)S(1)} %get-tuple-element.51.keep_ref, bf16[16,2048]{1,0:T(8,128)(2,1)S(1)} %collective-permute-done.18.other_ref, bf16[64,2048]{1,0:T(8,128)(2,1)S(1)} %get-tuple-element.31.cand_ref.base_ref, f32[1,2048]{1,0:T(1,128)S(1)} %bitcast.9, ...), custom_call_target="tpu_custom_call" | custom-call | bytes 533056 | tf_op jit(solution)/shard_map/pallas_call | solution.py:36
  (37 shorter events, 0.2 us)
Async XLA Ops:
  0.6 0.7 %copy-start.6 = (s32[1,64]{1,0:T(1,128)S(1)}, s32[1,64]{1,0:T(1,128)}, u32[]{:S(2)}) copy-start(s32[1,64]{1,0:T(1,128)} %ids_ref.1) | copy-start | bytes 772
  0.6 1.6 %copy-start.1 = (bf16[256,4096]{1,0:T(8,128)(2,1)S(1)}, bf16[256,4096]{1,0:T(8,128)(2,1)}, u32[]{:S(2)}) copy-start(bf16[256,4096]{1,0:T(8,128)(2,1)} %pool_ref.1) | copy-start | bytes 6291460
  0.7 4.0 %copy-start = (bf16[2048,2048]{1,0:T(8,128)(2,1)S(1)}, bf16[2048,2048]{1,0:T(8,128)(2,1)}, u32[]{:S(2)}) copy-start(bf16[2048,2048]{1,0:T(8,128)(2,1)} %weight_ref.6) | copy-start | bytes 25165828
  2.2 12.5 %copy-start.3 = (bf16[1,4096]{1,0:T(2,128)(2,1)S(1)}, bf16[1,4096]{1,0:T(2,128)(2,1)}, u32[]{:S(2)}) copy-start(bf16[1,4096]{1,0:T(2,128)(2,1)} %refs_0_.1) | copy-start | bytes 24580
  2.2 17.6 %copy-start.7 = (bf16[2048]{0:T(1024)(128)(2,1)S(1)}, bf16[2048]{0:T(1024)(128)(2,1)}, u32[]{:S(2)}) copy-start(bf16[2048]{0:T(1024)(128)(2,1)} %param.21) | copy-start | bytes 12292
  4.7 21.2 %slice-start = ((s8[8388608]{0:T(1024)(128)(4,1)}), s8[4194304]{0:T(1024)(128)(4,1)S(1)}, s32[]{:S(2)}) async-start(s8[8388608]{0:T(1024)(128)(4,1)} %bitcast.4), calls=%async_computation | async-start | bytes 8388608
  4.7 21.2 %copy-start.2 = (f32[2048]{0:T(1024)S(1)}, f32[2048]{0:T(1024)}, u32[]{:S(2)}) copy-start(f32[2048]{0:T(1024)} %param.20) | copy-start | bytes 24580
  4.7 29.8 %slice-start.2 = ((s8[8388608]{0:T(1024)(128)(4,1)}), s8[4194304]{0:T(1024)(128)(4,1)S(1)}, s32[]{:S(2)}) async-start(s8[8388608]{0:T(1024)(128)(4,1)} %bitcast.6), calls=%async_computation.2 | async-start | bytes 8388608
  4.7 1.5 %collective-permute-start.3 = (bf16[32,2048]{1,0:T(8,128)(2,1)S(1)}, bf16[32,2048]{1,0:T(8,128)(2,1)S(1)}, u32[]{:S(2)}, u32[]{:S(2)}) collective-permute-start(bf16[32,2048]{1,0:T(8,128)(2,1)S(1)} %get-tuple-element.34), channel_id=1, source_target_pairs={{0,1},{1,0},{2,3},{3,2},{4,5},{5,4},{6,7},{7,6},{8,9},{9,8},{10,11... | collective-permute-start | bytes 393224 | tf_op jit(solution)/shard_map/ppermute | solution.py:30
  6.3 8.3 %collective-permute-start.4 = (bf16[32,2048]{1,0:T(8,128)(2,1)S(1)}, bf16[32,2048]{1,0:T(8,128)(2,1)S(1)}, u32[]{:S(2)}, u32[]{:S(2)}) collective-permute-start(bf16[32,2048]{1,0:T(8,128)(2,1)S(1)} %get-tuple-element.36), channel_id=1, source_target_pairs={{0,2},{1,3},{2,0},{3,1},{4,6},{5,7},{6,4},{7,5},{8,10},{9,11},{10,... | collective-permute-start | bytes 393224 | tf_op jit(solution)/shard_map/ppermute | solution.py:30
  14.6 11.3 %slice-start.1 = ((s8[8388608]{0:T(1024)(128)(4,1)}), s8[4194304]{0:T(1024)(128)(4,1)S(1)}, s32[]{:S(2)}) async-start(s8[8388608]{0:T(1024)(128)(4,1)} %bitcast.4), calls=%async_computation.1 | async-start | bytes 8388608
  14.7 19.9 %collective-permute-start.5 = (bf16[32,2048]{1,0:T(8,128)(2,1)S(1)}, bf16[32,2048]{1,0:T(8,128)(2,1)S(1)}, u32[]{:S(2)}, u32[]{:S(2)}) collective-permute-start(bf16[32,2048]{1,0:T(8,128)(2,1)S(1)} %get-tuple-element.38), channel_id=1, source_target_pairs={{0,1},{1,0},{2,3},{3,2},{4,5},{5,4},{6,7},{7,6},{8,9},{9,8},{10,11... | collective-permute-start | bytes 393224 | tf_op jit(solution)/shard_map/ppermute | solution.py:30
  14.7 5.2 %collective-permute-start = (bf16[1,4096]{1,0:T(2,128)(2,1)S(1)}, bf16[1,4096]{1,0:T(2,128)(2,1)S(1)}, u32[]{:S(2)}, u32[]{:S(2)}) collective-permute-start(bf16[1,4096]{1,0:T(2,128)(2,1)S(1)} %copy-done.3), channel_id=1, source_target_pairs={{0,4},{4,0},{8,12},{12,8},{1,5},{5,1},{9,13},{13,9},{2,6},{6,2},{1... | collective-permute-start | bytes 24584 | tf_op jit(solution)/shard_map/ppermute | solution.py:30
  16.4 4.7 %collective-permute-start.1 = (bf16[1,4096]{1,0:T(2,128)(2,1)S(1)}, bf16[1,4096]{1,0:T(2,128)(2,1)S(1)}, u32[]{:S(2)}, u32[]{:S(2)}) collective-permute-start(bf16[1,4096]{1,0:T(2,128)(2,1)S(1)} %copy-done.3), channel_id=1, source_target_pairs={{0,8},{4,12},{8,0},{12,4},{1,9},{5,13},{9,1},{13,5},{2,10},{6,14},... | collective-permute-start | bytes 24584 | tf_op jit(solution)/shard_map/ppermute | solution.py:30
  19.0 5.5 %collective-permute-start.2 = (bf16[1,4096]{1,0:T(2,128)(2,1)S(1)}, bf16[1,4096]{1,0:T(2,128)(2,1)S(1)}, u32[]{:S(2)}, u32[]{:S(2)}) collective-permute-start(bf16[1,4096]{1,0:T(2,128)(2,1)S(1)} %copy-done.3), channel_id=1, source_target_pairs={{0,12},{4,8},{8,4},{12,0},{1,13},{5,9},{9,5},{13,1},{2,14},{6,10},... | collective-permute-start | bytes 24584 | tf_op jit(solution)/shard_map/ppermute | solution.py:30
  24.5 10.0 %slice-start.3 = ((s8[8388608]{0:T(1024)(128)(4,1)}), s8[4194304]{0:T(1024)(128)(4,1)S(1)}, s32[]{:S(2)}) async-start(s8[8388608]{0:T(1024)(128)(4,1)} %bitcast.6), calls=%async_computation.3 | async-start | bytes 8388608
  24.5 10.0 %copy-start.5 = (f32[2048]{0:T(1024)S(1)}, f32[2048]{0:T(1024)}, u32[]{:S(2)}) copy-start(f32[2048]{0:T(1024)} %param.16) | copy-start | bytes 24580
  25.9 18.6 %copy-start.4 = (f32[2048]{0:T(1024)S(1)}, f32[2048]{0:T(1024)}, u32[]{:S(2)}) copy-start(f32[2048]{0:T(1024)} %param.18) | copy-start | bytes 24580
  28.4 8.9 %collective-permute-start.11 = (bf16[16,2176]{1,0:T(8,128)(2,1)S(1)}, bf16[16,2176]{1,0:T(8,128)(2,1)S(1)}, u32[]{:S(2)}, u32[]{:S(2)}) collective-permute-start(bf16[16,2176]{1,0:T(8,128)(2,1)S(1)} %get-tuple-element.45), channel_id=1, source_target_pairs={{0,4},{4,0},{8,12},{12,8},{1,5},{5,1},{9,13},{13,9},{2,6},{6,2},{1... | collective-permute-start | bytes 208904 | tf_op jit(solution)/shard_map/ppermute | solution.py:30
  28.5 1.2 %collective-permute-start.6 = (f32[1,2048]{1,0:T(1,128)S(1)}, f32[1,2048]{1,0:T(1,128)S(1)}, u32[]{:S(2)}, u32[]{:S(2)}) collective-permute-start(f32[1,2048]{1,0:T(1,128)S(1)} %get-tuple-element.39.refs_0_), channel_id=1, source_target_pairs={{0,1},{1,0},{2,3},{3,2},{4,5},{5,4},{6,7},{7,6},{8,9},{9,8},{10,11... | collective-permute-start | bytes 24584 | tf_op jit(solution)/shard_map/ppermute | solution.py:30
  29.7 4.8 %collective-permute-start.7 = (f32[1,2048]{1,0:T(1,128)S(1)}, f32[1,2048]{1,0:T(1,128)S(1)}, u32[]{:S(2)}, u32[]{:S(2)}) collective-permute-start(f32[1,2048]{1,0:T(1,128)S(1)} %shard_map.129.user_ref), channel_id=1, source_target_pairs={{0,2},{1,3},{2,0},{3,1},{4,6},{5,7},{6,4},{7,5},{8,10},{9,11},{10,... | collective-permute-start | bytes 24584 | tf_op jit(solution)/shard_map/ppermute | solution.py:30
  30.2 10.5 %collective-permute-start.12 = (bf16[16,2176]{1,0:T(8,128)(2,1)S(1)}, bf16[16,2176]{1,0:T(8,128)(2,1)S(1)}, u32[]{:S(2)}, u32[]{:S(2)}) collective-permute-start(bf16[16,2176]{1,0:T(8,128)(2,1)S(1)} %get-tuple-element.46), channel_id=1, source_target_pairs={{0,8},{4,12},{8,0},{12,4},{1,9},{5,13},{9,1},{13,5},{2,10},{6,14},... | collective-permute-start | bytes 208904 | tf_op jit(solution)/shard_map/ppermute | solution.py:30
  31.2 9.5 %collective-permute-start.13 = (bf16[16,2176]{1,0:T(8,128)(2,1)S(1)}, bf16[16,2176]{1,0:T(8,128)(2,1)S(1)}, u32[]{:S(2)}, u32[]{:S(2)}) collective-permute-start(bf16[16,2176]{1,0:T(8,128)(2,1)S(1)} %get-tuple-element.47), channel_id=1, source_target_pairs={{0,12},{4,8},{8,4},{12,0},{1,13},{5,9},{9,5},{13,1},{2,14},{6,10},... | collective-permute-start | bytes 208904 | tf_op jit(solution)/shard_map/ppermute | solution.py:30
  36.2 4.7 %collective-permute-start.8 = (bf16[16,2048]{1,0:T(8,128)(2,1)S(1)}, bf16[16,2048]{1,0:T(8,128)(2,1)S(1)}, u32[]{:S(2)}, u32[]{:S(2)}) collective-permute-start(bf16[16,2048]{1,0:T(8,128)(2,1)S(1)} %get-tuple-element.41), channel_id=1, source_target_pairs={{0,4},{4,0},{8,12},{12,8},{1,5},{5,1},{9,13},{13,9},{2,6},{6,2},{1... | collective-permute-start | bytes 196616 | tf_op jit(solution)/shard_map/ppermute | solution.py:30
  37.1 7.4 %collective-permute-start.9 = (bf16[16,2048]{1,0:T(8,128)(2,1)S(1)}, bf16[16,2048]{1,0:T(8,128)(2,1)S(1)}, u32[]{:S(2)}, u32[]{:S(2)}) collective-permute-start(bf16[16,2048]{1,0:T(8,128)(2,1)S(1)} %get-tuple-element.42), channel_id=1, source_target_pairs={{0,8},{4,12},{8,0},{12,4},{1,9},{5,13},{9,1},{13,5},{2,10},{6,14},... | collective-permute-start | bytes 196616 | tf_op jit(solution)/shard_map/ppermute | solution.py:30
  37.3 7.1 %collective-permute-start.10 = (bf16[16,2048]{1,0:T(8,128)(2,1)S(1)}, bf16[16,2048]{1,0:T(8,128)(2,1)S(1)}, u32[]{:S(2)}, u32[]{:S(2)}) collective-permute-start(bf16[16,2048]{1,0:T(8,128)(2,1)S(1)} %get-tuple-element.43), channel_id=1, source_target_pairs={{0,12},{4,8},{8,4},{12,0},{1,13},{5,9},{9,5},{13,1},{2,14},{6,10},... | collective-permute-start | bytes 196616 | tf_op jit(solution)/shard_map/ppermute | solution.py:30
  44.6 6.1 %collective-permute-start.14 = (bf16[16,2304]{1,0:T(8,128)(2,1)S(1)}, bf16[16,2304]{1,0:T(8,128)(2,1)S(1)}, u32[]{:S(2)}, u32[]{:S(2)}) collective-permute-start(bf16[16,2304]{1,0:T(8,128)(2,1)S(1)} %shard_map.132.refs_0_), channel_id=1, source_target_pairs={{0,4},{4,0},{8,12},{12,8},{1,5},{5,1},{9,13},{13,9},{2,6},{6,2},{1... | collective-permute-start | bytes 221192 | tf_op jit(solution)/shard_map/ppermute | solution.py:30
  45.9 6.8 %collective-permute-start.15 = (bf16[16,2304]{1,0:T(8,128)(2,1)S(1)}, bf16[16,2304]{1,0:T(8,128)(2,1)S(1)}, u32[]{:S(2)}, u32[]{:S(2)}) collective-permute-start(bf16[16,2304]{1,0:T(8,128)(2,1)S(1)} %shard_map.132.refs_0_), channel_id=1, source_target_pairs={{0,8},{4,12},{8,0},{12,4},{1,9},{5,13},{9,1},{13,5},{2,10},{6,14},... | collective-permute-start | bytes 221192 | tf_op jit(solution)/shard_map/ppermute | solution.py:30
  47.6 6.3 %collective-permute-start.16 = (bf16[16,2304]{1,0:T(8,128)(2,1)S(1)}, bf16[16,2304]{1,0:T(8,128)(2,1)S(1)}, u32[]{:S(2)}, u32[]{:S(2)}) collective-permute-start(bf16[16,2304]{1,0:T(8,128)(2,1)S(1)} %shard_map.132.refs_0_), channel_id=1, source_target_pairs={{0,12},{4,8},{8,4},{12,0},{1,13},{5,9},{9,5},{13,1},{2,14},{6,10},... | collective-permute-start | bytes 221192 | tf_op jit(solution)/shard_map/ppermute | solution.py:30
  55.6 1.4 %collective-permute-start.17 = (bf16[32,2048]{1,0:T(8,128)(2,1)S(1)}, bf16[32,2048]{1,0:T(8,128)(2,1)S(1)}, u32[]{:S(2)}, u32[]{:S(2)}) collective-permute-start(bf16[32,2048]{1,0:T(8,128)(2,1)S(1)} %get-tuple-element.50), channel_id=1, source_target_pairs={{0,1},{1,0},{2,3},{3,2},{4,5},{5,4},{6,7},{7,6},{8,9},{9,8},{10,11... | collective-permute-start | bytes 393224 | tf_op jit(solution)/shard_map/ppermute | solution.py:30
  57.1 6.3 %collective-permute-start.18 = (bf16[16,2048]{1,0:T(8,128)(2,1)S(1)}, bf16[16,2048]{1,0:T(8,128)(2,1)S(1)}, u32[]{:S(2)}, u32[]{:S(2)}) collective-permute-start(bf16[16,2048]{1,0:T(8,128)(2,1)S(1)} %get-tuple-element.52), channel_id=1, source_target_pairs={{0,2},{1,3},{2,0},{3,1},{4,6},{5,7},{6,4},{7,5},{8,10},{9,11},{10,... | collective-permute-start | bytes 196616 | tf_op jit(solution)/shard_map/ppermute | solution.py:30
  58.7 1.2 %collective-permute-start.19 = (f32[4,16]{1,0:T(4,128)S(1)}, f32[4,16]{1,0:T(4,128)S(1)}, u32[]{:S(2)}, u32[]{:S(2)}) collective-permute-start(f32[4,16]{1,0:T(4,128)S(1)} %get-tuple-element.53.refs_0_), channel_id=1, source_target_pairs={{0,1},{1,0},{2,3},{3,2},{4,5},{5,4},{6,7},{7,6},{8,9},{9,8},{10,11... | collective-permute-start | bytes 776 | tf_op jit(solution)/shard_map/ppermute | solution.py:30
  59.9 3.6 %collective-permute-start.20 = (f32[4,16]{1,0:T(4,128)S(1)}, f32[4,16]{1,0:T(4,128)S(1)}, u32[]{:S(2)}, u32[]{:S(2)}) collective-permute-start(f32[4,16]{1,0:T(4,128)S(1)} %shard_map.136.total_ref), channel_id=1, source_target_pairs={{0,2},{1,3},{2,0},{3,1},{4,6},{5,7},{6,4},{7,5},{8,10},{9,11},{10,... | collective-permute-start | bytes 776 | tf_op jit(solution)/shard_map/ppermute | solution.py:30

commit v2 on v1

--- a/solution.py
+++ b/solution.py
@@ -289,9 +289,10 @@
         rounded = cross.astype(BF16)
         out_ref[:, cols] = rounded
         score = score + rounded.astype(F32) * added(map_refs, cols)
-    high = score.astype(BF16)
-    out_ref[:, pl.ds(width, LANES)] = high
-    out_ref[:, pl.ds(width + LANES, LANES)] = (score - high.astype(F32)).astype(BF16)
+    score = score[:, : LANES // 2] + score[:, LANES // 2 :]
+    high = score.astype(BF16).astype(F32)
+    both = jnp.concatenate([high, score - high], axis=1)
+    out_ref[:, pl.ds(width, LANES)] = both.astype(BF16)
 
 
 def assemble(*refs):
@@ -301,7 +302,6 @@
         block = lax.axis_index("cand") ^ bit
         rows_ref[aligned(block, part_ref.shape[0]), :] = part_ref[:, pl.ds(0, width)]
         lanes = part_ref[:, pl.ds(width, LANES)].astype(F32)
-        lanes = lanes + part_ref[:, pl.ds(width + LANES, LANES)].astype(F32)
         logit_ref[pl.ds(block, 1), :] = jnp.sum(lanes.T, axis=0, keepdims=True)
 
 
@@ -474,7 +474,7 @@
     if direct:
         (block,) = call(
             functools.partial(cross_scored, cand_count),
-            [((local_rows, feat_block + 2 * LANES), BF16)],
+            [((local_rows, feat_block + LANES), BF16)],
             [base_model, bias_two, *parts, *maps],
         )
         parts = [block] + [swap(block, "cand", bit) for bit in range(1, cand_count)]

time: 64.3 us -> 64.3 us (level)
  no operation moved by 1% of the time
where the time goes in v2:
time: 64.3 us; the launch traced here: 64.1 us
  starting transfers between devices  25.5 us (40%)
  waiting for transfers between devices  24.7 us (38%)
  Pallas kernels  8.9 us (14%)
  local copies, waits for them, and re-layouts  3.53 us (5%)
  between operations  1.53 us (2%)
    ppermute x21, starting transfers between devices, swap(): return lax.ppermute(value, axis, [(i, i ^ bit) for i in range(count)])  25.5 us
    ppermute x21, waiting for transfers between devices, swap(): return lax.ppermute(value, axis, [(i, i ^ bit) for i in range(count)])  24.7 us
    pallas_call x16, Pallas kernels, call(): pl.pallas_call(kernel, out_shape=[jax.ShapeDtypeStruct(s, d) for s, d in...  8.9 us
    unnamed x24, local copies, waits for them, and re-layouts  3.52 us
  transfers between devices with their start and end apart: 21, of which 13 were waited for; matrix products, arithmetic and copies ran while one was open for 0% of the time, Pallas kernels for 9%

profile of v2, /device:TPU:0, one launch (start us, length us, event | category | flops | bytes accessed | tf_op | source)
XLA Modules:
  0.0 64.1 jit_solution(3269716384688775201)
XLA Ops:
  0.7 0.6 copy-done.6
  1.3 1.0 %copy-done.1 = bf16[256,4096]{1,0:T(8,128)(2,1)S(1)} copy-done((bf16[256,4096]{1,0:T(8,128)(2,1)S(1)}, bf16[256,4096]{1,0:T(8,128)(2,1)}, u32[]{:S(2)}) %copy-start.1) | copy-done | bytes 2097176
  2.2 0.5 shard_map.124
  2.8 1.9 %copy-done = bf16[2048,2048]{1,0:T(8,128)(2,1)S(1)} copy-done((bf16[2048,2048]{1,0:T(8,128)(2,1)S(1)}, bf16[2048,2048]{1,0:T(8,128)(2,1)}, u32[]{:S(2)}) %copy-start) | copy-done | bytes 8388632
  4.7 0.6 collective-permute-start.3
  5.3 1.0 %collective-permute-done.3.other_ref = bf16[32,2048]{1,0:T(8,128)(2,1)S(1)} collective-permute-done((bf16[32,2048]{1,0:T(8,128)(2,1)S(1)}, bf16[32,2048]{1,0:T(8,128)(2,1)S(1)}, u32[]{:S(2)}, u32[]{:S(2)}) %collective-permute-start.3) | collective-permute-done | bytes 131104 | tf_op jit(solution)/shard_map/ppermute | solution.py:30
  6.3 4.5 %collective-permute-start.4 = (bf16[32,2048]{1,0:T(8,128)(2,1)S(1)}, bf16[32,2048]{1,0:T(8,128)(2,1)S(1)}, u32[]{:S(2)}, u32[]{:S(2)}) collective-permute-start(bf16[32,2048]{1,0:T(8,128)(2,1)S(1)} %get-tuple-element.36), channel_id=1, source_target_pairs={{0,2},{1,3},{2,0},{3,1},{4,6},{5,7},{6,4},{7,5},{8,10},{9,11},{10,... | collective-permute-start | bytes 393224 | tf_op jit(solution)/shard_map/ppermute | solution.py:30
  10.8 3.8 %collective-permute-done.4.other_ref = bf16[32,2048]{1,0:T(8,128)(2,1)S(1)} collective-permute-done((bf16[32,2048]{1,0:T(8,128)(2,1)S(1)}, bf16[32,2048]{1,0:T(8,128)(2,1)S(1)}, u32[]{:S(2)}, u32[]{:S(2)}) %collective-permute-start.4) | collective-permute-done | bytes 131104 | tf_op jit(solution)/shard_map/ppermute | solution.py:30
  14.7 0.1 collective-permute-start.5
  14.7 1.6 %collective-permute-start = (bf16[1,4096]{1,0:T(2,128)(2,1)S(1)}, bf16[1,4096]{1,0:T(2,128)(2,1)S(1)}, u32[]{:S(2)}, u32[]{:S(2)}) collective-permute-start(bf16[1,4096]{1,0:T(2,128)(2,1)S(1)} %copy-done.3), channel_id=1, source_target_pairs={{0,4},{4,0},{8,12},{12,8},{1,5},{5,1},{9,13},{13,9},{2,6},{6,2},{1... | collective-permute-start | bytes 24584 | tf_op jit(solution)/shard_map/ppermute | solution.py:30
  16.4 2.6 %collective-permute-start.1 = (bf16[1,4096]{1,0:T(2,128)(2,1)S(1)}, bf16[1,4096]{1,0:T(2,128)(2,1)S(1)}, u32[]{:S(2)}, u32[]{:S(2)}) collective-permute-start(bf16[1,4096]{1,0:T(2,128)(2,1)S(1)} %copy-done.3), channel_id=1, source_target_pairs={{0,8},{4,12},{8,0},{12,4},{1,9},{5,13},{9,1},{13,5},{2,10},{6,14},... | collective-permute-start | bytes 24584 | tf_op jit(solution)/shard_map/ppermute | solution.py:30
  19.0 0.2 collective-permute-start.2
  19.9 0.0 collective-permute-done.refs_1_
  19.9 1.2 %collective-permute-done.1.refs_2_ = bf16[1,4096]{1,0:T(2,128)(2,1)S(1)} collective-permute-done((bf16[1,4096]{1,0:T(2,128)(2,1)S(1)}, bf16[1,4096]{1,0:T(2,128)(2,1)S(1)}, u32[]{:S(2)}, u32[]{:S(2)}) %collective-permute-start.1) | collective-permute-done | bytes 8224 | tf_op jit(solution)/shard_map/ppermute | solution.py:30
  21.1 3.4 %collective-permute-done.2.refs_3_ = bf16[1,4096]{1,0:T(2,128)(2,1)S(1)} collective-permute-done((bf16[1,4096]{1,0:T(2,128)(2,1)S(1)}, bf16[1,4096]{1,0:T(2,128)(2,1)S(1)}, u32[]{:S(2)}, u32[]{:S(2)}) %collective-permute-start.2) | collective-permute-done | bytes 8224 | tf_op jit(solution)/shard_map/ppermute | solution.py:30
  24.5 1.3 %shard_map.125 = (bf16[64,2048]{1,0:T(8,128)(2,1)S(1)}, bf16[64,2048]{1,0:T(8,128)(2,1)S(1)}, f32[1,2048]{1,0:T(1,128)S(1)}) custom-call(s32[1,128]{1,0:T(1,128)S(1)} %shard_map.122.want_ref, bf16[2048,2048]{1,0:T(8,128)(2,1)S(1)} %copy-done, bf16[64,2048]{1,0:T(8,128)(2,1)S(1)} %get-tuple-element.29.pool_model_ref.rows_ref, ...), custom_call_target="tpu_custom_call" | custom-call | flops 536870912 | bytes 1090048 | tf_op jit(solution)/shard_map/pallas_call | solution.py:36
  25.9 0.0 copy-start.4
  25.9 2.5 %shard_map.131 = (f32[16,2176]{1,0:T(8,128)S(1)}, bf16[16,2176]{1,0:T(8,128)(2,1)S(1)}, bf16[16,2176]{1,0:T(8,128)(2,1)S(1)}, bf16[16,2176]{1,0:T(8,128)(2,1)S(1)}) custom-call(bf16[64,2048]{1,0:T(8,128)(2,1)S(1)} %get-tuple-element.31.cand_ref.base_ref, bf16[1,2048]{1,0:T(2,128)(2,1)S(1)} %reshape.21.score_ref, f32[1,2048]{1,0:T(1,128)S(1)} %bitcast.8, ...), custom_call_target="tpu_custom_call" | custom-call | flops 536870912 | bytes 622592 | tf_op jit(solution)/shard_map/pallas_call | solution.py:36
  28.4 0.1 collective-permute-start.11
  28.5 0.1 collective-permute-start.6
  28.6 1.2 %collective-permute-done.6.refs_1_ = f32[1,2048]{1,0:T(1,128)S(1)} collective-permute-done((f32[1,2048]{1,0:T(1,128)S(1)}, f32[1,2048]{1,0:T(1,128)S(1)}, u32[]{:S(2)}, u32[]{:S(2)}) %collective-permute-start.6) | collective-permute-done | bytes 8224 | tf_op jit(solution)/shard_map/ppermute | solution.py:30
  29.7 0.5 collective-permute-start.7
  30.2 1.0 %collective-permute-start.12 = (bf16[16,2176]{1,0:T(8,128)(2,1)S(1)}, bf16[16,2176]{1,0:T(8,128)(2,1)S(1)}, u32[]{:S(2)}, u32[]{:S(2)}) collective-permute-start(bf16[16,2176]{1,0:T(8,128)(2,1)S(1)} %get-tuple-element.46), channel_id=1, source_target_pairs={{0,8},{4,12},{8,0},{12,4},{1,9},{5,13},{9,1},{13,5},{2,10},{6,14},... | collective-permute-start | bytes 208904 | tf_op jit(solution)/shard_map/ppermute | solution.py:30
  31.2 3.3 %collective-permute-start.13 = (bf16[16,2176]{1,0:T(8,128)(2,1)S(1)}, bf16[16,2176]{1,0:T(8,128)(2,1)S(1)}, u32[]{:S(2)}, u32[]{:S(2)}) collective-permute-start(bf16[16,2176]{1,0:T(8,128)(2,1)S(1)} %get-tuple-element.47), channel_id=1, source_target_pairs={{0,12},{4,8},{8,4},{12,0},{1,13},{5,9},{9,5},{13,1},{2,14},{6,10},... | collective-permute-start | bytes 208904 | tf_op jit(solution)/shard_map/ppermute | solution.py:30
  34.5 0.0 collective-permute-done.7.user_other_ref
  34.5 0.0 collective-permute-done.5.other_ref
  34.5 1.7 %shard_map.130 = (f32[16,2048]{1,0:T(8,128)S(1)}, bf16[16,2048]{1,0:T(8,128)(2,1)S(1)}, bf16[16,2048]{1,0:T(8,128)(2,1)S(1)}, bf16[16,2048]{1,0:T(8,128)(2,1)S(1)}) custom-call(f32[32,2048]{1,0:T(8,128)S(1)} %get-tuple-element.37.mine_ref, bf16[32,2048]{1,0:T(8,128)(2,1)S(1)} %collective-permute-done.5.other_ref, f32[1,2048]{1,0:T(1,128)S(1)} %shard_map.129.user_ref, ...), custom_call_target="tpu_custom_call" | custom-call | flops 536870912 | bytes 1269760 | tf_op jit(solution)/shard_map/pallas_call | solution.py:36
  36.2 0.8 %collective-permute-start.8 = (bf16[16,2048]{1,0:T(8,128)(2,1)S(1)}, bf16[16,2048]{1,0:T(8,128)(2,1)S(1)}, u32[]{:S(2)}, u32[]{:S(2)}) collective-permute-start(bf16[16,2048]{1,0:T(8,128)(2,1)S(1)} %get-tuple-element.41), channel_id=1, source_target_pairs={{0,4},{4,0},{8,12},{12,8},{1,5},{5,1},{9,13},{13,9},{2,6},{6,2},{1... | collective-permute-start | bytes 196616 | tf_op jit(solution)/shard_map/ppermute | solution.py:30
  37.1 0.2 collective-permute-start.9
  37.3 3.4 %collective-permute-start.10 = (bf16[16,2048]{1,0:T(8,128)(2,1)S(1)}, bf16[16,2048]{1,0:T(8,128)(2,1)S(1)}, u32[]{:S(2)}, u32[]{:S(2)}) collective-permute-start(bf16[16,2048]{1,0:T(8,128)(2,1)S(1)} %get-tuple-element.43), channel_id=1, source_target_pairs={{0,12},{4,8},{8,4},{12,0},{1,13},{5,9},{9,5},{13,1},{2,14},{6,10},... | collective-permute-start | bytes 196616 | tf_op jit(solution)/shard_map/ppermute | solution.py:30
  40.7 0.2 collective-permute-done.8.refs_1_
  40.9 3.5 %collective-permute-done.9.refs_2_ = bf16[16,2048]{1,0:T(8,128)(2,1)S(1)} collective-permute-done((bf16[16,2048]{1,0:T(8,128)(2,1)S(1)}, bf16[16,2048]{1,0:T(8,128)(2,1)S(1)}, u32[]{:S(2)}, u32[]{:S(2)}) %collective-permute-start.9) | collective-permute-done | bytes 65568 | tf_op jit(solution)/shard_map/ppermute | solution.py:30
  44.5 0.2 shard_map.132.refs_0_
  44.7 1.3 %collective-permute-start.14 = (bf16[16,2176]{1,0:T(8,128)(2,1)S(1)}, bf16[16,2176]{1,0:T(8,128)(2,1)S(1)}, u32[]{:S(2)}, u32[]{:S(2)}) collective-permute-start(bf16[16,2176]{1,0:T(8,128)(2,1)S(1)} %shard_map.132.refs_0_), channel_id=1, source_target_pairs={{0,4},{4,0},{8,12},{12,8},{1,5},{5,1},{9,13},{13,9},{2,6},{6,2},{1... | collective-permute-start | bytes 208904 | tf_op jit(solution)/shard_map/ppermute | solution.py:30
  46.0 1.7 %collective-permute-start.15 = (bf16[16,2176]{1,0:T(8,128)(2,1)S(1)}, bf16[16,2176]{1,0:T(8,128)(2,1)S(1)}, u32[]{:S(2)}, u32[]{:S(2)}) collective-permute-start(bf16[16,2176]{1,0:T(8,128)(2,1)S(1)} %shard_map.132.refs_0_), channel_id=1, source_target_pairs={{0,8},{4,12},{8,0},{12,4},{1,9},{5,13},{9,1},{13,5},{2,10},{6,14},... | collective-permute-start | bytes 208904 | tf_op jit(solution)/shard_map/ppermute | solution.py:30
  47.6 1.5 %collective-permute-start.16 = (bf16[16,2176]{1,0:T(8,128)(2,1)S(1)}, bf16[16,2176]{1,0:T(8,128)(2,1)S(1)}, u32[]{:S(2)}, u32[]{:S(2)}) collective-permute-start(bf16[16,2176]{1,0:T(8,128)(2,1)S(1)} %shard_map.132.refs_0_), channel_id=1, source_target_pairs={{0,12},{4,8},{8,4},{12,0},{1,13},{5,9},{9,5},{13,1},{2,14},{6,10},... | collective-permute-start | bytes 208904 | tf_op jit(solution)/shard_map/ppermute | solution.py:30
  49.1 1.5 %collective-permute-done.14.refs_1_ = bf16[16,2176]{1,0:T(8,128)(2,1)S(1)} collective-permute-done((bf16[16,2176]{1,0:T(8,128)(2,1)S(1)}, bf16[16,2176]{1,0:T(8,128)(2,1)S(1)}, u32[]{:S(2)}, u32[]{:S(2)}) %collective-permute-start.14) | collective-permute-done | bytes 69664 | tf_op jit(solution)/shard_map/ppermute | solution.py:30
  50.6 1.9 %collective-permute-done.15.refs_2_ = bf16[16,2176]{1,0:T(8,128)(2,1)S(1)} collective-permute-done((bf16[16,2176]{1,0:T(8,128)(2,1)S(1)}, bf16[16,2176]{1,0:T(8,128)(2,1)S(1)}, u32[]{:S(2)}, u32[]{:S(2)}) %collective-permute-start.15) | collective-permute-done | bytes 69664 | tf_op jit(solution)/shard_map/ppermute | solution.py:30
  52.5 1.3 %collective-permute-done.16.refs_3_ = bf16[16,2176]{1,0:T(8,128)(2,1)S(1)} collective-permute-done((bf16[16,2176]{1,0:T(8,128)(2,1)S(1)}, bf16[16,2176]{1,0:T(8,128)(2,1)S(1)}, u32[]{:S(2)}, u32[]{:S(2)}) %collective-permute-start.16) | collective-permute-done | bytes 69664 | tf_op jit(solution)/shard_map/ppermute | solution.py:30
  53.8 0.1 shard_map.133
  54.0 1.7 %shard_map.134 = (f32[32,2048]{1,0:T(8,128)S(1)}, bf16[32,2048]{1,0:T(8,128)(2,1)S(1)}) custom-call(bf16[64,2048]{1,0:T(8,128)(2,1)S(1)} %get-tuple-element.31.cand_ref.base_ref, bf16[2048,2048]{1,0:T(8,128)(2,1)S(1)} %bitcast.5, bf16[64,2048]{1,0:T(8,128)(2,1)S(1)} %get-tuple-element.48.rows_ref), custom_call_target="tpu_custom_call" | custom-call | flops 536870912 | bytes 917504 | tf_op jit(solution)/shard_map/pallas_call | solution.py:36
  55.6 0.1 collective-permute-start.17
  55.7 1.3 %collective-permute-done.17.other_ref = bf16[32,2048]{1,0:T(8,128)(2,1)S(1)} collective-permute-done((bf16[32,2048]{1,0:T(8,128)(2,1)S(1)}, bf16[32,2048]{1,0:T(8,128)(2,1)S(1)}, u32[]{:S(2)}, u32[]{:S(2)}) %collective-permute-start.17) | collective-permute-done | bytes 131104 | tf_op jit(solution)/shard_map/ppermute | solution.py:30
  57.1 1.6 %collective-permute-start.18 = (bf16[16,2048]{1,0:T(8,128)(2,1)S(1)}, bf16[16,2048]{1,0:T(8,128)(2,1)S(1)}, u32[]{:S(2)}, u32[]{:S(2)}) collective-permute-start(bf16[16,2048]{1,0:T(8,128)(2,1)S(1)} %get-tuple-element.52), channel_id=1, source_target_pairs={{0,2},{1,3},{2,0},{3,1},{4,6},{5,7},{6,4},{7,5},{8,10},{9,11},{10,... | collective-permute-start | bytes 196616 | tf_op jit(solution)/shard_map/ppermute | solution.py:30
  58.7 1.2 %collective-permute-done.19.refs_1_ = f32[4,16]{1,0:T(4,128)S(1)} collective-permute-done((f32[4,16]{1,0:T(4,128)S(1)}, f32[4,16]{1,0:T(4,128)S(1)}, u32[]{:S(2)}, u32[]{:S(2)}) %collective-permute-start.19) | collective-permute-done | bytes 288 | tf_op jit(solution)/shard_map/ppermute | solution.py:30
  59.9 0.5 collective-permute-start.20
  60.4 3.1 %collective-permute-done.20.part_ref = f32[4,16]{1,0:T(4,128)S(1)} collective-permute-done((f32[4,16]{1,0:T(4,128)S(1)}, f32[4,16]{1,0:T(4,128)S(1)}, u32[]{:S(2)}, u32[]{:S(2)}) %collective-permute-start.20) | collective-permute-done | bytes 288 | tf_op jit(solution)/shard_map/ppermute | solution.py:30
  63.5 0.7 %shard_map.137 = (bf16[16,2048]{1,0:T(8,128)(2,1)}, f32[1,16]{1,0:T(1,128)}) custom-call(f32[16,2048]{1,0:T(8,128)S(1)} %get-tuple-element.51.keep_ref, bf16[16,2048]{1,0:T(8,128)(2,1)S(1)} %collective-permute-done.18.other_ref, bf16[64,2048]{1,0:T(8,128)(2,1)S(1)} %get-tuple-element.31.cand_ref.base_ref, f32[1,2048]{1,0:T(1,128)S(1)} %bitcast.9, ...), custom_call_target="tpu_custom_call" | custom-call | bytes 533056 | tf_op jit(solution)/shard_map/pallas_call | solution.py:36
  (37 shorter events, 0.2 us)
Async XLA Ops:
  0.6 0.7 %copy-start.6 = (s32[1,64]{1,0:T(1,128)S(1)}, s32[1,64]{1,0:T(1,128)}, u32[]{:S(2)}) copy-start(s32[1,64]{1,0:T(1,128)} %ids_ref.1) | copy-start | bytes 772
  0.6 1.6 %copy-start.1 = (bf16[256,4096]{1,0:T(8,128)(2,1)S(1)}, bf16[256,4096]{1,0:T(8,128)(2,1)}, u32[]{:S(2)}) copy-start(bf16[256,4096]{1,0:T(8,128)(2,1)} %pool_ref.1) | copy-start | bytes 6291460
  0.7 4.0 %copy-start = (bf16[2048,2048]{1,0:T(8,128)(2,1)S(1)}, bf16[2048,2048]{1,0:T(8,128)(2,1)}, u32[]{:S(2)}) copy-start(bf16[2048,2048]{1,0:T(8,128)(2,1)} %weight_ref.6) | copy-start | bytes 25165828
  2.2 12.5 %copy-start.3 = (bf16[1,4096]{1,0:T(2,128)(2,1)S(1)}, bf16[1,4096]{1,0:T(2,128)(2,1)}, u32[]{:S(2)}) copy-start(bf16[1,4096]{1,0:T(2,128)(2,1)} %refs_0_.1) | copy-start | bytes 24580
  2.2 17.6 %copy-start.7 = (bf16[2048]{0:T(1024)(128)(2,1)S(1)}, bf16[2048]{0:T(1024)(128)(2,1)}, u32[]{:S(2)}) copy-start(bf16[2048]{0:T(1024)(128)(2,1)} %param.21) | copy-start | bytes 12292
  4.7 21.2 %slice-start = ((s8[8388608]{0:T(1024)(128)(4,1)}), s8[4194304]{0:T(1024)(128)(4,1)S(1)}, s32[]{:S(2)}) async-start(s8[8388608]{0:T(1024)(128)(4,1)} %bitcast.4), calls=%async_computation | async-start | bytes 8388608
  4.7 21.2 %copy-start.2 = (f32[2048]{0:T(1024)S(1)}, f32[2048]{0:T(1024)}, u32[]{:S(2)}) copy-start(f32[2048]{0:T(1024)} %param.20) | copy-start | bytes 24580
  4.7 29.8 %slice-start.2 = ((s8[8388608]{0:T(1024)(128)(4,1)}), s8[4194304]{0:T(1024)(128)(4,1)S(1)}, s32[]{:S(2)}) async-start(s8[8388608]{0:T(1024)(128)(4,1)} %bitcast.6), calls=%async_computation.2 | async-start | bytes 8388608
  4.7 1.5 %collective-permute-start.3 = (bf16[32,2048]{1,0:T(8,128)(2,1)S(1)}, bf16[32,2048]{1,0:T(8,128)(2,1)S(1)}, u32[]{:S(2)}, u32[]{:S(2)}) collective-permute-start(bf16[32,2048]{1,0:T(8,128)(2,1)S(1)} %get-tuple-element.34), channel_id=1, source_target_pairs={{0,1},{1,0},{2,3},{3,2},{4,5},{5,4},{6,7},{7,6},{8,9},{9,8},{10,11... | collective-permute-start | bytes 393224 | tf_op jit(solution)/shard_map/ppermute | solution.py:30
  6.3 8.3 %collective-permute-start.4 = (bf16[32,2048]{1,0:T(8,128)(2,1)S(1)}, bf16[32,2048]{1,0:T(8,128)(2,1)S(1)}, u32[]{:S(2)}, u32[]{:S(2)}) collective-permute-start(bf16[32,2048]{1,0:T(8,128)(2,1)S(1)} %get-tuple-element.36), channel_id=1, source_target_pairs={{0,2},{1,3},{2,0},{3,1},{4,6},{5,7},{6,4},{7,5},{8,10},{9,11},{10,... | collective-permute-start | bytes 393224 | tf_op jit(solution)/shard_map/ppermute | solution.py:30
  14.6 11.3 %slice-start.1 = ((s8[8388608]{0:T(1024)(128)(4,1)}), s8[4194304]{0:T(1024)(128)(4,1)S(1)}, s32[]{:S(2)}) async-start(s8[8388608]{0:T(1024)(128)(4,1)} %bitcast.4), calls=%async_computation.1 | async-start | bytes 8388608
  14.7 19.9 %collective-permute-start.5 = (bf16[32,2048]{1,0:T(8,128)(2,1)S(1)}, bf16[32,2048]{1,0:T(8,128)(2,1)S(1)}, u32[]{:S(2)}, u32[]{:S(2)}) collective-permute-start(bf16[32,2048]{1,0:T(8,128)(2,1)S(1)} %get-tuple-element.38), channel_id=1, source_target_pairs={{0,1},{1,0},{2,3},{3,2},{4,5},{5,4},{6,7},{7,6},{8,9},{9,8},{10,11... | collective-permute-start | bytes 393224 | tf_op jit(solution)/shard_map/ppermute | solution.py:30
  14.7 5.2 %collective-permute-start = (bf16[1,4096]{1,0:T(2,128)(2,1)S(1)}, bf16[1,4096]{1,0:T(2,128)(2,1)S(1)}, u32[]{:S(2)}, u32[]{:S(2)}) collective-permute-start(bf16[1,4096]{1,0:T(2,128)(2,1)S(1)} %copy-done.3), channel_id=1, source_target_pairs={{0,4},{4,0},{8,12},{12,8},{1,5},{5,1},{9,13},{13,9},{2,6},{6,2},{1... | collective-permute-start | bytes 24584 | tf_op jit(solution)/shard_map/ppermute | solution.py:30
  16.4 4.7 %collective-permute-start.1 = (bf16[1,4096]{1,0:T(2,128)(2,1)S(1)}, bf16[1,4096]{1,0:T(2,128)(2,1)S(1)}, u32[]{:S(2)}, u32[]{:S(2)}) collective-permute-start(bf16[1,4096]{1,0:T(2,128)(2,1)S(1)} %copy-done.3), channel_id=1, source_target_pairs={{0,8},{4,12},{8,0},{12,4},{1,9},{5,13},{9,1},{13,5},{2,10},{6,14},... | collective-permute-start | bytes 24584 | tf_op jit(solution)/shard_map/ppermute | solution.py:30
  19.0 5.5 %collective-permute-start.2 = (bf16[1,4096]{1,0:T(2,128)(2,1)S(1)}, bf16[1,4096]{1,0:T(2,128)(2,1)S(1)}, u32[]{:S(2)}, u32[]{:S(2)}) collective-permute-start(bf16[1,4096]{1,0:T(2,128)(2,1)S(1)} %copy-done.3), channel_id=1, source_target_pairs={{0,12},{4,8},{8,4},{12,0},{1,13},{5,9},{9,5},{13,1},{2,14},{6,10},... | collective-permute-start | bytes 24584 | tf_op jit(solution)/shard_map/ppermute | solution.py:30
  24.5 10.0 %slice-start.3 = ((s8[8388608]{0:T(1024)(128)(4,1)}), s8[4194304]{0:T(1024)(128)(4,1)S(1)}, s32[]{:S(2)}) async-start(s8[8388608]{0:T(1024)(128)(4,1)} %bitcast.6), calls=%async_computation.3 | async-start | bytes 8388608
  24.5 10.0 %copy-start.5 = (f32[2048]{0:T(1024)S(1)}, f32[2048]{0:T(1024)}, u32[]{:S(2)}) copy-start(f32[2048]{0:T(1024)} %param.16) | copy-start | bytes 24580
  25.9 18.6 %copy-start.4 = (f32[2048]{0:T(1024)S(1)}, f32[2048]{0:T(1024)}, u32[]{:S(2)}) copy-start(f32[2048]{0:T(1024)} %param.18) | copy-start | bytes 24580
  28.4 8.9 %collective-permute-start.11 = (bf16[16,2176]{1,0:T(8,128)(2,1)S(1)}, bf16[16,2176]{1,0:T(8,128)(2,1)S(1)}, u32[]{:S(2)}, u32[]{:S(2)}) collective-permute-start(bf16[16,2176]{1,0:T(8,128)(2,1)S(1)} %get-tuple-element.45), channel_id=1, source_target_pairs={{0,4},{4,0},{8,12},{12,8},{1,5},{5,1},{9,13},{13,9},{2,6},{6,2},{1... | collective-permute-start | bytes 208904 | tf_op jit(solution)/shard_map/ppermute | solution.py:30
  28.5 1.2 %collective-permute-start.6 = (f32[1,2048]{1,0:T(1,128)S(1)}, f32[1,2048]{1,0:T(1,128)S(1)}, u32[]{:S(2)}, u32[]{:S(2)}) collective-permute-start(f32[1,2048]{1,0:T(1,128)S(1)} %get-tuple-element.39.refs_0_), channel_id=1, source_target_pairs={{0,1},{1,0},{2,3},{3,2},{4,5},{5,4},{6,7},{7,6},{8,9},{9,8},{10,11... | collective-permute-start | bytes 24584 | tf_op jit(solution)/shard_map/ppermute | solution.py:30
  29.7 4.8 %collective-permute-start.7 = (f32[1,2048]{1,0:T(1,128)S(1)}, f32[1,2048]{1,0:T(1,128)S(1)}, u32[]{:S(2)}, u32[]{:S(2)}) collective-permute-start(f32[1,2048]{1,0:T(1,128)S(1)} %shard_map.129.user_ref), channel_id=1, source_target_pairs={{0,2},{1,3},{2,0},{3,1},{4,6},{5,7},{6,4},{7,5},{8,10},{9,11},{10,... | collective-permute-start | bytes 24584 | tf_op jit(solution)/shard_map/ppermute | solution.py:30
  30.2 10.5 %collective-permute-start.12 = (bf16[16,2176]{1,0:T(8,128)(2,1)S(1)}, bf16[16,2176]{1,0:T(8,128)(2,1)S(1)}, u32[]{:S(2)}, u32[]{:S(2)}) collective-permute-start(bf16[16,2176]{1,0:T(8,128)(2,1)S(1)} %get-tuple-element.46), channel_id=1, source_target_pairs={{0,8},{4,12},{8,0},{12,4},{1,9},{5,13},{9,1},{13,5},{2,10},{6,14},... | collective-permute-start | bytes 208904 | tf_op jit(solution)/shard_map/ppermute | solution.py:30
  31.2 9.5 %collective-permute-start.13 = (bf16[16,2176]{1,0:T(8,128)(2,1)S(1)}, bf16[16,2176]{1,0:T(8,128)(2,1)S(1)}, u32[]{:S(2)}, u32[]{:S(2)}) collective-permute-start(bf16[16,2176]{1,0:T(8,128)(2,1)S(1)} %get-tuple-element.47), channel_id=1, source_target_pairs={{0,12},{4,8},{8,4},{12,0},{1,13},{5,9},{9,5},{13,1},{2,14},{6,10},... | collective-permute-start | bytes 208904 | tf_op jit(solution)/shard_map/ppermute | solution.py:30
  36.2 4.7 %collective-permute-start.8 = (bf16[16,2048]{1,0:T(8,128)(2,1)S(1)}, bf16[16,2048]{1,0:T(8,128)(2,1)S(1)}, u32[]{:S(2)}, u32[]{:S(2)}) collective-permute-start(bf16[16,2048]{1,0:T(8,128)(2,1)S(1)} %get-tuple-element.41), channel_id=1, source_target_pairs={{0,4},{4,0},{8,12},{12,8},{1,5},{5,1},{9,13},{13,9},{2,6},{6,2},{1... | collective-permute-start | bytes 196616 | tf_op jit(solution)/shard_map/ppermute | solution.py:30
  37.1 7.4 %collective-permute-start.9 = (bf16[16,2048]{1,0:T(8,128)(2,1)S(1)}, bf16[16,2048]{1,0:T(8,128)(2,1)S(1)}, u32[]{:S(2)}, u32[]{:S(2)}) collective-permute-start(bf16[16,2048]{1,0:T(8,128)(2,1)S(1)} %get-tuple-element.42), channel_id=1, source_target_pairs={{0,8},{4,12},{8,0},{12,4},{1,9},{5,13},{9,1},{13,5},{2,10},{6,14},... | collective-permute-start | bytes 196616 | tf_op jit(solution)/shard_map/ppermute | solution.py:30
  37.3 7.1 %collective-permute-start.10 = (bf16[16,2048]{1,0:T(8,128)(2,1)S(1)}, bf16[16,2048]{1,0:T(8,128)(2,1)S(1)}, u32[]{:S(2)}, u32[]{:S(2)}) collective-permute-start(bf16[16,2048]{1,0:T(8,128)(2,1)S(1)} %get-tuple-element.43), channel_id=1, source_target_pairs={{0,12},{4,8},{8,4},{12,0},{1,13},{5,9},{9,5},{13,1},{2,14},{6,10},... | collective-permute-start | bytes 196616 | tf_op jit(solution)/shard_map/ppermute | solution.py:30
  44.7 5.9 %collective-permute-start.14 = (bf16[16,2176]{1,0:T(8,128)(2,1)S(1)}, bf16[16,2176]{1,0:T(8,128)(2,1)S(1)}, u32[]{:S(2)}, u32[]{:S(2)}) collective-permute-start(bf16[16,2176]{1,0:T(8,128)(2,1)S(1)} %shard_map.132.refs_0_), channel_id=1, source_target_pairs={{0,4},{4,0},{8,12},{12,8},{1,5},{5,1},{9,13},{13,9},{2,6},{6,2},{1... | collective-permute-start | bytes 208904 | tf_op jit(solution)/shard_map/ppermute | solution.py:30
  46.0 6.5 %collective-permute-start.15 = (bf16[16,2176]{1,0:T(8,128)(2,1)S(1)}, bf16[16,2176]{1,0:T(8,128)(2,1)S(1)}, u32[]{:S(2)}, u32[]{:S(2)}) collective-permute-start(bf16[16,2176]{1,0:T(8,128)(2,1)S(1)} %shard_map.132.refs_0_), channel_id=1, source_target_pairs={{0,8},{4,12},{8,0},{12,4},{1,9},{5,13},{9,1},{13,5},{2,10},{6,14},... | collective-permute-start | bytes 208904 | tf_op jit(solution)/shard_map/ppermute | solution.py:30
  47.6 6.2 %collective-permute-start.16 = (bf16[16,2176]{1,0:T(8,128)(2,1)S(1)}, bf16[16,2176]{1,0:T(8,128)(2,1)S(1)}, u32[]{:S(2)}, u32[]{:S(2)}) collective-permute-start(bf16[16,2176]{1,0:T(8,128)(2,1)S(1)} %shard_map.132.refs_0_), channel_id=1, source_target_pairs={{0,12},{4,8},{8,4},{12,0},{1,13},{5,9},{9,5},{13,1},{2,14},{6,10},... | collective-permute-start | bytes 208904 | tf_op jit(solution)/shard_map/ppermute | solution.py:30
  55.6 1.4 %collective-permute-start.17 = (bf16[32,2048]{1,0:T(8,128)(2,1)S(1)}, bf16[32,2048]{1,0:T(8,128)(2,1)S(1)}, u32[]{:S(2)}, u32[]{:S(2)}) collective-permute-start(bf16[32,2048]{1,0:T(8,128)(2,1)S(1)} %get-tuple-element.50), channel_id=1, source_target_pairs={{0,1},{1,0},{2,3},{3,2},{4,5},{5,4},{6,7},{7,6},{8,9},{9,8},{10,11... | collective-permute-start | bytes 393224 | tf_op jit(solution)/shard_map/ppermute | solution.py:30
  57.1 6.3 %collective-permute-start.18 = (bf16[16,2048]{1,0:T(8,128)(2,1)S(1)}, bf16[16,2048]{1,0:T(8,128)(2,1)S(1)}, u32[]{:S(2)}, u32[]{:S(2)}) collective-permute-start(bf16[16,2048]{1,0:T(8,128)(2,1)S(1)} %get-tuple-element.52), channel_id=1, source_target_pairs={{0,2},{1,3},{2,0},{3,1},{4,6},{5,7},{6,4},{7,5},{8,10},{9,11},{10,... | collective-permute-start | bytes 196616 | tf_op jit(solution)/shard_map/ppermute | solution.py:30
  58.7 1.2 %collective-permute-start.19 = (f32[4,16]{1,0:T(4,128)S(1)}, f32[4,16]{1,0:T(4,128)S(1)}, u32[]{:S(2)}, u32[]{:S(2)}) collective-permute-start(f32[4,16]{1,0:T(4,128)S(1)} %get-tuple-element.53.refs_0_), channel_id=1, source_target_pairs={{0,1},{1,0},{2,3},{3,2},{4,5},{5,4},{6,7},{7,6},{8,9},{9,8},{10,11... | collective-permute-start | bytes 776 | tf_op jit(solution)/shard_map/ppermute | solution.py:30
  59.9 3.6 %collective-permute-start.20 = (f32[4,16]{1,0:T(4,128)S(1)}, f32[4,16]{1,0:T(4,128)S(1)}, u32[]{:S(2)}, u32[]{:S(2)}) collective-permute-start(f32[4,16]{1,0:T(4,128)S(1)} %shard_map.136.total_ref), channel_id=1, source_target_pairs={{0,2},{1,3},{2,0},{3,1},{4,6},{5,7},{6,4},{7,5},{8,10},{9,11},{10,... | collective-permute-start | bytes 776 | tf_op jit(solution)/shard_map/ppermute | solution.py:30

commit v3 on v2

--- a/solution.py
+++ b/solution.py
@@ -65,10 +65,18 @@
     out_ref[...] = jnp.zeros_like(out_ref)
 
 
-def choose_user(local, bit, slot_ref, own_ref, other_ref, out_ref):
-    want = (slot_ref[...] // local) ^ lax.axis_index("cand")
-    other, own = other_ref[...].astype(F32), own_ref[...].astype(F32)
-    out_ref[...] = jnp.where((jnp.broadcast_to(want, own.shape) & bit) != 0, other, own).astype(BF16)
+def from_owner(want_ref, bit, own, other):
+    differs = (jnp.broadcast_to(want_ref[:, :1], own.shape) & bit) != 0
+    return jnp.where(differs, other.astype(F32), own.astype(F32))
+
+
+def pair_rows(own_ref, other_ref, out_ref):
+    rows = [own_ref[...].astype(F32), other_ref[...].astype(F32)]
+    out_ref[...] = jnp.concatenate(rows, axis=0).astype(BF16)
+
+
+def choose_user(bit, want_ref, own_ref, other_ref, out_ref):
+    out_ref[...] = from_owner(want_ref, bit, own_ref[...], other_ref[...]).astype(BF16)
 
 
 def owner_steps(local, slot_ref, out_ref):
@@ -124,10 +132,10 @@
 
 
 def user_terms(
-    half, want_ref, weight_ref, pool_model_ref, pool_cand_ref, *refs
+    half, bit, want_ref, weight_ref, pool_model_ref, pool_cand_ref, own_ref, other_ref,
+    model_ref, cand_ref, terms_ref,
 ):
-    *part_refs, model_ref, cand_ref, terms_ref = refs
-    users = part_refs[0].shape[0]
+    users = terms_ref.shape[0]
     terms_ref[...] = jnp.zeros_like(terms_ref)
     for axis, pool_ref, out_ref in (
         ("mp", pool_model_ref, model_ref),
@@ -140,11 +148,13 @@
         @pl.when(inside)
         def _():
             cols = aligned(block % (half // width), width)
-            parts = [part_ref[:, cols] for part_ref in part_refs]
-            chosen = parts[0].astype(F32)
-            want = jnp.broadcast_to(want_ref[:, :1], chosen.shape)
-            for bit in range(1, len(parts)):
-                chosen = jnp.where(want == bit, parts[bit].astype(F32), chosen)
+            if own_ref.shape[0] == users:
+                chosen = from_owner(want_ref, bit, own_ref[:, cols], other_ref[:, cols])
+            else:
+                own, other = own_ref[:, cols].astype(F32), other_ref[:, cols].astype(F32)
+                near = from_owner(want_ref, bit, own[:users], other[:users])
+                far = from_owner(want_ref, bit, own[users:], other[users:])
+                chosen = from_owner(want_ref, bit // 2, near, far)
             for user in range(users):
                 out_ref[pl.ds(user * (rows // users), rows // users), :] = jnp.broadcast_to(
                     chosen[user : user + 1], (rows // users, width)
@@ -365,7 +375,7 @@
     row_block = row_total // model_count
     half_rows = row_total // 2
     flops = 2 * row_total * col_block * feat_block
-    direct = cand_count <= DIRECT and cand_count == model_count
+    direct = cand_count == DIRECT and cand_count == model_count
     score, bias = score_weight.reshape(1, -1), third_bias.reshape(1, -1)
 
     if local > 1:
@@ -389,17 +399,18 @@
         [user_slot],
         smem=(0,),
     )
+    *bits, last_bit = bits_of(cand_count)
     if direct:
-        users = [users] + [swap(users, "cand", bit) for bit in range(1, cand_count)]
-    else:
-        slots = user_slot.reshape(-1, 1)
-        for bit in bits_of(cand_count):
-            (users,) = call(
-                functools.partial(choose_user, local, bit),
-                [((user_count, half_width), BF16)],
-                [slots, users, swap(users, "cand", bit)],
-            )
-        users = [users]
+        users_other = swap(users, "cand", 1)
+        (users,) = call(pair_rows, [((2 * user_count, half_width), BF16)], [users, users_other])
+        bits = []
+    for bit in bits:
+        (users,) = call(
+            functools.partial(choose_user, bit),
+            [((user_count, half_width), BF16)],
+            [want, users, swap(users, "cand", bit)],
+        )
+    users_other = swap(users, "cand", last_bit)
 
     half_outs = [((half_rows, col_block), F32), ((half_rows, col_block), BF16)]
     keep, send = call(
@@ -415,13 +426,13 @@
     pool_other = swap(send, "mp", 1)
 
     base_model, base_cand, user_sum = call(
-        functools.partial(user_terms, half_width),
+        functools.partial(user_terms, half_width, last_bit),
         [
             ((row_total, feat_block), BF16),
             ((row_total, col_block), BF16),
             ((user_count, col_block), F32),
         ],
-        [want, first_weight, pool_model, pool_cand, *users],
+        [want, first_weight, pool_model, pool_cand, users, users_other],
         flops=flops,
         limit=12 * MIB,
     )

time: 64.3 us -> 60.8 us (0.946)
  waiting for transfers between devices: 24.7 us -> 21.7 us
    ppermute x21 -> x20, waiting for transfers between devices: 24.7 us -> 21.7 us  [swap(): return lax.ppermute(value, axis, [(i, i ^ bit) for i in range(count)])]
    ppermute x21 -> x20, starting transfers between devices: 25.5 us -> 24.9 us  [swap(): return lax.ppermute(value, axis, [(i, i ^ bit) for i in range(count)])]
    pallas_call x16 -> x17, Pallas kernels: 8.9 us -> 8.92 us  [call(): pl.pallas_call(kernel, out_shape=[jax.ShapeDtypeStruct(s, d) for s, d in...]
  transfers between devices with their start and end apart: 21 -> 20, of which waited for: 13 -> 13; matrix products, arithmetic and copies ran while one was open for 0% -> 0% of each run, Pallas kernels for 9% -> 9%
where the time goes in v3:
time: 60.8 us; the launch traced here: 60.7 us
  starting transfers between devices  24.9 us (41%)
  waiting for transfers between devices  21.7 us (36%)
  Pallas kernels  8.92 us (15%)
  local copies, waits for them, and re-layouts  3.53 us (6%)
  between operations  1.64 us (3%)
    ppermute x20, starting transfers between devices, swap(): return lax.ppermute(value, axis, [(i, i ^ bit) for i in range(count)])  24.9 us
    ppermute x20, waiting for transfers between devices, swap(): return lax.ppermute(value, axis, [(i, i ^ bit) for i in range(count)])  21.7 us
    pallas_call x17, Pallas kernels, call(): pl.pallas_call(kernel, out_shape=[jax.ShapeDtypeStruct(s, d) for s, d in...  8.92 us
    unnamed x24, local copies, waits for them, and re-layouts  3.52 us
  transfers between devices with their start and end apart: 20, of which 13 were waited for; matrix products, arithmetic and copies ran while one was open for 0% of the time, Pallas kernels for 9%

profile of v3, /device:TPU:0, one launch (start us, length us, event | category | flops | bytes accessed | tf_op | source)
XLA Modules:
  0.0 60.7 jit_solution(9755207380785648810)
XLA Ops:
  0.7 0.6 %copy-done.6 = s32[1,64]{1,0:T(1,128)S(1)} copy-done((s32[1,64]{1,0:T(1,128)S(1)}, s32[1,64]{1,0:T(1,128)}, u32[]{:S(2)}) %copy-start.6) | copy-done | bytes 280
  1.3 1.0 %copy-done.1 = bf16[256,4096]{1,0:T(8,128)(2,1)S(1)} copy-done((bf16[256,4096]{1,0:T(8,128)(2,1)S(1)}, bf16[256,4096]{1,0:T(8,128)(2,1)}, u32[]{:S(2)}) %copy-start.1) | copy-done | bytes 2097176
  2.2 0.5 shard_map.124
  2.8 1.9 %copy-done = bf16[2048,2048]{1,0:T(8,128)(2,1)S(1)} copy-done((bf16[2048,2048]{1,0:T(8,128)(2,1)S(1)}, bf16[2048,2048]{1,0:T(8,128)(2,1)}, u32[]{:S(2)}) %copy-start) | copy-done | bytes 8388632
  4.7 0.6 collective-permute-start.2
  5.3 1.0 %collective-permute-done.2.other_ref = bf16[32,2048]{1,0:T(8,128)(2,1)S(1)} collective-permute-done((bf16[32,2048]{1,0:T(8,128)(2,1)S(1)}, bf16[32,2048]{1,0:T(8,128)(2,1)S(1)}, u32[]{:S(2)}, u32[]{:S(2)}) %collective-permute-start.2) | collective-permute-done | bytes 131104 | tf_op jit(solution)/shard_map/ppermute | solution.py:30
  6.3 4.5 %collective-permute-start.3 = (bf16[32,2048]{1,0:T(8,128)(2,1)S(1)}, bf16[32,2048]{1,0:T(8,128)(2,1)S(1)}, u32[]{:S(2)}, u32[]{:S(2)}) collective-permute-start(bf16[32,2048]{1,0:T(8,128)(2,1)S(1)} %get-tuple-element.36), channel_id=1, source_target_pairs={{0,2},{1,3},{2,0},{3,1},{4,6},{5,7},{6,4},{7,5},{8,10},{9,11},{10,... | collective-permute-start | bytes 393224 | tf_op jit(solution)/shard_map/ppermute | solution.py:30
  10.8 1.6 %collective-permute-start = (bf16[1,4096]{1,0:T(2,128)(2,1)S(1)}, bf16[1,4096]{1,0:T(2,128)(2,1)S(1)}, u32[]{:S(2)}, u32[]{:S(2)}) collective-permute-start(bf16[1,4096]{1,0:T(2,128)(2,1)S(1)} %copy-done.3), channel_id=1, source_target_pairs={{0,4},{4,0},{8,12},{12,8},{1,5},{5,1},{9,13},{13,9},{2,6},{6,2},{1... | collective-permute-start | bytes 24584 | tf_op jit(solution)/shard_map/ppermute | solution.py:30
  12.4 2.2 %collective-permute-done.other_ref = bf16[1,4096]{1,0:T(2,128)(2,1)S(1)} collective-permute-done((bf16[1,4096]{1,0:T(2,128)(2,1)S(1)}, bf16[1,4096]{1,0:T(2,128)(2,1)S(1)}, u32[]{:S(2)}, u32[]{:S(2)}) %collective-permute-start) | collective-permute-done | bytes 8224 | tf_op jit(solution)/shard_map/ppermute | solution.py:30
  14.6 2.7 %collective-permute-start.1 = (bf16[2,4096]{1,0:T(2,128)(2,1)S(1)}, bf16[2,4096]{1,0:T(2,128)(2,1)S(1)}, u32[]{:S(2)}, u32[]{:S(2)}) collective-permute-start(bf16[2,4096]{1,0:T(2,128)(2,1)S(1)} %shard_map.125.own_ref), channel_id=1, source_target_pairs={{0,8},{4,12},{8,0},{12,4},{1,9},{5,13},{9,1},{13,5},{2,10},{6,14},... | collective-permute-start | bytes 49160 | tf_op jit(solution)/shard_map/ppermute | solution.py:30
  17.3 0.1 collective-permute-start.4
  18.2 1.1 %collective-permute-done.1.other_ref = bf16[2,4096]{1,0:T(2,128)(2,1)S(1)} collective-permute-done((bf16[2,4096]{1,0:T(2,128)(2,1)S(1)}, bf16[2,4096]{1,0:T(2,128)(2,1)S(1)}, u32[]{:S(2)}, u32[]{:S(2)}) %collective-permute-start.1) | collective-permute-done | bytes 16416 | tf_op jit(solution)/shard_map/ppermute | solution.py:30
  19.3 1.3 %shard_map.126 = (bf16[64,2048]{1,0:T(8,128)(2,1)S(1)}, bf16[64,2048]{1,0:T(8,128)(2,1)S(1)}, f32[1,2048]{1,0:T(1,128)S(1)}) custom-call(s32[1,128]{1,0:T(1,128)S(1)} %shard_map.122.want_ref, bf16[2048,2048]{1,0:T(8,128)(2,1)S(1)} %copy-done, bf16[64,2048]{1,0:T(8,128)(2,1)S(1)} %get-tuple-element.29.pool_model_ref.rows_ref, ...), custom_call_target="tpu_custom_call" | custom-call | flops 536870912 | bytes 1090048 | tf_op jit(solution)/shard_map/pallas_call | solution.py:36
  20.7 0.0 copy-start.4
  20.7 2.5 %shard_map.132 = (f32[16,2176]{1,0:T(8,128)S(1)}, bf16[16,2176]{1,0:T(8,128)(2,1)S(1)}, bf16[16,2176]{1,0:T(8,128)(2,1)S(1)}, bf16[16,2176]{1,0:T(8,128)(2,1)S(1)}) custom-call(bf16[64,2048]{1,0:T(8,128)(2,1)S(1)} %get-tuple-element.31.cand_ref.base_ref, bf16[1,2048]{1,0:T(2,128)(2,1)S(1)} %reshape.21.score_ref, f32[1,2048]{1,0:T(1,128)S(1)} %bitcast.8, ...), custom_call_target="tpu_custom_call" | custom-call | flops 536870912 | bytes 622592 | tf_op jit(solution)/shard_map/pallas_call | solution.py:36
  23.2 1.6 %collective-permute-start.10 = (bf16[16,2176]{1,0:T(8,128)(2,1)S(1)}, bf16[16,2176]{1,0:T(8,128)(2,1)S(1)}, u32[]{:S(2)}, u32[]{:S(2)}) collective-permute-start(bf16[16,2176]{1,0:T(8,128)(2,1)S(1)} %get-tuple-element.45), channel_id=1, source_target_pairs={{0,4},{4,0},{8,12},{12,8},{1,5},{5,1},{9,13},{13,9},{2,6},{6,2},{1... | collective-permute-start | bytes 208904 | tf_op jit(solution)/shard_map/ppermute | solution.py:30
  24.8 0.0 collective-permute-start.5
  24.8 1.2 %collective-permute-done.5.refs_1_ = f32[1,2048]{1,0:T(1,128)S(1)} collective-permute-done((f32[1,2048]{1,0:T(1,128)S(1)}, f32[1,2048]{1,0:T(1,128)S(1)}, u32[]{:S(2)}, u32[]{:S(2)}) %collective-permute-start.5) | collective-permute-done | bytes 8224 | tf_op jit(solution)/shard_map/ppermute | solution.py:30
  25.9 0.0 collective-permute-start.6
  25.9 2.9 %collective-permute-start.11 = (bf16[16,2176]{1,0:T(8,128)(2,1)S(1)}, bf16[16,2176]{1,0:T(8,128)(2,1)S(1)}, u32[]{:S(2)}, u32[]{:S(2)}) collective-permute-start(bf16[16,2176]{1,0:T(8,128)(2,1)S(1)} %get-tuple-element.46), channel_id=1, source_target_pairs={{0,8},{4,12},{8,0},{12,4},{1,9},{5,13},{9,1},{13,5},{2,10},{6,14},... | collective-permute-start | bytes 208904 | tf_op jit(solution)/shard_map/ppermute | solution.py:30
  28.9 0.7 %collective-permute-done.6.user_other_ref = f32[1,2048]{1,0:T(1,128)S(1)} collective-permute-done((f32[1,2048]{1,0:T(1,128)S(1)}, f32[1,2048]{1,0:T(1,128)S(1)}, u32[]{:S(2)}, u32[]{:S(2)}) %collective-permute-start.6) | collective-permute-done | bytes 8224 | tf_op jit(solution)/shard_map/ppermute | solution.py:30
  29.6 0.0 collective-permute-done.4.other_ref
  29.6 1.7 %shard_map.131 = (f32[16,2048]{1,0:T(8,128)S(1)}, bf16[16,2048]{1,0:T(8,128)(2,1)S(1)}, bf16[16,2048]{1,0:T(8,128)(2,1)S(1)}, bf16[16,2048]{1,0:T(8,128)(2,1)S(1)}) custom-call(f32[32,2048]{1,0:T(8,128)S(1)} %get-tuple-element.37.mine_ref, bf16[32,2048]{1,0:T(8,128)(2,1)S(1)} %collective-permute-done.4.other_ref, f32[1,2048]{1,0:T(1,128)S(1)} %shard_map.130.user_ref, ...), custom_call_target="tpu_custom_call" | custom-call | flops 536870912 | bytes 1269760 | tf_op jit(solution)/shard_map/pallas_call | solution.py:36
  31.3 0.5 collective-permute-start.7
  31.9 3.1 %collective-permute-start.8 = (bf16[16,2048]{1,0:T(8,128)(2,1)S(1)}, bf16[16,2048]{1,0:T(8,128)(2,1)S(1)}, u32[]{:S(2)}, u32[]{:S(2)}) collective-permute-start(bf16[16,2048]{1,0:T(8,128)(2,1)S(1)} %get-tuple-element.42), channel_id=1, source_target_pairs={{0,8},{4,12},{8,0},{12,4},{1,9},{5,13},{9,1},{13,5},{2,10},{6,14},... | collective-permute-start | bytes 196616 | tf_op jit(solution)/shard_map/ppermute | solution.py:30
  35.0 0.0 collective-permute-done.10.refs_5_
  35.0 0.8 %collective-permute-start.9 = (bf16[16,2048]{1,0:T(8,128)(2,1)S(1)}, bf16[16,2048]{1,0:T(8,128)(2,1)S(1)}, u32[]{:S(2)}, u32[]{:S(2)}) collective-permute-start(bf16[16,2048]{1,0:T(8,128)(2,1)S(1)} %get-tuple-element.43), channel_id=1, source_target_pairs={{0,12},{4,8},{8,4},{12,0},{1,13},{5,9},{9,5},{13,1},{2,14},{6,10},... | collective-permute-start | bytes 196616 | tf_op jit(solution)/shard_map/ppermute | solution.py:30
  35.8 0.0 collective-permute-done.11.refs_6_
  35.8 0.0 collective-permute-done.12.refs_7_
  35.8 0.6 collective-permute-done.7.refs_1_
  36.4 3.3 %collective-permute-done.8.refs_2_ = bf16[16,2048]{1,0:T(8,128)(2,1)S(1)} collective-permute-done((bf16[16,2048]{1,0:T(8,128)(2,1)S(1)}, bf16[16,2048]{1,0:T(8,128)(2,1)S(1)}, u32[]{:S(2)}, u32[]{:S(2)}) %collective-permute-start.8) | collective-permute-done | bytes 65568 | tf_op jit(solution)/shard_map/ppermute | solution.py:30
  39.6 1.6 %collective-permute-done.9.refs_3_ = bf16[16,2048]{1,0:T(8,128)(2,1)S(1)} collective-permute-done((bf16[16,2048]{1,0:T(8,128)(2,1)S(1)}, bf16[16,2048]{1,0:T(8,128)(2,1)S(1)}, u32[]{:S(2)}, u32[]{:S(2)}) %collective-permute-start.9) | collective-permute-done | bytes 65568 | tf_op jit(solution)/shard_map/ppermute | solution.py:30
  41.2 0.2 shard_map.133.refs_0_
  41.4 0.8 %collective-permute-start.13 = (bf16[16,2176]{1,0:T(8,128)(2,1)S(1)}, bf16[16,2176]{1,0:T(8,128)(2,1)S(1)}, u32[]{:S(2)}, u32[]{:S(2)}) collective-permute-start(bf16[16,2176]{1,0:T(8,128)(2,1)S(1)} %shard_map.133.refs_0_), channel_id=1, source_target_pairs={{0,4},{4,0},{8,12},{12,8},{1,5},{5,1},{9,13},{13,9},{2,6},{6,2},{1... | collective-permute-start | bytes 208904 | tf_op jit(solution)/shard_map/ppermute | solution.py:30
  42.2 1.7 %collective-permute-start.14 = (bf16[16,2176]{1,0:T(8,128)(2,1)S(1)}, bf16[16,2176]{1,0:T(8,128)(2,1)S(1)}, u32[]{:S(2)}, u32[]{:S(2)}) collective-permute-start(bf16[16,2176]{1,0:T(8,128)(2,1)S(1)} %shard_map.133.refs_0_), channel_id=1, source_target_pairs={{0,8},{4,12},{8,0},{12,4},{1,9},{5,13},{9,1},{13,5},{2,10},{6,14},... | collective-permute-start | bytes 208904 | tf_op jit(solution)/shard_map/ppermute | solution.py:30
  43.8 2.0 %collective-permute-start.15 = (bf16[16,2176]{1,0:T(8,128)(2,1)S(1)}, bf16[16,2176]{1,0:T(8,128)(2,1)S(1)}, u32[]{:S(2)}, u32[]{:S(2)}) collective-permute-start(bf16[16,2176]{1,0:T(8,128)(2,1)S(1)} %shard_map.133.refs_0_), channel_id=1, source_target_pairs={{0,12},{4,8},{8,4},{12,0},{1,13},{5,9},{9,5},{13,1},{2,14},{6,10},... | collective-permute-start | bytes 208904 | tf_op jit(solution)/shard_map/ppermute | solution.py:30
  45.8 0.1 collective-permute-done.13.refs_1_
  45.9 4.2 %collective-permute-done.14.refs_2_ = bf16[16,2176]{1,0:T(8,128)(2,1)S(1)} collective-permute-done((bf16[16,2176]{1,0:T(8,128)(2,1)S(1)}, bf16[16,2176]{1,0:T(8,128)(2,1)S(1)}, u32[]{:S(2)}, u32[]{:S(2)}) %collective-permute-start.14) | collective-permute-done | bytes 69664 | tf_op jit(solution)/shard_map/ppermute | solution.py:30
  50.2 0.0 collective-permute-done.15.refs_3_
  50.2 0.1 shard_map.134
  50.3 1.7 %shard_map.135 = (f32[32,2048]{1,0:T(8,128)S(1)}, bf16[32,2048]{1,0:T(8,128)(2,1)S(1)}) custom-call(bf16[64,2048]{1,0:T(8,128)(2,1)S(1)} %get-tuple-element.31.cand_ref.base_ref, bf16[2048,2048]{1,0:T(8,128)(2,1)S(1)} %bitcast.5, bf16[64,2048]{1,0:T(8,128)(2,1)S(1)} %get-tuple-element.48.rows_ref), custom_call_target="tpu_custom_call" | custom-call | flops 536870912 | bytes 917504 | tf_op jit(solution)/shard_map/pallas_call | solution.py:36
  52.0 0.1 collective-permute-start.16
  52.1 1.3 %collective-permute-done.16.other_ref = bf16[32,2048]{1,0:T(8,128)(2,1)S(1)} collective-permute-done((bf16[32,2048]{1,0:T(8,128)(2,1)S(1)}, bf16[32,2048]{1,0:T(8,128)(2,1)S(1)}, u32[]{:S(2)}, u32[]{:S(2)}) %collective-permute-start.16) | collective-permute-done | bytes 131104 | tf_op jit(solution)/shard_map/ppermute | solution.py:30
  53.4 1.8 %collective-permute-start.17 = (bf16[16,2048]{1,0:T(8,128)(2,1)S(1)}, bf16[16,2048]{1,0:T(8,128)(2,1)S(1)}, u32[]{:S(2)}, u32[]{:S(2)}) collective-permute-start(bf16[16,2048]{1,0:T(8,128)(2,1)S(1)} %get-tuple-element.52), channel_id=1, source_target_pairs={{0,2},{1,3},{2,0},{3,1},{4,6},{5,7},{6,4},{7,5},{8,10},{9,11},{10,... | collective-permute-start | bytes 196616 | tf_op jit(solution)/shard_map/ppermute | solution.py:30
  55.2 1.2 %collective-permute-done.18.refs_1_ = f32[4,16]{1,0:T(4,128)S(1)} collective-permute-done((f32[4,16]{1,0:T(4,128)S(1)}, f32[4,16]{1,0:T(4,128)S(1)}, u32[]{:S(2)}, u32[]{:S(2)}) %collective-permute-start.18) | collective-permute-done | bytes 288 | tf_op jit(solution)/shard_map/ppermute | solution.py:30
  56.4 0.3 collective-permute-start.19
  56.7 3.3 %collective-permute-done.19.part_ref = f32[4,16]{1,0:T(4,128)S(1)} collective-permute-done((f32[4,16]{1,0:T(4,128)S(1)}, f32[4,16]{1,0:T(4,128)S(1)}, u32[]{:S(2)}, u32[]{:S(2)}) %collective-permute-start.19) | collective-permute-done | bytes 288 | tf_op jit(solution)/shard_map/ppermute | solution.py:30
  60.0 0.7 %shard_map.138 = (bf16[16,2048]{1,0:T(8,128)(2,1)}, f32[1,16]{1,0:T(1,128)}) custom-call(f32[16,2048]{1,0:T(8,128)S(1)} %get-tuple-element.51.keep_ref, bf16[16,2048]{1,0:T(8,128)(2,1)S(1)} %collective-permute-done.17.other_ref, bf16[64,2048]{1,0:T(8,128)(2,1)S(1)} %get-tuple-element.31.cand_ref.base_ref, f32[1,2048]{1,0:T(1,128)S(1)} %bitcast.9, ...), custom_call_target="tpu_custom_call" | custom-call | bytes 533056 | tf_op jit(solution)/shard_map/pallas_call | solution.py:36
  (36 shorter events, 0.2 us)
Async XLA Ops:
  0.6 0.7 %copy-start.6 = (s32[1,64]{1,0:T(1,128)S(1)}, s32[1,64]{1,0:T(1,128)}, u32[]{:S(2)}) copy-start(s32[1,64]{1,0:T(1,128)} %ids_ref.1) | copy-start | bytes 772
  0.6 1.6 %copy-start.1 = (bf16[256,4096]{1,0:T(8,128)(2,1)S(1)}, bf16[256,4096]{1,0:T(8,128)(2,1)}, u32[]{:S(2)}) copy-start(bf16[256,4096]{1,0:T(8,128)(2,1)} %pool_ref.1) | copy-start | bytes 6291460
  0.7 4.0 %copy-start = (bf16[2048,2048]{1,0:T(8,128)(2,1)S(1)}, bf16[2048,2048]{1,0:T(8,128)(2,1)}, u32[]{:S(2)}) copy-start(bf16[2048,2048]{1,0:T(8,128)(2,1)} %weight_ref.6) | copy-start | bytes 25165828
  2.2 8.6 %copy-start.3 = (bf16[1,4096]{1,0:T(2,128)(2,1)S(1)}, bf16[1,4096]{1,0:T(2,128)(2,1)}, u32[]{:S(2)}) copy-start(bf16[1,4096]{1,0:T(2,128)(2,1)} %own_ref.1) | copy-start | bytes 24580
  2.2 15.9 %copy-start.7 = (bf16[2048]{0:T(1024)(128)(2,1)S(1)}, bf16[2048]{0:T(1024)(128)(2,1)}, u32[]{:S(2)}) copy-start(bf16[2048]{0:T(1024)(128)(2,1)} %param.21) | copy-start | bytes 12292
  4.7 16.0 %slice-start = ((s8[8388608]{0:T(1024)(128)(4,1)}), s8[4194304]{0:T(1024)(128)(4,1)S(1)}, s32[]{:S(2)}) async-start(s8[8388608]{0:T(1024)(128)(4,1)} %bitcast.4), calls=%async_computation | async-start | bytes 8388608
  4.7 16.0 %copy-start.2 = (f32[2048]{0:T(1024)S(1)}, f32[2048]{0:T(1024)}, u32[]{:S(2)}) copy-start(f32[2048]{0:T(1024)} %param.20) | copy-start | bytes 24580
  4.7 24.9 %slice-start.2 = ((s8[8388608]{0:T(1024)(128)(4,1)}), s8[4194304]{0:T(1024)(128)(4,1)S(1)}, s32[]{:S(2)}) async-start(s8[8388608]{0:T(1024)(128)(4,1)} %bitcast.6), calls=%async_computation.2 | async-start | bytes 8388608
  4.7 1.5 %collective-permute-start.2 = (bf16[32,2048]{1,0:T(8,128)(2,1)S(1)}, bf16[32,2048]{1,0:T(8,128)(2,1)S(1)}, u32[]{:S(2)}, u32[]{:S(2)}) collective-permute-start(bf16[32,2048]{1,0:T(8,128)(2,1)S(1)} %get-tuple-element.34), channel_id=1, source_target_pairs={{0,1},{1,0},{2,3},{3,2},{4,5},{5,4},{6,7},{7,6},{8,9},{9,8},{10,11... | collective-permute-start | bytes 393224 | tf_op jit(solution)/shard_map/ppermute | solution.py:30
  6.3 10.9 %collective-permute-start.3 = (bf16[32,2048]{1,0:T(8,128)(2,1)S(1)}, bf16[32,2048]{1,0:T(8,128)(2,1)S(1)}, u32[]{:S(2)}, u32[]{:S(2)}) collective-permute-start(bf16[32,2048]{1,0:T(8,128)(2,1)S(1)} %get-tuple-element.36), channel_id=1, source_target_pairs={{0,2},{1,3},{2,0},{3,1},{4,6},{5,7},{6,4},{7,5},{8,10},{9,11},{10,... | collective-permute-start | bytes 393224 | tf_op jit(solution)/shard_map/ppermute | solution.py:30
  10.8 3.7 %collective-permute-start = (bf16[1,4096]{1,0:T(2,128)(2,1)S(1)}, bf16[1,4096]{1,0:T(2,128)(2,1)S(1)}, u32[]{:S(2)}, u32[]{:S(2)}) collective-permute-start(bf16[1,4096]{1,0:T(2,128)(2,1)S(1)} %copy-done.3), channel_id=1, source_target_pairs={{0,4},{4,0},{8,12},{12,8},{1,5},{5,1},{9,13},{13,9},{2,6},{6,2},{1... | collective-permute-start | bytes 24584 | tf_op jit(solution)/shard_map/ppermute | solution.py:30
  14.6 4.7 %collective-permute-start.1 = (bf16[2,4096]{1,0:T(2,128)(2,1)S(1)}, bf16[2,4096]{1,0:T(2,128)(2,1)S(1)}, u32[]{:S(2)}, u32[]{:S(2)}) collective-permute-start(bf16[2,4096]{1,0:T(2,128)(2,1)S(1)} %shard_map.125.own_ref), channel_id=1, source_target_pairs={{0,8},{4,12},{8,0},{12,4},{1,9},{5,13},{9,1},{13,5},{2,10},{6,14},... | collective-permute-start | bytes 49160 | tf_op jit(solution)/shard_map/ppermute | solution.py:30
  17.2 3.4 %slice-start.1 = ((s8[8388608]{0:T(1024)(128)(4,1)}), s8[4194304]{0:T(1024)(128)(4,1)S(1)}, s32[]{:S(2)}) async-start(s8[8388608]{0:T(1024)(128)(4,1)} %bitcast.4), calls=%async_computation.1 | async-start | bytes 8388608
  17.3 12.3 %collective-permute-start.4 = (bf16[32,2048]{1,0:T(8,128)(2,1)S(1)}, bf16[32,2048]{1,0:T(8,128)(2,1)S(1)}, u32[]{:S(2)}, u32[]{:S(2)}) collective-permute-start(bf16[32,2048]{1,0:T(8,128)(2,1)S(1)} %get-tuple-element.38), channel_id=1, source_target_pairs={{0,1},{1,0},{2,3},{3,2},{4,5},{5,4},{6,7},{7,6},{8,9},{9,8},{10,11... | collective-permute-start | bytes 393224 | tf_op jit(solution)/shard_map/ppermute | solution.py:30
  19.3 10.3 %slice-start.3 = ((s8[8388608]{0:T(1024)(128)(4,1)}), s8[4194304]{0:T(1024)(128)(4,1)S(1)}, s32[]{:S(2)}) async-start(s8[8388608]{0:T(1024)(128)(4,1)} %bitcast.6), calls=%async_computation.3 | async-start | bytes 8388608
  19.3 10.3 %copy-start.5 = (f32[2048]{0:T(1024)S(1)}, f32[2048]{0:T(1024)}, u32[]{:S(2)}) copy-start(f32[2048]{0:T(1024)} %param.16) | copy-start | bytes 24580
  20.7 20.5 %copy-start.4 = (f32[2048]{0:T(1024)S(1)}, f32[2048]{0:T(1024)}, u32[]{:S(2)}) copy-start(f32[2048]{0:T(1024)} %param.18) | copy-start | bytes 24580
  23.2 11.8 %collective-permute-start.10 = (bf16[16,2176]{1,0:T(8,128)(2,1)S(1)}, bf16[16,2176]{1,0:T(8,128)(2,1)S(1)}, u32[]{:S(2)}, u32[]{:S(2)}) collective-permute-start(bf16[16,2176]{1,0:T(8,128)(2,1)S(1)} %get-tuple-element.45), channel_id=1, source_target_pairs={{0,4},{4,0},{8,12},{12,8},{1,5},{5,1},{9,13},{13,9},{2,6},{6,2},{1... | collective-permute-start | bytes 208904 | tf_op jit(solution)/shard_map/ppermute | solution.py:30
  24.8 1.2 %collective-permute-start.5 = (f32[1,2048]{1,0:T(1,128)S(1)}, f32[1,2048]{1,0:T(1,128)S(1)}, u32[]{:S(2)}, u32[]{:S(2)}) collective-permute-start(f32[1,2048]{1,0:T(1,128)S(1)} %get-tuple-element.39.refs_0_), channel_id=1, source_target_pairs={{0,1},{1,0},{2,3},{3,2},{4,5},{5,4},{6,7},{7,6},{8,9},{9,8},{10,11... | collective-permute-start | bytes 24584 | tf_op jit(solution)/shard_map/ppermute | solution.py:30
  25.9 3.7 %collective-permute-start.6 = (f32[1,2048]{1,0:T(1,128)S(1)}, f32[1,2048]{1,0:T(1,128)S(1)}, u32[]{:S(2)}, u32[]{:S(2)}) collective-permute-start(f32[1,2048]{1,0:T(1,128)S(1)} %shard_map.130.user_ref), channel_id=1, source_target_pairs={{0,2},{1,3},{2,0},{3,1},{4,6},{5,7},{6,4},{7,5},{8,10},{9,11},{10,... | collective-permute-start | bytes 24584 | tf_op jit(solution)/shard_map/ppermute | solution.py:30
  25.9 9.8 %collective-permute-start.11 = (bf16[16,2176]{1,0:T(8,128)(2,1)S(1)}, bf16[16,2176]{1,0:T(8,128)(2,1)S(1)}, u32[]{:S(2)}, u32[]{:S(2)}) collective-permute-start(bf16[16,2176]{1,0:T(8,128)(2,1)S(1)} %get-tuple-element.46), channel_id=1, source_target_pairs={{0,8},{4,12},{8,0},{12,4},{1,9},{5,13},{9,1},{13,5},{2,10},{6,14},... | collective-permute-start | bytes 208904 | tf_op jit(solution)/shard_map/ppermute | solution.py:30
  28.8 6.9 %collective-permute-start.12 = (bf16[16,2176]{1,0:T(8,128)(2,1)S(1)}, bf16[16,2176]{1,0:T(8,128)(2,1)S(1)}, u32[]{:S(2)}, u32[]{:S(2)}) collective-permute-start(bf16[16,2176]{1,0:T(8,128)(2,1)S(1)} %get-tuple-element.47), channel_id=1, source_target_pairs={{0,12},{4,8},{8,4},{12,0},{1,13},{5,9},{9,5},{13,1},{2,14},{6,10},... | collective-permute-start | bytes 208904 | tf_op jit(solution)/shard_map/ppermute | solution.py:30
  31.3 5.0 %collective-permute-start.7 = (bf16[16,2048]{1,0:T(8,128)(2,1)S(1)}, bf16[16,2048]{1,0:T(8,128)(2,1)S(1)}, u32[]{:S(2)}, u32[]{:S(2)}) collective-permute-start(bf16[16,2048]{1,0:T(8,128)(2,1)S(1)} %get-tuple-element.41), channel_id=1, source_target_pairs={{0,4},{4,0},{8,12},{12,8},{1,5},{5,1},{9,13},{13,9},{2,6},{6,2},{1... | collective-permute-start | bytes 196616 | tf_op jit(solution)/shard_map/ppermute | solution.py:30
  31.9 7.8 %collective-permute-start.8 = (bf16[16,2048]{1,0:T(8,128)(2,1)S(1)}, bf16[16,2048]{1,0:T(8,128)(2,1)S(1)}, u32[]{:S(2)}, u32[]{:S(2)}) collective-permute-start(bf16[16,2048]{1,0:T(8,128)(2,1)S(1)} %get-tuple-element.42), channel_id=1, source_target_pairs={{0,8},{4,12},{8,0},{12,4},{1,9},{5,13},{9,1},{13,5},{2,10},{6,14},... | collective-permute-start | bytes 196616 | tf_op jit(solution)/shard_map/ppermute | solution.py:30
  35.0 6.2 %collective-permute-start.9 = (bf16[16,2048]{1,0:T(8,128)(2,1)S(1)}, bf16[16,2048]{1,0:T(8,128)(2,1)S(1)}, u32[]{:S(2)}, u32[]{:S(2)}) collective-permute-start(bf16[16,2048]{1,0:T(8,128)(2,1)S(1)} %get-tuple-element.43), channel_id=1, source_target_pairs={{0,12},{4,8},{8,4},{12,0},{1,13},{5,9},{9,5},{13,1},{2,14},{6,10},... | collective-permute-start | bytes 196616 | tf_op jit(solution)/shard_map/ppermute | solution.py:30
  41.4 4.5 %collective-permute-start.13 = (bf16[16,2176]{1,0:T(8,128)(2,1)S(1)}, bf16[16,2176]{1,0:T(8,128)(2,1)S(1)}, u32[]{:S(2)}, u32[]{:S(2)}) collective-permute-start(bf16[16,2176]{1,0:T(8,128)(2,1)S(1)} %shard_map.133.refs_0_), channel_id=1, source_target_pairs={{0,4},{4,0},{8,12},{12,8},{1,5},{5,1},{9,13},{13,9},{2,6},{6,2},{1... | collective-permute-start | bytes 208904 | tf_op jit(solution)/shard_map/ppermute | solution.py:30
  42.2 8.0 %collective-permute-start.14 = (bf16[16,2176]{1,0:T(8,128)(2,1)S(1)}, bf16[16,2176]{1,0:T(8,128)(2,1)S(1)}, u32[]{:S(2)}, u32[]{:S(2)}) collective-permute-start(bf16[16,2176]{1,0:T(8,128)(2,1)S(1)} %shard_map.133.refs_0_), channel_id=1, source_target_pairs={{0,8},{4,12},{8,0},{12,4},{1,9},{5,13},{9,1},{13,5},{2,10},{6,14},... | collective-permute-start | bytes 208904 | tf_op jit(solution)/shard_map/ppermute | solution.py:30
  43.8 6.3 %collective-permute-start.15 = (bf16[16,2176]{1,0:T(8,128)(2,1)S(1)}, bf16[16,2176]{1,0:T(8,128)(2,1)S(1)}, u32[]{:S(2)}, u32[]{:S(2)}) collective-permute-start(bf16[16,2176]{1,0:T(8,128)(2,1)S(1)} %shard_map.133.refs_0_), channel_id=1, source_target_pairs={{0,12},{4,8},{8,4},{12,0},{1,13},{5,9},{9,5},{13,1},{2,14},{6,10},... | collective-permute-start | bytes 208904 | tf_op jit(solution)/shard_map/ppermute | solution.py:30
  52.0 1.4 %collective-permute-start.16 = (bf16[32,2048]{1,0:T(8,128)(2,1)S(1)}, bf16[32,2048]{1,0:T(8,128)(2,1)S(1)}, u32[]{:S(2)}, u32[]{:S(2)}) collective-permute-start(bf16[32,2048]{1,0:T(8,128)(2,1)S(1)} %get-tuple-element.50), channel_id=1, source_target_pairs={{0,1},{1,0},{2,3},{3,2},{4,5},{5,4},{6,7},{7,6},{8,9},{9,8},{10,11... | collective-permute-start | bytes 393224 | tf_op jit(solution)/shard_map/ppermute | solution.py:30
  53.4 6.5 %collective-permute-start.17 = (bf16[16,2048]{1,0:T(8,128)(2,1)S(1)}, bf16[16,2048]{1,0:T(8,128)(2,1)S(1)}, u32[]{:S(2)}, u32[]{:S(2)}) collective-permute-start(bf16[16,2048]{1,0:T(8,128)(2,1)S(1)} %get-tuple-element.52), channel_id=1, source_target_pairs={{0,2},{1,3},{2,0},{3,1},{4,6},{5,7},{6,4},{7,5},{8,10},{9,11},{10,... | collective-permute-start | bytes 196616 | tf_op jit(solution)/shard_map/ppermute | solution.py:30
  55.2 1.2 %collective-permute-start.18 = (f32[4,16]{1,0:T(4,128)S(1)}, f32[4,16]{1,0:T(4,128)S(1)}, u32[]{:S(2)}, u32[]{:S(2)}) collective-permute-start(f32[4,16]{1,0:T(4,128)S(1)} %get-tuple-element.53.refs_0_), channel_id=1, source_target_pairs={{0,1},{1,0},{2,3},{3,2},{4,5},{5,4},{6,7},{7,6},{8,9},{9,8},{10,11... | collective-permute-start | bytes 776 | tf_op jit(solution)/shard_map/ppermute | solution.py:30
  56.4 3.6 %collective-permute-start.19 = (f32[4,16]{1,0:T(4,128)S(1)}, f32[4,16]{1,0:T(4,128)S(1)}, u32[]{:S(2)}, u32[]{:S(2)}) collective-permute-start(f32[4,16]{1,0:T(4,128)S(1)} %shard_map.137.total_ref), channel_id=1, source_target_pairs={{0,2},{1,3},{2,0},{3,1},{4,6},{5,7},{6,4},{7,5},{8,10},{9,11},{10,... | collective-permute-start | bytes 776 | tf_op jit(solution)/shard_map/ppermute | solution.py:30

commit v4 on v2

--- a/solution.py
+++ b/solution.py
@@ -169,6 +169,20 @@
     send_ref[...] = total.astype(BF16)
 
 
+def merge(keep_ref, other_ref, user_ref, user_other_ref, sum_ref, send_ref, users_ref):
+    low = lax.axis_index("mp") % 2
+    size, users = keep_ref.shape[0], user_ref.shape[0]
+    assert users == 1 or users % 2 == 0
+    users_ref[...] = user_ref[...] + user_other_ref[...]
+    each = max(users // 2, 1)
+    for piece in range(each):
+        user = low * each + piece if users > 1 else 0
+        part = pl.ds(piece * (size // each), size // each)
+        total = keep_ref[part, :] + other_ref[part, :].astype(F32) + users_ref[pl.ds(user, 1), :]
+        sum_ref[part, :] = total
+        send_ref[part, :] = total.astype(BF16)
+
+
 def add_own_columns(terms_ref, rows_ref, have, want):
     width, wanted = rows_ref.shape[1], terms_ref.shape[1]
     small = min(width, wanted)
@@ -184,24 +198,15 @@
         terms_ref[:, there] += rows_ref[:, here].astype(F32)
 
 
-def layer_two(
-    mine_ref, other_ref, user_ref, user_other_ref, bias_ref, cand_ref, base_ref, weight_ref, *refs
-):
-    *out_refs, rows_ref, terms_ref, user_sum_ref = refs
+def layer_two(mine_ref, other_ref, bias_ref, cand_ref, base_ref, weight_ref, *refs):
+    *out_refs, rows_ref, terms_ref = refs
     low = lax.axis_index("mp") % 2
     size = mine_ref.shape[0]
-    users = user_ref.shape[0]
-    assert users == 1 or users % 2 == 0
-    user_sum_ref[...] = user_ref[...] + user_other_ref[...] + bias_ref[...]
-    each = max(users // 2, 1)
-    for index, pool_ref in ((low, mine_ref), (1 - low, other_ref)):
-        for piece in range(each):
-            user = index * each + piece if users > 1 else 0
-            part = pl.ds(piece * (size // each), size // each)
-            here = aligned(index * each + piece, size // each)
-            base = cand_ref[here, :].astype(F32)
-            total = pool_ref[part, :].astype(F32) + user_sum_ref[pl.ds(user, 1), :]
-            rows_ref[here, :] = (base * total + base).astype(BF16)
+    for index, sum_ref in ((low, mine_ref), (1 - low, other_ref)):
+        here = aligned(index, size)
+        base = cand_ref[here, :].astype(F32)
+        total = sum_ref[...].astype(F32) + bias_ref[...]
+        rows_ref[here, :] = (base * total + base).astype(BF16)
     multiply(rows_ref, weight_ref, terms_ref, base_ref)
     cand = lax.axis_index("cand")
     add_own_columns(terms_ref, rows_ref, cand, lax.axis_index("mp"))
@@ -410,10 +415,6 @@
         flops=flops,
         limit=12 * MIB,
     )
-    for bit in bits_of(model_count):
-        keep, send = call(add_up, half_outs, [keep, swap(send, "mp", bit)])
-    pool_other = swap(send, "mp", 1)
-
     base_model, base_cand, user_sum = call(
         functools.partial(user_terms, half_width),
         [
@@ -426,10 +427,24 @@
         limit=12 * MIB,
     )
     *bits, last_bit = bits_of(model_count)
+    assert bits
     for bit in bits:
-        other = swap(user_sum, "mp", bit)
-        (user_sum,) = call(add_to, [((user_count, col_block), F32)], [user_sum, other])
-    user_other = swap(user_sum, "mp", last_bit)
+        other = swap(send, "mp", bit)
+        user_other = swap(user_sum, "mp", bit)
+        if bit == bits[-1]:
+            keep, send = call(
+                merge,
+                half_outs,
+                [keep, other, user_sum, user_other],
+                scratch=[pltpu.VMEM((user_count, col_block), F32)],
+            )
+        else:
+            keep, send = call(add_up, half_outs, [keep, other])
+            (user_sum,) = call(
+                add_to, [((user_count, col_block), F32)], [user_sum, user_other]
+            )
+    keep, send = call(add_up, half_outs, [keep, swap(send, "mp", last_bit)])
+    pool_other = swap(send, "mp", 1)
 
     if direct:
         outs = [
@@ -455,13 +470,11 @@
         layer_two,
         outs,
         [
-            keep, pool_other, user_sum, user_other, first_bias.reshape(1, -1), base_cand,
-            base_model, second_weight,
+            keep, pool_other, first_bias.reshape(1, -1), base_cand, base_model, second_weight,
         ],
         scratch=[
             pltpu.VMEM((row_total, col_block), BF16),
             pltpu.VMEM((row_total, feat_block), F32),
-            pltpu.VMEM((user_count, col_block), F32),
         ],
         flops=flops,
         limit=12 * MIB,

time: 64.3 us -> 62.1 us (0.966)
  starting transfers between devices: 25.5 us -> 23.3 us
    ppermute x21 -> x20, starting transfers between devices: 25.5 us -> 23.3 us  [swap(): return lax.ppermute(value, axis, [(i, i ^ bit) for i in range(count)])]
    ppermute x21 -> x20, waiting for transfers between devices: 24.7 us -> 24.6 us  [swap(): return lax.ppermute(value, axis, [(i, i ^ bit) for i in range(count)])]
    pallas_call x16 -> x15, Pallas kernels: 8.9 us -> 8.91 us  [call(): pl.pallas_call(kernel, out_shape=[jax.ShapeDtypeStruct(s, d) for s, d in...]
  transfers between devices with their start and end apart: 21 -> 20, of which waited for: 13 -> 10; matrix products, arithmetic and copies ran while one was open for 0% -> 0% of each run, Pallas kernels for 9% -> 9%
where the time goes in v4:
time: 62.1 us; the launch traced here: 61.9 us
  waiting for transfers between devices  24.6 us (40%)
  starting transfers between devices  23.3 us (38%)
  Pallas kernels  8.91 us (14%)
  local copies, waits for them, and re-layouts  3.53 us (6%)
  between operations  1.52 us (2%)
    ppermute x20, waiting for transfers between devices, swap(): return lax.ppermute(value, axis, [(i, i ^ bit) for i in range(count)])  24.6 us
    ppermute x20, starting transfers between devices, swap(): return lax.ppermute(value, axis, [(i, i ^ bit) for i in range(count)])  23.3 us
    pallas_call x15, Pallas kernels, call(): pl.pallas_call(kernel, out_shape=[jax.ShapeDtypeStruct(s, d) for s, d in...  8.91 us
    unnamed x24, local copies, waits for them, and re-layouts  3.52 us
  transfers between devices with their start and end apart: 20, of which 10 were waited for; matrix products, arithmetic and copies ran while one was open for 0% of the time, Pallas kernels for 9%

profile of v4, /device:TPU:0, one launch (start us, length us, event | category | flops | bytes accessed | tf_op | source)
XLA Modules:
  0.0 61.9 jit_solution(13385289959048045009)
XLA Ops:
  0.7 0.6 copy-done.6
  1.3 1.0 %copy-done.1 = bf16[256,4096]{1,0:T(8,128)(2,1)S(1)} copy-done((bf16[256,4096]{1,0:T(8,128)(2,1)S(1)}, bf16[256,4096]{1,0:T(8,128)(2,1)}, u32[]{:S(2)}) %copy-start.1) | copy-done | bytes 2097176
  2.2 0.5 shard_map.124
  2.8 1.9 %copy-done = bf16[2048,2048]{1,0:T(8,128)(2,1)S(1)} copy-done((bf16[2048,2048]{1,0:T(8,128)(2,1)S(1)}, bf16[2048,2048]{1,0:T(8,128)(2,1)}, u32[]{:S(2)}) %copy-start) | copy-done | bytes 8388632
  4.7 0.6 collective-permute-start.3
  5.3 2.6 %collective-permute-start = (bf16[1,4096]{1,0:T(2,128)(2,1)S(1)}, bf16[1,4096]{1,0:T(2,128)(2,1)S(1)}, u32[]{:S(2)}, u32[]{:S(2)}) collective-permute-start(bf16[1,4096]{1,0:T(2,128)(2,1)S(1)} %copy-done.3), channel_id=1, source_target_pairs={{0,4},{4,0},{8,12},{12,8},{1,5},{5,1},{9,13},{13,9},{2,6},{6,2},{1... | collective-permute-start | bytes 24584 | tf_op jit(solution)/shard_map/ppermute | solution.py:30
  7.9 2.6 %collective-permute-start.1 = (bf16[1,4096]{1,0:T(2,128)(2,1)S(1)}, bf16[1,4096]{1,0:T(2,128)(2,1)S(1)}, u32[]{:S(2)}, u32[]{:S(2)}) collective-permute-start(bf16[1,4096]{1,0:T(2,128)(2,1)S(1)} %copy-done.3), channel_id=1, source_target_pairs={{0,8},{4,12},{8,0},{12,4},{1,9},{5,13},{9,1},{13,5},{2,10},{6,14},... | collective-permute-start | bytes 24584 | tf_op jit(solution)/shard_map/ppermute | solution.py:30
  10.5 0.0 collective-permute-start.2
  11.2 0.0 collective-permute-done.refs_1_
  11.2 1.4 %collective-permute-done.1.refs_2_ = bf16[1,4096]{1,0:T(2,128)(2,1)S(1)} collective-permute-done((bf16[1,4096]{1,0:T(2,128)(2,1)S(1)}, bf16[1,4096]{1,0:T(2,128)(2,1)S(1)}, u32[]{:S(2)}, u32[]{:S(2)}) %collective-permute-start.1) | collective-permute-done | bytes 8224 | tf_op jit(solution)/shard_map/ppermute | solution.py:30
  12.6 3.5 %collective-permute-done.2.refs_3_ = bf16[1,4096]{1,0:T(2,128)(2,1)S(1)} collective-permute-done((bf16[1,4096]{1,0:T(2,128)(2,1)S(1)}, bf16[1,4096]{1,0:T(2,128)(2,1)S(1)}, u32[]{:S(2)}, u32[]{:S(2)}) %collective-permute-start.2) | collective-permute-done | bytes 8224 | tf_op jit(solution)/shard_map/ppermute | solution.py:30
  16.1 1.3 %shard_map.125 = (bf16[64,2048]{1,0:T(8,128)(2,1)S(1)}, bf16[64,2048]{1,0:T(8,128)(2,1)S(1)}, f32[1,2048]{1,0:T(1,128)S(1)}) custom-call(s32[1,128]{1,0:T(1,128)S(1)} %shard_map.122.want_ref, bf16[2048,2048]{1,0:T(8,128)(2,1)S(1)} %copy-done, bf16[64,2048]{1,0:T(8,128)(2,1)S(1)} %get-tuple-element.29.pool_model_ref.rows_ref, ...), custom_call_target="tpu_custom_call" | custom-call | flops 536870912 | bytes 1090048 | tf_op jit(solution)/shard_map/pallas_call | solution.py:36
  17.4 0.1 collective-permute-start.4
  17.5 1.2 %collective-permute-done.4.user_other_ref = f32[1,2048]{1,0:T(1,128)S(1)} collective-permute-done((f32[1,2048]{1,0:T(1,128)S(1)}, f32[1,2048]{1,0:T(1,128)S(1)}, u32[]{:S(2)}, u32[]{:S(2)}) %collective-permute-start.4) | collective-permute-done | bytes 8224 | tf_op jit(solution)/shard_map/ppermute | solution.py:30
  18.7 0.0 collective-permute-done.3.other_ref
  18.7 1.9 %collective-permute-start.5 = (bf16[32,2048]{1,0:T(8,128)(2,1)S(1)}, bf16[32,2048]{1,0:T(8,128)(2,1)S(1)}, u32[]{:S(2)}, u32[]{:S(2)}) collective-permute-start(bf16[32,2048]{1,0:T(8,128)(2,1)S(1)} %get-tuple-element.37), channel_id=1, source_target_pairs={{0,2},{1,3},{2,0},{3,1},{4,6},{5,7},{6,4},{7,5},{8,10},{9,11},{10,... | collective-permute-start | bytes 393224 | tf_op jit(solution)/shard_map/ppermute | solution.py:30
  20.7 3.8 %collective-permute-done.5.other_ref = bf16[32,2048]{1,0:T(8,128)(2,1)S(1)} collective-permute-done((bf16[32,2048]{1,0:T(8,128)(2,1)S(1)}, bf16[32,2048]{1,0:T(8,128)(2,1)S(1)}, u32[]{:S(2)}, u32[]{:S(2)}) %collective-permute-start.5) | collective-permute-done | bytes 131104 | tf_op jit(solution)/shard_map/ppermute | solution.py:30
  24.5 0.1 collective-permute-start.6
  24.7 0.0 copy-start.4
  24.7 2.5 %shard_map.130 = (f32[16,2176]{1,0:T(8,128)S(1)}, bf16[16,2176]{1,0:T(8,128)(2,1)S(1)}, bf16[16,2176]{1,0:T(8,128)(2,1)S(1)}, bf16[16,2176]{1,0:T(8,128)(2,1)S(1)}) custom-call(bf16[64,2048]{1,0:T(8,128)(2,1)S(1)} %get-tuple-element.31.cand_ref.base_ref, bf16[1,2048]{1,0:T(2,128)(2,1)S(1)} %reshape.21.score_ref, f32[1,2048]{1,0:T(1,128)S(1)} %bitcast.8, ...), custom_call_target="tpu_custom_call" | custom-call | flops 536870912 | bytes 622592 | tf_op jit(solution)/shard_map/pallas_call | solution.py:36
  27.2 0.1 collective-permute-start.10
  27.2 1.0 %collective-permute-start.11 = (bf16[16,2176]{1,0:T(8,128)(2,1)S(1)}, bf16[16,2176]{1,0:T(8,128)(2,1)S(1)}, u32[]{:S(2)}, u32[]{:S(2)}) collective-permute-start(bf16[16,2176]{1,0:T(8,128)(2,1)S(1)} %get-tuple-element.46), channel_id=1, source_target_pairs={{0,8},{4,12},{8,0},{12,4},{1,9},{5,13},{9,1},{13,5},{2,10},{6,14},... | collective-permute-start | bytes 208904 | tf_op jit(solution)/shard_map/ppermute | solution.py:30
  28.2 3.4 %collective-permute-start.12 = (bf16[16,2176]{1,0:T(8,128)(2,1)S(1)}, bf16[16,2176]{1,0:T(8,128)(2,1)S(1)}, u32[]{:S(2)}, u32[]{:S(2)}) collective-permute-start(bf16[16,2176]{1,0:T(8,128)(2,1)S(1)} %get-tuple-element.47), channel_id=1, source_target_pairs={{0,12},{4,8},{8,4},{12,0},{1,13},{5,9},{9,5},{13,1},{2,14},{6,10},... | collective-permute-start | bytes 208904 | tf_op jit(solution)/shard_map/ppermute | solution.py:30
  31.6 1.7 %shard_map.129 = (f32[16,2048]{1,0:T(8,128)S(1)}, bf16[16,2048]{1,0:T(8,128)(2,1)S(1)}, bf16[16,2048]{1,0:T(8,128)(2,1)S(1)}, bf16[16,2048]{1,0:T(8,128)(2,1)S(1)}) custom-call(f32[32,2048]{1,0:T(8,128)S(1)} %get-tuple-element.38.mine_ref, bf16[32,2048]{1,0:T(8,128)(2,1)S(1)} %collective-permute-done.6.other_ref, f32[1,2048]{1,0:T(1,128)S(1)} %bitcast.11, ...), custom_call_target="tpu_custom_call" | custom-call | flops 536870912 | bytes 1253376 | tf_op jit(solution)/shard_map/pallas_call | solution.py:36
  33.4 0.1 collective-permute-start.7
  33.4 0.9 %collective-permute-start.8 = (bf16[16,2048]{1,0:T(8,128)(2,1)S(1)}, bf16[16,2048]{1,0:T(8,128)(2,1)S(1)}, u32[]{:S(2)}, u32[]{:S(2)}) collective-permute-start(bf16[16,2048]{1,0:T(8,128)(2,1)S(1)} %get-tuple-element.42), channel_id=1, source_target_pairs={{0,8},{4,12},{8,0},{12,4},{1,9},{5,13},{9,1},{13,5},{2,10},{6,14},... | collective-permute-start | bytes 196616 | tf_op jit(solution)/shard_map/ppermute | solution.py:30
  34.4 0.0 collective-permute-done.10.refs_5_
  34.4 3.4 %collective-permute-start.9 = (bf16[16,2048]{1,0:T(8,128)(2,1)S(1)}, bf16[16,2048]{1,0:T(8,128)(2,1)S(1)}, u32[]{:S(2)}, u32[]{:S(2)}) collective-permute-start(bf16[16,2048]{1,0:T(8,128)(2,1)S(1)} %get-tuple-element.43), channel_id=1, source_target_pairs={{0,12},{4,8},{8,4},{12,0},{1,13},{5,9},{9,5},{13,1},{2,14},{6,10},... | collective-permute-start | bytes 196616 | tf_op jit(solution)/shard_map/ppermute | solution.py:30
  37.8 0.0 collective-permute-done.11.refs_6_
  37.8 0.0 collective-permute-done.12.refs_7_
  37.8 0.2 collective-permute-done.7.refs_1_
  38.1 3.9 %collective-permute-done.8.refs_2_ = bf16[16,2048]{1,0:T(8,128)(2,1)S(1)} collective-permute-done((bf16[16,2048]{1,0:T(8,128)(2,1)S(1)}, bf16[16,2048]{1,0:T(8,128)(2,1)S(1)}, u32[]{:S(2)}, u32[]{:S(2)}) %collective-permute-start.8) | collective-permute-done | bytes 65568 | tf_op jit(solution)/shard_map/ppermute | solution.py:30
  42.0 0.0 collective-permute-done.9.refs_3_
  42.0 0.2 shard_map.131.refs_0_
  42.2 1.4 %collective-permute-start.13 = (bf16[16,2176]{1,0:T(8,128)(2,1)S(1)}, bf16[16,2176]{1,0:T(8,128)(2,1)S(1)}, u32[]{:S(2)}, u32[]{:S(2)}) collective-permute-start(bf16[16,2176]{1,0:T(8,128)(2,1)S(1)} %shard_map.131.refs_0_), channel_id=1, source_target_pairs={{0,4},{4,0},{8,12},{12,8},{1,5},{5,1},{9,13},{13,9},{2,6},{6,2},{1... | collective-permute-start | bytes 208904 | tf_op jit(solution)/shard_map/ppermute | solution.py:30
  43.7 1.1 %collective-permute-start.14 = (bf16[16,2176]{1,0:T(8,128)(2,1)S(1)}, bf16[16,2176]{1,0:T(8,128)(2,1)S(1)}, u32[]{:S(2)}, u32[]{:S(2)}) collective-permute-start(bf16[16,2176]{1,0:T(8,128)(2,1)S(1)} %shard_map.131.refs_0_), channel_id=1, source_target_pairs={{0,8},{4,12},{8,0},{12,4},{1,9},{5,13},{9,1},{13,5},{2,10},{6,14},... | collective-permute-start | bytes 208904 | tf_op jit(solution)/shard_map/ppermute | solution.py:30
  44.8 1.8 %collective-permute-start.15 = (bf16[16,2176]{1,0:T(8,128)(2,1)S(1)}, bf16[16,2176]{1,0:T(8,128)(2,1)S(1)}, u32[]{:S(2)}, u32[]{:S(2)}) collective-permute-start(bf16[16,2176]{1,0:T(8,128)(2,1)S(1)} %shard_map.131.refs_0_), channel_id=1, source_target_pairs={{0,12},{4,8},{8,4},{12,0},{1,13},{5,9},{9,5},{13,1},{2,14},{6,10},... | collective-permute-start | bytes 208904 | tf_op jit(solution)/shard_map/ppermute | solution.py:30
  46.6 0.0 collective-permute-done.13.refs_1_
  46.6 4.8 %collective-permute-done.14.refs_2_ = bf16[16,2176]{1,0:T(8,128)(2,1)S(1)} collective-permute-done((bf16[16,2176]{1,0:T(8,128)(2,1)S(1)}, bf16[16,2176]{1,0:T(8,128)(2,1)S(1)}, u32[]{:S(2)}, u32[]{:S(2)}) %collective-permute-start.14) | collective-permute-done | bytes 69664 | tf_op jit(solution)/shard_map/ppermute | solution.py:30
  51.4 0.1 shard_map.132
  51.5 1.7 %shard_map.133 = (f32[32,2048]{1,0:T(8,128)S(1)}, bf16[32,2048]{1,0:T(8,128)(2,1)S(1)}) custom-call(bf16[64,2048]{1,0:T(8,128)(2,1)S(1)} %get-tuple-element.31.cand_ref.base_ref, bf16[2048,2048]{1,0:T(8,128)(2,1)S(1)} %bitcast.5, bf16[64,2048]{1,0:T(8,128)(2,1)S(1)} %get-tuple-element.48.rows_ref), custom_call_target="tpu_custom_call" | custom-call | flops 536870912 | bytes 917504 | tf_op jit(solution)/shard_map/pallas_call | solution.py:36
  53.2 0.1 collective-permute-start.16
  53.3 1.3 %collective-permute-done.16.other_ref = bf16[32,2048]{1,0:T(8,128)(2,1)S(1)} collective-permute-done((bf16[32,2048]{1,0:T(8,128)(2,1)S(1)}, bf16[32,2048]{1,0:T(8,128)(2,1)S(1)}, u32[]{:S(2)}, u32[]{:S(2)}) %collective-permute-start.16) | collective-permute-done | bytes 131104 | tf_op jit(solution)/shard_map/ppermute | solution.py:30
  54.7 1.8 %collective-permute-start.17 = (bf16[16,2048]{1,0:T(8,128)(2,1)S(1)}, bf16[16,2048]{1,0:T(8,128)(2,1)S(1)}, u32[]{:S(2)}, u32[]{:S(2)}) collective-permute-start(bf16[16,2048]{1,0:T(8,128)(2,1)S(1)} %get-tuple-element.52), channel_id=1, source_target_pairs={{0,2},{1,3},{2,0},{3,1},{4,6},{5,7},{6,4},{7,5},{8,10},{9,11},{10,... | collective-permute-start | bytes 196616 | tf_op jit(solution)/shard_map/ppermute | solution.py:30
  56.5 1.2 %collective-permute-done.18.refs_1_ = f32[4,16]{1,0:T(4,128)S(1)} collective-permute-done((f32[4,16]{1,0:T(4,128)S(1)}, f32[4,16]{1,0:T(4,128)S(1)}, u32[]{:S(2)}, u32[]{:S(2)}) %collective-permute-start.18) | collective-permute-done | bytes 288 | tf_op jit(solution)/shard_map/ppermute | solution.py:30
  57.7 0.3 collective-permute-start.19
  57.9 3.3 %collective-permute-done.19.part_ref = f32[4,16]{1,0:T(4,128)S(1)} collective-permute-done((f32[4,16]{1,0:T(4,128)S(1)}, f32[4,16]{1,0:T(4,128)S(1)}, u32[]{:S(2)}, u32[]{:S(2)}) %collective-permute-start.19) | collective-permute-done | bytes 288 | tf_op jit(solution)/shard_map/ppermute | solution.py:30
  61.3 0.7 %shard_map.136 = (bf16[16,2048]{1,0:T(8,128)(2,1)}, f32[1,16]{1,0:T(1,128)}) custom-call(f32[16,2048]{1,0:T(8,128)S(1)} %get-tuple-element.51.keep_ref, bf16[16,2048]{1,0:T(8,128)(2,1)S(1)} %collective-permute-done.17.other_ref, bf16[64,2048]{1,0:T(8,128)(2,1)S(1)} %get-tuple-element.31.cand_ref.base_ref, f32[1,2048]{1,0:T(1,128)S(1)} %bitcast.9, ...), custom_call_target="tpu_custom_call" | custom-call | bytes 533056 | tf_op jit(solution)/shard_map/pallas_call | solution.py:36
  (34 shorter events, 0.2 us)
Async XLA Ops:
  0.6 0.7 %copy-start.6 = (s32[1,64]{1,0:T(1,128)S(1)}, s32[1,64]{1,0:T(1,128)}, u32[]{:S(2)}) copy-start(s32[1,64]{1,0:T(1,128)} %ids_ref.1) | copy-start | bytes 772
  0.6 1.6 %copy-start.1 = (bf16[256,4096]{1,0:T(8,128)(2,1)S(1)}, bf16[256,4096]{1,0:T(8,128)(2,1)}, u32[]{:S(2)}) copy-start(bf16[256,4096]{1,0:T(8,128)(2,1)} %pool_ref.1) | copy-start | bytes 6291460
  0.7 4.0 %copy-start = (bf16[2048,2048]{1,0:T(8,128)(2,1)S(1)}, bf16[2048,2048]{1,0:T(8,128)(2,1)}, u32[]{:S(2)}) copy-start(bf16[2048,2048]{1,0:T(8,128)(2,1)} %weight_ref.6) | copy-start | bytes 25165828
  2.2 3.1 %copy-start.3 = (bf16[1,4096]{1,0:T(2,128)(2,1)S(1)}, bf16[1,4096]{1,0:T(2,128)(2,1)}, u32[]{:S(2)}) copy-start(bf16[1,4096]{1,0:T(2,128)(2,1)} %refs_0_.1) | copy-start | bytes 24580
  4.7 19.9 %copy-start.7 = (bf16[2048]{0:T(1024)(128)(2,1)S(1)}, bf16[2048]{0:T(1024)(128)(2,1)}, u32[]{:S(2)}) copy-start(bf16[2048]{0:T(1024)(128)(2,1)} %param.21) | copy-start | bytes 12292
  4.7 20.0 %slice-start = ((s8[8388608]{0:T(1024)(128)(4,1)}), s8[4194304]{0:T(1024)(128)(4,1)S(1)}, s32[]{:S(2)}) async-start(s8[8388608]{0:T(1024)(128)(4,1)} %bitcast.4), calls=%async_computation | async-start | bytes 8388608
  4.7 20.0 %copy-start.2 = (f32[2048]{0:T(1024)S(1)}, f32[2048]{0:T(1024)}, u32[]{:S(2)}) copy-start(f32[2048]{0:T(1024)} %param.20) | copy-start | bytes 24580
  4.7 26.9 %slice-start.2 = ((s8[8388608]{0:T(1024)(128)(4,1)}), s8[4194304]{0:T(1024)(128)(4,1)S(1)}, s32[]{:S(2)}) async-start(s8[8388608]{0:T(1024)(128)(4,1)} %bitcast.6), calls=%async_computation.2 | async-start | bytes 8388608
  4.7 13.9 %collective-permute-start.3 = (bf16[32,2048]{1,0:T(8,128)(2,1)S(1)}, bf16[32,2048]{1,0:T(8,128)(2,1)S(1)}, u32[]{:S(2)}, u32[]{:S(2)}) collective-permute-start(bf16[32,2048]{1,0:T(8,128)(2,1)S(1)} %get-tuple-element.34), channel_id=1, source_target_pairs={{0,1},{1,0},{2,3},{3,2},{4,5},{5,4},{6,7},{7,6},{8,9},{9,8},{10,11... | collective-permute-start | bytes 393224 | tf_op jit(solution)/shard_map/ppermute | solution.py:30
  5.3 5.9 %collective-permute-start = (bf16[1,4096]{1,0:T(2,128)(2,1)S(1)}, bf16[1,4096]{1,0:T(2,128)(2,1)S(1)}, u32[]{:S(2)}, u32[]{:S(2)}) collective-permute-start(bf16[1,4096]{1,0:T(2,128)(2,1)S(1)} %copy-done.3), channel_id=1, source_target_pairs={{0,4},{4,0},{8,12},{12,8},{1,5},{5,1},{9,13},{13,9},{2,6},{6,2},{1... | collective-permute-start | bytes 24584 | tf_op jit(solution)/shard_map/ppermute | solution.py:30
  7.9 4.6 %collective-permute-start.1 = (bf16[1,4096]{1,0:T(2,128)(2,1)S(1)}, bf16[1,4096]{1,0:T(2,128)(2,1)S(1)}, u32[]{:S(2)}, u32[]{:S(2)}) collective-permute-start(bf16[1,4096]{1,0:T(2,128)(2,1)S(1)} %copy-done.3), channel_id=1, source_target_pairs={{0,8},{4,12},{8,0},{12,4},{1,9},{5,13},{9,1},{13,5},{2,10},{6,14},... | collective-permute-start | bytes 24584 | tf_op jit(solution)/shard_map/ppermute | solution.py:30
  10.5 5.5 %collective-permute-start.2 = (bf16[1,4096]{1,0:T(2,128)(2,1)S(1)}, bf16[1,4096]{1,0:T(2,128)(2,1)S(1)}, u32[]{:S(2)}, u32[]{:S(2)}) collective-permute-start(bf16[1,4096]{1,0:T(2,128)(2,1)S(1)} %copy-done.3), channel_id=1, source_target_pairs={{0,12},{4,8},{8,4},{12,0},{1,13},{5,9},{9,5},{13,1},{2,14},{6,10},... | collective-permute-start | bytes 24584 | tf_op jit(solution)/shard_map/ppermute | solution.py:30
  16.1 8.6 %slice-start.1 = ((s8[8388608]{0:T(1024)(128)(4,1)}), s8[4194304]{0:T(1024)(128)(4,1)S(1)}, s32[]{:S(2)}) async-start(s8[8388608]{0:T(1024)(128)(4,1)} %bitcast.4), calls=%async_computation.1 | async-start | bytes 8388608
  16.1 15.6 %slice-start.3 = ((s8[8388608]{0:T(1024)(128)(4,1)}), s8[4194304]{0:T(1024)(128)(4,1)S(1)}, s32[]{:S(2)}) async-start(s8[8388608]{0:T(1024)(128)(4,1)} %bitcast.6), calls=%async_computation.3 | async-start | bytes 8388608
  16.1 15.6 %copy-start.5 = (f32[2048]{0:T(1024)S(1)}, f32[2048]{0:T(1024)}, u32[]{:S(2)}) copy-start(f32[2048]{0:T(1024)} %param.16) | copy-start | bytes 24580
  17.4 1.2 %collective-permute-start.4 = (f32[1,2048]{1,0:T(1,128)S(1)}, f32[1,2048]{1,0:T(1,128)S(1)}, u32[]{:S(2)}, u32[]{:S(2)}) collective-permute-start(f32[1,2048]{1,0:T(1,128)S(1)} %get-tuple-element.35.user_ref), channel_id=1, source_target_pairs={{0,1},{1,0},{2,3},{3,2},{4,5},{5,4},{6,7},{7,6},{8,9},{9,8},{10,11... | collective-permute-start | bytes 24584 | tf_op jit(solution)/shard_map/ppermute | solution.py:30
  18.7 5.8 %collective-permute-start.5 = (bf16[32,2048]{1,0:T(8,128)(2,1)S(1)}, bf16[32,2048]{1,0:T(8,128)(2,1)S(1)}, u32[]{:S(2)}, u32[]{:S(2)}) collective-permute-start(bf16[32,2048]{1,0:T(8,128)(2,1)S(1)} %get-tuple-element.37), channel_id=1, source_target_pairs={{0,2},{1,3},{2,0},{3,1},{4,6},{5,7},{6,4},{7,5},{8,10},{9,11},{10,... | collective-permute-start | bytes 393224 | tf_op jit(solution)/shard_map/ppermute | solution.py:30
  24.5 7.1 %collective-permute-start.6 = (bf16[32,2048]{1,0:T(8,128)(2,1)S(1)}, bf16[32,2048]{1,0:T(8,128)(2,1)S(1)}, u32[]{:S(2)}, u32[]{:S(2)}) collective-permute-start(bf16[32,2048]{1,0:T(8,128)(2,1)S(1)} %get-tuple-element.39), channel_id=1, source_target_pairs={{0,1},{1,0},{2,3},{3,2},{4,5},{5,4},{6,7},{7,6},{8,9},{9,8},{10,11... | collective-permute-start | bytes 393224 | tf_op jit(solution)/shard_map/ppermute | solution.py:30
  24.7 17.3 %copy-start.4 = (f32[2048]{0:T(1024)S(1)}, f32[2048]{0:T(1024)}, u32[]{:S(2)}) copy-start(f32[2048]{0:T(1024)} %param.18) | copy-start | bytes 24580
  27.2 7.2 %collective-permute-start.10 = (bf16[16,2176]{1,0:T(8,128)(2,1)S(1)}, bf16[16,2176]{1,0:T(8,128)(2,1)S(1)}, u32[]{:S(2)}, u32[]{:S(2)}) collective-permute-start(bf16[16,2176]{1,0:T(8,128)(2,1)S(1)} %get-tuple-element.45), channel_id=1, source_target_pairs={{0,4},{4,0},{8,12},{12,8},{1,5},{5,1},{9,13},{13,9},{2,6},{6,2},{1... | collective-permute-start | bytes 208904 | tf_op jit(solution)/shard_map/ppermute | solution.py:30
  27.2 10.6 %collective-permute-start.11 = (bf16[16,2176]{1,0:T(8,128)(2,1)S(1)}, bf16[16,2176]{1,0:T(8,128)(2,1)S(1)}, u32[]{:S(2)}, u32[]{:S(2)}) collective-permute-start(bf16[16,2176]{1,0:T(8,128)(2,1)S(1)} %get-tuple-element.46), channel_id=1, source_target_pairs={{0,8},{4,12},{8,0},{12,4},{1,9},{5,13},{9,1},{13,5},{2,10},{6,14},... | collective-permute-start | bytes 208904 | tf_op jit(solution)/shard_map/ppermute | solution.py:30
  28.2 9.6 %collective-permute-start.12 = (bf16[16,2176]{1,0:T(8,128)(2,1)S(1)}, bf16[16,2176]{1,0:T(8,128)(2,1)S(1)}, u32[]{:S(2)}, u32[]{:S(2)}) collective-permute-start(bf16[16,2176]{1,0:T(8,128)(2,1)S(1)} %get-tuple-element.47), channel_id=1, source_target_pairs={{0,12},{4,8},{8,4},{12,0},{1,13},{5,9},{9,5},{13,1},{2,14},{6,10},... | collective-permute-start | bytes 208904 | tf_op jit(solution)/shard_map/ppermute | solution.py:30
  33.4 4.7 %collective-permute-start.7 = (bf16[16,2048]{1,0:T(8,128)(2,1)S(1)}, bf16[16,2048]{1,0:T(8,128)(2,1)S(1)}, u32[]{:S(2)}, u32[]{:S(2)}) collective-permute-start(bf16[16,2048]{1,0:T(8,128)(2,1)S(1)} %get-tuple-element.41), channel_id=1, source_target_pairs={{0,4},{4,0},{8,12},{12,8},{1,5},{5,1},{9,13},{13,9},{2,6},{6,2},{1... | collective-permute-start | bytes 196616 | tf_op jit(solution)/shard_map/ppermute | solution.py:30
  33.4 8.6 %collective-permute-start.8 = (bf16[16,2048]{1,0:T(8,128)(2,1)S(1)}, bf16[16,2048]{1,0:T(8,128)(2,1)S(1)}, u32[]{:S(2)}, u32[]{:S(2)}) collective-permute-start(bf16[16,2048]{1,0:T(8,128)(2,1)S(1)} %get-tuple-element.42), channel_id=1, source_target_pairs={{0,8},{4,12},{8,0},{12,4},{1,9},{5,13},{9,1},{13,5},{2,10},{6,14},... | collective-permute-start | bytes 196616 | tf_op jit(solution)/shard_map/ppermute | solution.py:30
  34.4 7.6 %collective-permute-start.9 = (bf16[16,2048]{1,0:T(8,128)(2,1)S(1)}, bf16[16,2048]{1,0:T(8,128)(2,1)S(1)}, u32[]{:S(2)}, u32[]{:S(2)}) collective-permute-start(bf16[16,2048]{1,0:T(8,128)(2,1)S(1)} %get-tuple-element.43), channel_id=1, source_target_pairs={{0,12},{4,8},{8,4},{12,0},{1,13},{5,9},{9,5},{13,1},{2,14},{6,10},... | collective-permute-start | bytes 196616 | tf_op jit(solution)/shard_map/ppermute | solution.py:30
  42.2 4.4 %collective-permute-start.13 = (bf16[16,2176]{1,0:T(8,128)(2,1)S(1)}, bf16[16,2176]{1,0:T(8,128)(2,1)S(1)}, u32[]{:S(2)}, u32[]{:S(2)}) collective-permute-start(bf16[16,2176]{1,0:T(8,128)(2,1)S(1)} %shard_map.131.refs_0_), channel_id=1, source_target_pairs={{0,4},{4,0},{8,12},{12,8},{1,5},{5,1},{9,13},{13,9},{2,6},{6,2},{1... | collective-permute-start | bytes 208904 | tf_op jit(solution)/shard_map/ppermute | solution.py:30
  43.7 7.8 %collective-permute-start.14 = (bf16[16,2176]{1,0:T(8,128)(2,1)S(1)}, bf16[16,2176]{1,0:T(8,128)(2,1)S(1)}, u32[]{:S(2)}, u32[]{:S(2)}) collective-permute-start(bf16[16,2176]{1,0:T(8,128)(2,1)S(1)} %shard_map.131.refs_0_), channel_id=1, source_target_pairs={{0,8},{4,12},{8,0},{12,4},{1,9},{5,13},{9,1},{13,5},{2,10},{6,14},... | collective-permute-start | bytes 208904 | tf_op jit(solution)/shard_map/ppermute | solution.py:30
  44.8 6.6 %collective-permute-start.15 = (bf16[16,2176]{1,0:T(8,128)(2,1)S(1)}, bf16[16,2176]{1,0:T(8,128)(2,1)S(1)}, u32[]{:S(2)}, u32[]{:S(2)}) collective-permute-start(bf16[16,2176]{1,0:T(8,128)(2,1)S(1)} %shard_map.131.refs_0_), channel_id=1, source_target_pairs={{0,12},{4,8},{8,4},{12,0},{1,13},{5,9},{9,5},{13,1},{2,14},{6,10},... | collective-permute-start | bytes 208904 | tf_op jit(solution)/shard_map/ppermute | solution.py:30
  53.2 1.4 %collective-permute-start.16 = (bf16[32,2048]{1,0:T(8,128)(2,1)S(1)}, bf16[32,2048]{1,0:T(8,128)(2,1)S(1)}, u32[]{:S(2)}, u32[]{:S(2)}) collective-permute-start(bf16[32,2048]{1,0:T(8,128)(2,1)S(1)} %get-tuple-element.50), channel_id=1, source_target_pairs={{0,1},{1,0},{2,3},{3,2},{4,5},{5,4},{6,7},{7,6},{8,9},{9,8},{10,11... | collective-permute-start | bytes 393224 | tf_op jit(solution)/shard_map/ppermute | solution.py:30
  54.7 6.6 %collective-permute-start.17 = (bf16[16,2048]{1,0:T(8,128)(2,1)S(1)}, bf16[16,2048]{1,0:T(8,128)(2,1)S(1)}, u32[]{:S(2)}, u32[]{:S(2)}) collective-permute-start(bf16[16,2048]{1,0:T(8,128)(2,1)S(1)} %get-tuple-element.52), channel_id=1, source_target_pairs={{0,2},{1,3},{2,0},{3,1},{4,6},{5,7},{6,4},{7,5},{8,10},{9,11},{10,... | collective-permute-start | bytes 196616 | tf_op jit(solution)/shard_map/ppermute | solution.py:30
  56.5 1.2 %collective-permute-start.18 = (f32[4,16]{1,0:T(4,128)S(1)}, f32[4,16]{1,0:T(4,128)S(1)}, u32[]{:S(2)}, u32[]{:S(2)}) collective-permute-start(f32[4,16]{1,0:T(4,128)S(1)} %get-tuple-element.53.refs_0_), channel_id=1, source_target_pairs={{0,1},{1,0},{2,3},{3,2},{4,5},{5,4},{6,7},{7,6},{8,9},{9,8},{10,11... | collective-permute-start | bytes 776 | tf_op jit(solution)/shard_map/ppermute | solution.py:30
  57.7 3.6 %collective-permute-start.19 = (f32[4,16]{1,0:T(4,128)S(1)}, f32[4,16]{1,0:T(4,128)S(1)}, u32[]{:S(2)}, u32[]{:S(2)}) collective-permute-start(f32[4,16]{1,0:T(4,128)S(1)} %shard_map.135.total_ref), channel_id=1, source_target_pairs={{0,2},{1,3},{2,0},{3,1},{4,6},{5,7},{6,4},{7,5},{8,10},{9,11},{10,... | collective-permute-start | bytes 776 | tf_op jit(solution)/shard_map/ppermute | solution.py:30

commit v5 on v4

--- a/solution.py
+++ b/solution.py
@@ -169,18 +169,17 @@
     send_ref[...] = total.astype(BF16)
 
 
-def merge(keep_ref, other_ref, user_ref, user_other_ref, sum_ref, send_ref, users_ref):
+def merge(keep_ref, part_ref, user_ref, sum_ref, send_ref):
     low = lax.axis_index("mp") % 2
     size, users = keep_ref.shape[0], user_ref.shape[0]
     assert users == 1 or users % 2 == 0
-    users_ref[...] = user_ref[...] + user_other_ref[...]
     each = max(users // 2, 1)
-    for piece in range(each):
-        user = low * each + piece if users > 1 else 0
-        part = pl.ds(piece * (size // each), size // each)
-        total = keep_ref[part, :] + other_ref[part, :].astype(F32) + users_ref[pl.ds(user, 1), :]
-        sum_ref[part, :] = total
-        send_ref[part, :] = total.astype(BF16)
+    for index, in_ref, out_ref in ((low, keep_ref, sum_ref), (1 - low, part_ref, send_ref)):
+        for piece in range(each):
+            user = index * each + piece if users > 1 else 0
+            part = pl.ds(piece * (size // each), size // each)
+            total = in_ref[part, :].astype(F32) + user_ref[pl.ds(user, 1), :]
+            out_ref[part, :] = total.astype(out_ref.dtype)
 
 
 def add_own_columns(terms_ref, rows_ref, have, want):
@@ -426,24 +425,11 @@
         flops=flops,
         limit=12 * MIB,
     )
+    keep, send = call(merge, half_outs, [keep, send, user_sum])
     *bits, last_bit = bits_of(model_count)
     assert bits
-    for bit in bits:
-        other = swap(send, "mp", bit)
-        user_other = swap(user_sum, "mp", bit)
-        if bit == bits[-1]:
-            keep, send = call(
-                merge,
-                half_outs,
-                [keep, other, user_sum, user_other],
-                scratch=[pltpu.VMEM((user_count, col_block), F32)],
-            )
-        else:
-            keep, send = call(add_up, half_outs, [keep, other])
-            (user_sum,) = call(
-                add_to, [((user_count, col_block), F32)], [user_sum, user_other]
-            )
-    keep, send = call(add_up, half_outs, [keep, swap(send, "mp", last_bit)])
+    for bit in [*bits, last_bit]:
+        keep, send = call(add_up, half_outs, [keep, swap(send, "mp", bit)])
     pool_other = swap(send, "mp", 1)
 
     if direct:

time: 62.1 us -> 57 us (0.918)
  local copies, waits for them, and re-layouts: 3.53 us -> 0.07 us
  starting transfers between devices: 23.3 us -> 21.6 us
    unnamed x24, local copies, waits for them, and re-layouts: 3.52 us -> 0.06 us
    ppermute x20 -> x19, starting transfers between devices: 23.3 us -> 21.6 us  [swap(): return lax.ppermute(value, axis, [(i, i ^ bit) for i in range(count)])]
    ppermute x20 -> x19, waiting for transfers between devices: 24.6 us -> 24.5 us  [swap(): return lax.ppermute(value, axis, [(i, i ^ bit) for i in range(count)])]
    pallas_call x15 -> x16, Pallas kernels: 8.91 us -> 8.97 us  [call(): pl.pallas_call(kernel, out_shape=[jax.ShapeDtypeStruct(s, d) for s, d in...]
  transfers between devices with their start and end apart: 20 -> 19, of which waited for: 10 -> 10; matrix products, arithmetic and copies ran while one was open for 0% -> 0% of each run, Pallas kernels for 9% -> 8%
where the time goes in v5:
time: 57 us; the launch traced here: 56.9 us
  waiting for transfers between devices  24.5 us (43%)
  starting transfers between devices  21.6 us (38%)
  Pallas kernels  8.97 us (16%)
  between operations  1.72 us (3%)
    ppermute x19, waiting for transfers between devices, swap(): return lax.ppermute(value, axis, [(i, i ^ bit) for i in range(count)])  24.5 us
    ppermute x19, starting transfers between devices, swap(): return lax.ppermute(value, axis, [(i, i ^ bit) for i in range(count)])  21.6 us
    pallas_call x16, Pallas kernels, call(): pl.pallas_call(kernel, out_shape=[jax.ShapeDtypeStruct(s, d) for s, d in...  8.97 us
  transfers between devices with their start and end apart: 19, of which 10 were waited for; matrix products, arithmetic and copies ran while one was open for 0% of the time, Pallas kernels for 8%

profile of v5, /device:TPU:0, one launch (start us, length us, event | category | flops | bytes accessed | tf_op | source)
XLA Modules:
  0.0 56.9 jit_solution(15304539393822262333)
XLA Ops:
  0.7 3.1 %collective-permute-start = (bf16[1,4096]{1,0:T(2,128)(2,1)}, bf16[1,4096]{1,0:T(2,128)(2,1)S(1)}, u32[]{:S(2)}, u32[]{:S(2)}) collective-permute-start(bf16[1,4096]{1,0:T(2,128)(2,1)} %refs_0_.1), channel_id=1, source_target_pairs={{0,4},{4,0},{8,12},{12,8},{1,5},{5,1},{9,13},{13,9},{2,6},{6,2},{1... | collective-permute-start | bytes 24584 | tf_op jit(solution)/shard_map/ppermute | solution.py:30
  3.8 2.6 %collective-permute-start.1 = (bf16[1,4096]{1,0:T(2,128)(2,1)}, bf16[1,4096]{1,0:T(2,128)(2,1)S(1)}, u32[]{:S(2)}, u32[]{:S(2)}) collective-permute-start(bf16[1,4096]{1,0:T(2,128)(2,1)} %refs_0_.1), channel_id=1, source_target_pairs={{0,8},{4,12},{8,0},{12,4},{1,9},{5,13},{9,1},{13,5},{2,10},{6,14},... | collective-permute-start | bytes 24584 | tf_op jit(solution)/shard_map/ppermute | solution.py:30
  6.4 0.0 collective-permute-start.2
  6.4 0.0 copy-start.3
  6.4 0.5 shard_map.124
  6.9 0.0 copy-start.7
  6.9 0.0 slice-start
  6.9 0.0 copy-start.2
  7.0 0.0 slice-start.2
  7.8 0.0 collective-permute-done.refs_1_
  7.8 0.9 %collective-permute-done.1.refs_2_ = bf16[1,4096]{1,0:T(2,128)(2,1)S(1)} collective-permute-done((bf16[1,4096]{1,0:T(2,128)(2,1)}, bf16[1,4096]{1,0:T(2,128)(2,1)S(1)}, u32[]{:S(2)}, u32[]{:S(2)}) %collective-permute-start.1) | collective-permute-done | bytes 8224 | tf_op jit(solution)/shard_map/ppermute | solution.py:30
  8.7 3.4 %collective-permute-done.2.refs_3_ = bf16[1,4096]{1,0:T(2,128)(2,1)S(1)} collective-permute-done((bf16[1,4096]{1,0:T(2,128)(2,1)}, bf16[1,4096]{1,0:T(2,128)(2,1)S(1)}, u32[]{:S(2)}, u32[]{:S(2)}) %collective-permute-start.2) | collective-permute-done | bytes 8224 | tf_op jit(solution)/shard_map/ppermute | solution.py:30
  12.1 1.4 %shard_map.125 = (bf16[64,2048]{1,0:T(8,128)(2,1)S(1)}, bf16[64,2048]{1,0:T(8,128)(2,1)S(1)}, f32[1,2048]{1,0:T(1,128)S(1)}) custom-call(s32[1,128]{1,0:T(1,128)S(1)} %shard_map.122.want_ref, bf16[2048,2048]{1,0:T(8,128)(2,1)S(1)} %copy-done, bf16[64,2048]{1,0:T(8,128)(2,1)S(1)} %get-tuple-element.31.pool_model_ref.rows_ref, ...), custom_call_target="tpu_custom_call" | custom-call | flops 536870912 | bytes 1090048 | tf_op jit(solution)/shard_map/pallas_call | solution.py:36
  13.5 0.1 collective-permute-start.3
  13.6 1.3 %collective-permute-done.3.other_ref = bf16[32,2048]{1,0:T(8,128)(2,1)S(1)} collective-permute-done((bf16[32,2048]{1,0:T(8,128)(2,1)S(1)}, bf16[32,2048]{1,0:T(8,128)(2,1)S(1)}, u32[]{:S(2)}, u32[]{:S(2)}) %collective-permute-start.3) | collective-permute-done | bytes 131104 | tf_op jit(solution)/shard_map/ppermute | solution.py:30
  15.0 0.3 collective-permute-start.4
  15.3 5.3 %collective-permute-done.4.other_ref = bf16[32,2048]{1,0:T(8,128)(2,1)S(1)} collective-permute-done((bf16[32,2048]{1,0:T(8,128)(2,1)S(1)}, bf16[32,2048]{1,0:T(8,128)(2,1)S(1)}, u32[]{:S(2)}, u32[]{:S(2)}) %collective-permute-start.4) | collective-permute-done | bytes 131104 | tf_op jit(solution)/shard_map/ppermute | solution.py:30
  20.7 0.1 collective-permute-start.5
  20.8 0.0 copy-start.4
  20.8 2.5 %shard_map.131 = (f32[16,2176]{1,0:T(8,128)S(1)}, bf16[16,2176]{1,0:T(8,128)(2,1)S(1)}, bf16[16,2176]{1,0:T(8,128)(2,1)S(1)}, bf16[16,2176]{1,0:T(8,128)(2,1)S(1)}) custom-call(bf16[64,2048]{1,0:T(8,128)(2,1)S(1)} %get-tuple-element.33.cand_ref.base_ref, bf16[1,2048]{1,0:T(2,128)(2,1)S(1)} %reshape.21.score_ref, f32[1,2048]{1,0:T(1,128)S(1)} %bitcast.8, ...), custom_call_target="tpu_custom_call" | custom-call | flops 536870912 | bytes 622592 | tf_op jit(solution)/shard_map/pallas_call | solution.py:36
  23.3 0.1 collective-permute-start.9
  23.4 1.1 %collective-permute-start.10 = (bf16[16,2176]{1,0:T(8,128)(2,1)S(1)}, bf16[16,2176]{1,0:T(8,128)(2,1)S(1)}, u32[]{:S(2)}, u32[]{:S(2)}) collective-permute-start(bf16[16,2176]{1,0:T(8,128)(2,1)S(1)} %get-tuple-element.50), channel_id=1, source_target_pairs={{0,8},{4,12},{8,0},{12,4},{1,9},{5,13},{9,1},{13,5},{2,10},{6,14},... | collective-permute-start | bytes 208904 | tf_op jit(solution)/shard_map/ppermute | solution.py:30
  24.5 3.3 %collective-permute-start.11 = (bf16[16,2176]{1,0:T(8,128)(2,1)S(1)}, bf16[16,2176]{1,0:T(8,128)(2,1)S(1)}, u32[]{:S(2)}, u32[]{:S(2)}) collective-permute-start(bf16[16,2176]{1,0:T(8,128)(2,1)S(1)} %get-tuple-element.51), channel_id=1, source_target_pairs={{0,12},{4,8},{8,4},{12,0},{1,13},{5,9},{9,5},{13,1},{2,14},{6,10},... | collective-permute-start | bytes 208904 | tf_op jit(solution)/shard_map/ppermute | solution.py:30
  27.8 0.0 collective-permute-done.5.other_ref
  27.8 1.7 %shard_map.130 = (f32[16,2048]{1,0:T(8,128)S(1)}, bf16[16,2048]{1,0:T(8,128)(2,1)S(1)}, bf16[16,2048]{1,0:T(8,128)(2,1)S(1)}, bf16[16,2048]{1,0:T(8,128)(2,1)S(1)}) custom-call(f32[32,2048]{1,0:T(8,128)S(1)} %get-tuple-element.42.mine_ref, bf16[32,2048]{1,0:T(8,128)(2,1)S(1)} %collective-permute-done.5.other_ref, f32[1,2048]{1,0:T(1,128)S(1)} %bitcast.11, ...), custom_call_target="tpu_custom_call" | custom-call | flops 536870912 | bytes 1253376 | tf_op jit(solution)/shard_map/pallas_call | solution.py:36
  29.5 0.1 collective-permute-start.6
  29.6 1.1 %collective-permute-start.7 = (bf16[16,2048]{1,0:T(8,128)(2,1)S(1)}, bf16[16,2048]{1,0:T(8,128)(2,1)S(1)}, u32[]{:S(2)}, u32[]{:S(2)}) collective-permute-start(bf16[16,2048]{1,0:T(8,128)(2,1)S(1)} %get-tuple-element.46), channel_id=1, source_target_pairs={{0,8},{4,12},{8,0},{12,4},{1,9},{5,13},{9,1},{13,5},{2,10},{6,14},... | collective-permute-start | bytes 196616 | tf_op jit(solution)/shard_map/ppermute | solution.py:30
  30.6 3.3 %collective-permute-start.8 = (bf16[16,2048]{1,0:T(8,128)(2,1)S(1)}, bf16[16,2048]{1,0:T(8,128)(2,1)S(1)}, u32[]{:S(2)}, u32[]{:S(2)}) collective-permute-start(bf16[16,2048]{1,0:T(8,128)(2,1)S(1)} %get-tuple-element.47), channel_id=1, source_target_pairs={{0,12},{4,8},{8,4},{12,0},{1,13},{5,9},{9,5},{13,1},{2,14},{6,10},... | collective-permute-start | bytes 196616 | tf_op jit(solution)/shard_map/ppermute | solution.py:30
  34.0 0.0 collective-permute-done.10.refs_6_
  34.0 0.0 collective-permute-done.11.refs_7_
  34.0 0.2 collective-permute-done.6.refs_1_
  34.2 3.9 %collective-permute-done.7.refs_2_ = bf16[16,2048]{1,0:T(8,128)(2,1)S(1)} collective-permute-done((bf16[16,2048]{1,0:T(8,128)(2,1)S(1)}, bf16[16,2048]{1,0:T(8,128)(2,1)S(1)}, u32[]{:S(2)}, u32[]{:S(2)}) %collective-permute-start.7) | collective-permute-done | bytes 65568 | tf_op jit(solution)/shard_map/ppermute | solution.py:30
  38.1 0.2 shard_map.132.refs_0_
  38.4 1.4 %collective-permute-start.12 = (bf16[16,2176]{1,0:T(8,128)(2,1)S(1)}, bf16[16,2176]{1,0:T(8,128)(2,1)S(1)}, u32[]{:S(2)}, u32[]{:S(2)}) collective-permute-start(bf16[16,2176]{1,0:T(8,128)(2,1)S(1)} %shard_map.132.refs_0_), channel_id=1, source_target_pairs={{0,4},{4,0},{8,12},{12,8},{1,5},{5,1},{9,13},{13,9},{2,6},{6,2},{1... | collective-permute-start | bytes 208904 | tf_op jit(solution)/shard_map/ppermute | solution.py:30
  39.8 1.1 %collective-permute-start.13 = (bf16[16,2176]{1,0:T(8,128)(2,1)S(1)}, bf16[16,2176]{1,0:T(8,128)(2,1)S(1)}, u32[]{:S(2)}, u32[]{:S(2)}) collective-permute-start(bf16[16,2176]{1,0:T(8,128)(2,1)S(1)} %shard_map.132.refs_0_), channel_id=1, source_target_pairs={{0,8},{4,12},{8,0},{12,4},{1,9},{5,13},{9,1},{13,5},{2,10},{6,14},... | collective-permute-start | bytes 208904 | tf_op jit(solution)/shard_map/ppermute | solution.py:30
  40.9 1.8 %collective-permute-start.14 = (bf16[16,2176]{1,0:T(8,128)(2,1)S(1)}, bf16[16,2176]{1,0:T(8,128)(2,1)S(1)}, u32[]{:S(2)}, u32[]{:S(2)}) collective-permute-start(bf16[16,2176]{1,0:T(8,128)(2,1)S(1)} %shard_map.132.refs_0_), channel_id=1, source_target_pairs={{0,12},{4,8},{8,4},{12,0},{1,13},{5,9},{9,5},{13,1},{2,14},{6,10},... | collective-permute-start | bytes 208904 | tf_op jit(solution)/shard_map/ppermute | solution.py:30
  42.8 4.8 %collective-permute-done.13.refs_2_ = bf16[16,2176]{1,0:T(8,128)(2,1)S(1)} collective-permute-done((bf16[16,2176]{1,0:T(8,128)(2,1)S(1)}, bf16[16,2176]{1,0:T(8,128)(2,1)S(1)}, u32[]{:S(2)}, u32[]{:S(2)}) %collective-permute-start.13) | collective-permute-done | bytes 69664 | tf_op jit(solution)/shard_map/ppermute | solution.py:30
  47.5 0.0 collective-permute-done.14.refs_3_
  47.5 0.1 shard_map.133
  47.7 1.7 %shard_map.134 = (f32[32,2048]{1,0:T(8,128)S(1)}, bf16[32,2048]{1,0:T(8,128)(2,1)S(1)}) custom-call(bf16[64,2048]{1,0:T(8,128)(2,1)S(1)} %get-tuple-element.33.cand_ref.base_ref, bf16[2048,2048]{1,0:T(8,128)(2,1)S(1)} %bitcast.5, bf16[64,2048]{1,0:T(8,128)(2,1)S(1)} %get-tuple-element.52.rows_ref), custom_call_target="tpu_custom_call" | custom-call | flops 536870912 | bytes 917504 | tf_op jit(solution)/shard_map/pallas_call | solution.py:36
  49.4 0.1 collective-permute-start.15
  49.4 1.3 %collective-permute-done.15.other_ref = bf16[32,2048]{1,0:T(8,128)(2,1)S(1)} collective-permute-done((bf16[32,2048]{1,0:T(8,128)(2,1)S(1)}, bf16[32,2048]{1,0:T(8,128)(2,1)S(1)}, u32[]{:S(2)}, u32[]{:S(2)}) %collective-permute-start.15) | collective-permute-done | bytes 131104 | tf_op jit(solution)/shard_map/ppermute | solution.py:30
  50.8 0.6 %collective-permute-start.16 = (bf16[16,2048]{1,0:T(8,128)(2,1)S(1)}, bf16[16,2048]{1,0:T(8,128)(2,1)S(1)}, u32[]{:S(2)}, u32[]{:S(2)}) collective-permute-start(bf16[16,2048]{1,0:T(8,128)(2,1)S(1)} %get-tuple-element.56), channel_id=1, source_target_pairs={{0,2},{1,3},{2,0},{3,1},{4,6},{5,7},{6,4},{7,5},{8,10},{9,11},{10,... | collective-permute-start | bytes 196616 | tf_op jit(solution)/shard_map/ppermute | solution.py:30
  51.4 1.2 %collective-permute-done.17.refs_1_ = f32[4,16]{1,0:T(4,128)S(1)} collective-permute-done((f32[4,16]{1,0:T(4,128)S(1)}, f32[4,16]{1,0:T(4,128)S(1)}, u32[]{:S(2)}, u32[]{:S(2)}) %collective-permute-start.17) | collective-permute-done | bytes 288 | tf_op jit(solution)/shard_map/ppermute | solution.py:30
  52.6 1.5 %collective-permute-start.18 = (f32[4,16]{1,0:T(4,128)S(1)}, f32[4,16]{1,0:T(4,128)S(1)}, u32[]{:S(2)}, u32[]{:S(2)}) collective-permute-start(f32[4,16]{1,0:T(4,128)S(1)} %shard_map.136.total_ref), channel_id=1, source_target_pairs={{0,2},{1,3},{2,0},{3,1},{4,6},{5,7},{6,4},{7,5},{8,10},{9,11},{10,... | collective-permute-start | bytes 776 | tf_op jit(solution)/shard_map/ppermute | solution.py:30
  54.1 2.1 %collective-permute-done.18.part_ref = f32[4,16]{1,0:T(4,128)S(1)} collective-permute-done((f32[4,16]{1,0:T(4,128)S(1)}, f32[4,16]{1,0:T(4,128)S(1)}, u32[]{:S(2)}, u32[]{:S(2)}) %collective-permute-start.18) | collective-permute-done | bytes 288 | tf_op jit(solution)/shard_map/ppermute | solution.py:30
  56.2 0.0 collective-permute-done.16.other_ref
  56.2 0.7 %shard_map.137 = (bf16[16,2048]{1,0:T(8,128)(2,1)}, f32[1,16]{1,0:T(1,128)}) custom-call(f32[16,2048]{1,0:T(8,128)S(1)} %get-tuple-element.55.keep_ref, bf16[16,2048]{1,0:T(8,128)(2,1)S(1)} %collective-permute-done.16.other_ref, bf16[64,2048]{1,0:T(8,128)(2,1)S(1)} %get-tuple-element.33.cand_ref.base_ref, f32[1,2048]{1,0:T(1,128)S(1)} %bitcast.9, ...), custom_call_target="tpu_custom_call" | custom-call | bytes 533056 | tf_op jit(solution)/shard_map/pallas_call | solution.py:36
  (33 shorter events, 0.3 us)
Async XLA Ops:
  0.6 5.7 %copy-start.6 = (s32[1,64]{1,0:T(1,128)S(1)}, s32[1,64]{1,0:T(1,128)}, u32[]{:S(2)}) copy-start(s32[1,64]{1,0:T(1,128)} %ids_ref.1) | copy-start | bytes 772
  0.6 5.7 %copy-start.1 = (bf16[256,4096]{1,0:T(8,128)(2,1)S(1)}, bf16[256,4096]{1,0:T(8,128)(2,1)}, u32[]{:S(2)}) copy-start(bf16[256,4096]{1,0:T(8,128)(2,1)} %pool_ref.1) | copy-start | bytes 6291460
  0.7 6.3 %copy-start = (bf16[2048,2048]{1,0:T(8,128)(2,1)S(1)}, bf16[2048,2048]{1,0:T(8,128)(2,1)}, u32[]{:S(2)}) copy-start(bf16[2048,2048]{1,0:T(8,128)(2,1)} %weight_ref.6) | copy-start | bytes 25165828
  0.7 7.2 %collective-permute-start = (bf16[1,4096]{1,0:T(2,128)(2,1)}, bf16[1,4096]{1,0:T(2,128)(2,1)S(1)}, u32[]{:S(2)}, u32[]{:S(2)}) collective-permute-start(bf16[1,4096]{1,0:T(2,128)(2,1)} %refs_0_.1), channel_id=1, source_target_pairs={{0,4},{4,0},{8,12},{12,8},{1,5},{5,1},{9,13},{13,9},{2,6},{6,2},{1... | collective-permute-start | bytes 24584 | tf_op jit(solution)/shard_map/ppermute | solution.py:30
  3.8 4.9 %collective-permute-start.1 = (bf16[1,4096]{1,0:T(2,128)(2,1)}, bf16[1,4096]{1,0:T(2,128)(2,1)S(1)}, u32[]{:S(2)}, u32[]{:S(2)}) collective-permute-start(bf16[1,4096]{1,0:T(2,128)(2,1)} %refs_0_.1), channel_id=1, source_target_pairs={{0,8},{4,12},{8,0},{12,4},{1,9},{5,13},{9,1},{13,5},{2,10},{6,14},... | collective-permute-start | bytes 24584 | tf_op jit(solution)/shard_map/ppermute | solution.py:30
  6.4 5.7 %collective-permute-start.2 = (bf16[1,4096]{1,0:T(2,128)(2,1)}, bf16[1,4096]{1,0:T(2,128)(2,1)S(1)}, u32[]{:S(2)}, u32[]{:S(2)}) collective-permute-start(bf16[1,4096]{1,0:T(2,128)(2,1)} %refs_0_.1), channel_id=1, source_target_pairs={{0,12},{4,8},{8,4},{12,0},{1,13},{5,9},{9,5},{13,1},{2,14},{6,10},... | collective-permute-start | bytes 24584 | tf_op jit(solution)/shard_map/ppermute | solution.py:30
  6.4 5.7 %copy-start.3 = (bf16[1,4096]{1,0:T(2,128)(2,1)S(1)}, bf16[1,4096]{1,0:T(2,128)(2,1)}, u32[]{:S(2)}) copy-start(bf16[1,4096]{1,0:T(2,128)(2,1)} %refs_0_.1) | copy-start | bytes 24580
  6.9 13.8 %copy-start.7 = (bf16[2048]{0:T(1024)(128)(2,1)S(1)}, bf16[2048]{0:T(1024)(128)(2,1)}, u32[]{:S(2)}) copy-start(bf16[2048]{0:T(1024)(128)(2,1)} %param.21) | copy-start | bytes 12292
  6.9 13.8 %slice-start = ((s8[8388608]{0:T(1024)(128)(4,1)}), s8[4194304]{0:T(1024)(128)(4,1)S(1)}, s32[]{:S(2)}) async-start(s8[8388608]{0:T(1024)(128)(4,1)} %bitcast.4), calls=%async_computation | async-start | bytes 8388608
  6.9 13.8 %copy-start.2 = (f32[2048]{0:T(1024)S(1)}, f32[2048]{0:T(1024)}, u32[]{:S(2)}) copy-start(f32[2048]{0:T(1024)} %param.20) | copy-start | bytes 24580
  7.0 20.8 %slice-start.2 = ((s8[8388608]{0:T(1024)(128)(4,1)}), s8[4194304]{0:T(1024)(128)(4,1)S(1)}, s32[]{:S(2)}) async-start(s8[8388608]{0:T(1024)(128)(4,1)} %bitcast.6), calls=%async_computation.2 | async-start | bytes 8388608
  12.1 8.7 %slice-start.1 = ((s8[8388608]{0:T(1024)(128)(4,1)}), s8[4194304]{0:T(1024)(128)(4,1)S(1)}, s32[]{:S(2)}) async-start(s8[8388608]{0:T(1024)(128)(4,1)} %bitcast.4), calls=%async_computation.1 | async-start | bytes 8388608
  12.1 15.6 %slice-start.3 = ((s8[8388608]{0:T(1024)(128)(4,1)}), s8[4194304]{0:T(1024)(128)(4,1)S(1)}, s32[]{:S(2)}) async-start(s8[8388608]{0:T(1024)(128)(4,1)} %bitcast.6), calls=%async_computation.3 | async-start | bytes 8388608
  12.1 15.7 %copy-start.5 = (f32[2048]{0:T(1024)S(1)}, f32[2048]{0:T(1024)}, u32[]{:S(2)}) copy-start(f32[2048]{0:T(1024)} %param.16) | copy-start | bytes 24580
  13.5 1.4 %collective-permute-start.3 = (bf16[32,2048]{1,0:T(8,128)(2,1)S(1)}, bf16[32,2048]{1,0:T(8,128)(2,1)S(1)}, u32[]{:S(2)}, u32[]{:S(2)}) collective-permute-start(bf16[32,2048]{1,0:T(8,128)(2,1)S(1)} %get-tuple-element.39), channel_id=1, source_target_pairs={{0,1},{1,0},{2,3},{3,2},{4,5},{5,4},{6,7},{7,6},{8,9},{9,8},{10,11... | collective-permute-start | bytes 393224 | tf_op jit(solution)/shard_map/ppermute | solution.py:30
  15.0 5.6 %collective-permute-start.4 = (bf16[32,2048]{1,0:T(8,128)(2,1)S(1)}, bf16[32,2048]{1,0:T(8,128)(2,1)S(1)}, u32[]{:S(2)}, u32[]{:S(2)}) collective-permute-start(bf16[32,2048]{1,0:T(8,128)(2,1)S(1)} %get-tuple-element.41), channel_id=1, source_target_pairs={{0,2},{1,3},{2,0},{3,1},{4,6},{5,7},{6,4},{7,5},{8,10},{9,11},{10,... | collective-permute-start | bytes 393224 | tf_op jit(solution)/shard_map/ppermute | solution.py:30
  20.7 7.1 %collective-permute-start.5 = (bf16[32,2048]{1,0:T(8,128)(2,1)S(1)}, bf16[32,2048]{1,0:T(8,128)(2,1)S(1)}, u32[]{:S(2)}, u32[]{:S(2)}) collective-permute-start(bf16[32,2048]{1,0:T(8,128)(2,1)S(1)} %get-tuple-element.43), channel_id=1, source_target_pairs={{0,1},{1,0},{2,3},{3,2},{4,5},{5,4},{6,7},{7,6},{8,9},{9,8},{10,11... | collective-permute-start | bytes 393224 | tf_op jit(solution)/shard_map/ppermute | solution.py:30
  20.8 17.3 %copy-start.4 = (f32[2048]{0:T(1024)S(1)}, f32[2048]{0:T(1024)}, u32[]{:S(2)}) copy-start(f32[2048]{0:T(1024)} %param.18) | copy-start | bytes 24580
  23.3 7.3 %collective-permute-start.9 = (bf16[16,2176]{1,0:T(8,128)(2,1)S(1)}, bf16[16,2176]{1,0:T(8,128)(2,1)S(1)}, u32[]{:S(2)}, u32[]{:S(2)}) collective-permute-start(bf16[16,2176]{1,0:T(8,128)(2,1)S(1)} %get-tuple-element.49), channel_id=1, source_target_pairs={{0,4},{4,0},{8,12},{12,8},{1,5},{5,1},{9,13},{13,9},{2,6},{6,2},{1... | collective-permute-start | bytes 208904 | tf_op jit(solution)/shard_map/ppermute | solution.py:30
  23.4 10.6 %collective-permute-start.10 = (bf16[16,2176]{1,0:T(8,128)(2,1)S(1)}, bf16[16,2176]{1,0:T(8,128)(2,1)S(1)}, u32[]{:S(2)}, u32[]{:S(2)}) collective-permute-start(bf16[16,2176]{1,0:T(8,128)(2,1)S(1)} %get-tuple-element.50), channel_id=1, source_target_pairs={{0,8},{4,12},{8,0},{12,4},{1,9},{5,13},{9,1},{13,5},{2,10},{6,14},... | collective-permute-start | bytes 208904 | tf_op jit(solution)/shard_map/ppermute | solution.py:30
  24.5 9.5 %collective-permute-start.11 = (bf16[16,2176]{1,0:T(8,128)(2,1)S(1)}, bf16[16,2176]{1,0:T(8,128)(2,1)S(1)}, u32[]{:S(2)}, u32[]{:S(2)}) collective-permute-start(bf16[16,2176]{1,0:T(8,128)(2,1)S(1)} %get-tuple-element.51), channel_id=1, source_target_pairs={{0,12},{4,8},{8,4},{12,0},{1,13},{5,9},{9,5},{13,1},{2,14},{6,10},... | collective-permute-start | bytes 208904 | tf_op jit(solution)/shard_map/ppermute | solution.py:30
  29.5 4.7 %collective-permute-start.6 = (bf16[16,2048]{1,0:T(8,128)(2,1)S(1)}, bf16[16,2048]{1,0:T(8,128)(2,1)S(1)}, u32[]{:S(2)}, u32[]{:S(2)}) collective-permute-start(bf16[16,2048]{1,0:T(8,128)(2,1)S(1)} %get-tuple-element.45), channel_id=1, source_target_pairs={{0,4},{4,0},{8,12},{12,8},{1,5},{5,1},{9,13},{13,9},{2,6},{6,2},{1... | collective-permute-start | bytes 196616 | tf_op jit(solution)/shard_map/ppermute | solution.py:30
  29.6 8.6 %collective-permute-start.7 = (bf16[16,2048]{1,0:T(8,128)(2,1)S(1)}, bf16[16,2048]{1,0:T(8,128)(2,1)S(1)}, u32[]{:S(2)}, u32[]{:S(2)}) collective-permute-start(bf16[16,2048]{1,0:T(8,128)(2,1)S(1)} %get-tuple-element.46), channel_id=1, source_target_pairs={{0,8},{4,12},{8,0},{12,4},{1,9},{5,13},{9,1},{13,5},{2,10},{6,14},... | collective-permute-start | bytes 196616 | tf_op jit(solution)/shard_map/ppermute | solution.py:30
  30.6 7.5 %collective-permute-start.8 = (bf16[16,2048]{1,0:T(8,128)(2,1)S(1)}, bf16[16,2048]{1,0:T(8,128)(2,1)S(1)}, u32[]{:S(2)}, u32[]{:S(2)}) collective-permute-start(bf16[16,2048]{1,0:T(8,128)(2,1)S(1)} %get-tuple-element.47), channel_id=1, source_target_pairs={{0,12},{4,8},{8,4},{12,0},{1,13},{5,9},{9,5},{13,1},{2,14},{6,10},... | collective-permute-start | bytes 196616 | tf_op jit(solution)/shard_map/ppermute | solution.py:30
  38.4 4.4 %collective-permute-start.12 = (bf16[16,2176]{1,0:T(8,128)(2,1)S(1)}, bf16[16,2176]{1,0:T(8,128)(2,1)S(1)}, u32[]{:S(2)}, u32[]{:S(2)}) collective-permute-start(bf16[16,2176]{1,0:T(8,128)(2,1)S(1)} %shard_map.132.refs_0_), channel_id=1, source_target_pairs={{0,4},{4,0},{8,12},{12,8},{1,5},{5,1},{9,13},{13,9},{2,6},{6,2},{1... | collective-permute-start | bytes 208904 | tf_op jit(solution)/shard_map/ppermute | solution.py:30
  39.8 7.8 %collective-permute-start.13 = (bf16[16,2176]{1,0:T(8,128)(2,1)S(1)}, bf16[16,2176]{1,0:T(8,128)(2,1)S(1)}, u32[]{:S(2)}, u32[]{:S(2)}) collective-permute-start(bf16[16,2176]{1,0:T(8,128)(2,1)S(1)} %shard_map.132.refs_0_), channel_id=1, source_target_pairs={{0,8},{4,12},{8,0},{12,4},{1,9},{5,13},{9,1},{13,5},{2,10},{6,14},... | collective-permute-start | bytes 208904 | tf_op jit(solution)/shard_map/ppermute | solution.py:30
  40.9 6.6 %collective-permute-start.14 = (bf16[16,2176]{1,0:T(8,128)(2,1)S(1)}, bf16[16,2176]{1,0:T(8,128)(2,1)S(1)}, u32[]{:S(2)}, u32[]{:S(2)}) collective-permute-start(bf16[16,2176]{1,0:T(8,128)(2,1)S(1)} %shard_map.132.refs_0_), channel_id=1, source_target_pairs={{0,12},{4,8},{8,4},{12,0},{1,13},{5,9},{9,5},{13,1},{2,14},{6,10},... | collective-permute-start | bytes 208904 | tf_op jit(solution)/shard_map/ppermute | solution.py:30
  49.4 1.4 %collective-permute-start.15 = (bf16[32,2048]{1,0:T(8,128)(2,1)S(1)}, bf16[32,2048]{1,0:T(8,128)(2,1)S(1)}, u32[]{:S(2)}, u32[]{:S(2)}) collective-permute-start(bf16[32,2048]{1,0:T(8,128)(2,1)S(1)} %get-tuple-element.54), channel_id=1, source_target_pairs={{0,1},{1,0},{2,3},{3,2},{4,5},{5,4},{6,7},{7,6},{8,9},{9,8},{10,11... | collective-permute-start | bytes 393224 | tf_op jit(solution)/shard_map/ppermute | solution.py:30
  50.8 5.4 %collective-permute-start.16 = (bf16[16,2048]{1,0:T(8,128)(2,1)S(1)}, bf16[16,2048]{1,0:T(8,128)(2,1)S(1)}, u32[]{:S(2)}, u32[]{:S(2)}) collective-permute-start(bf16[16,2048]{1,0:T(8,128)(2,1)S(1)} %get-tuple-element.56), channel_id=1, source_target_pairs={{0,2},{1,3},{2,0},{3,1},{4,6},{5,7},{6,4},{7,5},{8,10},{9,11},{10,... | collective-permute-start | bytes 196616 | tf_op jit(solution)/shard_map/ppermute | solution.py:30
  51.4 1.2 %collective-permute-start.17 = (f32[4,16]{1,0:T(4,128)S(1)}, f32[4,16]{1,0:T(4,128)S(1)}, u32[]{:S(2)}, u32[]{:S(2)}) collective-permute-start(f32[4,16]{1,0:T(4,128)S(1)} %get-tuple-element.57.refs_0_), channel_id=1, source_target_pairs={{0,1},{1,0},{2,3},{3,2},{4,5},{5,4},{6,7},{7,6},{8,9},{9,8},{10,11... | collective-permute-start | bytes 776 | tf_op jit(solution)/shard_map/ppermute | solution.py:30
  52.6 3.6 %collective-permute-start.18 = (f32[4,16]{1,0:T(4,128)S(1)}, f32[4,16]{1,0:T(4,128)S(1)}, u32[]{:S(2)}, u32[]{:S(2)}) collective-permute-start(f32[4,16]{1,0:T(4,128)S(1)} %shard_map.136.total_ref), channel_id=1, source_target_pairs={{0,2},{1,3},{2,0},{3,1},{4,6},{5,7},{6,4},{7,5},{8,10},{9,11},{10,... | collective-permute-start | bytes 776 | tf_op jit(solution)/shard_map/ppermute | solution.py:30
